TPU v7x, 32 devices: a whole 2x2x4 slice. The times are simulated.
32 devices in a mesh: slab: 8 (over z, x), depth: 4 (over y, core).
Axes of the slice: x: 2, y: 2, z: 4, core: 2. Of those that a mesh axis runs over, the one named last changes fastest.
Arguments:
- alpha: float32 [128, 256, 512], P('slab', 'depth'), may hold values from 0 to 1
- vel_x: float32 [128, 256, 512], P('slab', 'depth'), may hold values from -1 to 1
- vel_z: float32 [128, 256, 512], P('slab', 'depth'), may hold values from -1 to 1
- divergence: float32 [128, 256, 512], P('slab', 'depth'), may hold values from -6 to 6
- press_guess: float32 [128, 256, 512], P('slab', 'depth'), may hold values from -6 to 6
- panel_records: bfloat16 [8192, 128], P(('slab', 'depth')), may hold values from -6 to 6
- panel_dest: int32 [8192, 1], P(('slab', 'depth')), may hold values from 0 to 31; in each aligned block of 256 rows (0 to 255, 256 to 511, ...) at most 16 rows name the same one
- panel_segment: int32 [8192, 1], P(('slab', 'depth')), may hold values from 0 to 4095
Outputs:
- pressure: float32 [128, 256, 512], P('slab', 'depth')
- alpha_next: float32 [128, 256, 512], P('slab', 'depth')
- panel_pressure: bfloat16 [8192, 128], P(('slab', 'depth'))
Inputs may be any that keep to these rules, and one draw needn't show every extreme that they name: `panel_dest`: among the 256 panels of one device no fluid device is named more than 16 times.
All inputs are finite; a program needn't handle non-finite values.
Results may differ from a plain program's by a relative error of at most 0.001.
Values may be sent and summed in bfloat16 or wider, within the bound.
No kernel may reach another device: no remote copies, remote signals or barrier semaphores. Data moves between devices by JAX's collectives and lax.ppermute only.
A program may use at most 64 MiB of HBM per device.

v0:
```python
import jax
import jax.numpy as jnp
from jax import lax
from jax.sharding import PartitionSpec as P

COURANT = 0.2


def with_halo(block, sides, width):
    for axis, dim in sides:
        count = lax.axis_size(axis)
        forward = [(i, i + 1) for i in range(count - 1)]
        backward = [(target, source) for source, target in forward]
        low = lax.ppermute(
            lax.slice_in_dim(block, block.shape[dim] - width, None, axis=dim), axis, forward
        )
        high = lax.ppermute(lax.slice_in_dim(block, 0, width, axis=dim), axis, backward)
        block = jnp.concatenate([low, block, high], axis=dim)
    return block


def advect_core(alpha_pad, velx_pad, velz_pad):
    face_x = velx_pad[1:, 1:-1] * jnp.where(
        velx_pad[1:, 1:-1] > 0, alpha_pad[:-1, 1:-1], alpha_pad[1:, 1:-1]
    )
    face_z = velz_pad[1:-1, 1:] * jnp.where(
        velz_pad[1:-1, 1:] > 0, alpha_pad[1:-1, :-1], alpha_pad[1:-1, 1:]
    )
    change = face_x[1:] - face_x[:-1] + face_z[:, 1:] - face_z[:, :-1]
    return alpha_pad[1:-1, 1:-1] - COURANT * change


def sweep(press_pad, dens_pad, rhs):
    press_pad = jnp.pad(press_pad, ((0, 0), (0, 0), (1, 1)))
    dens_pad = jnp.pad(dens_pad, ((0, 0), (0, 0), (1, 1)))
    rows_all = rhs.shape[0]
    cols_all = rhs.shape[1]
    beam = rhs.shape[2]
    own_rho = dens_pad[1 : 1 + rows_all, 1 : 1 + cols_all, 1 : 1 + beam]
    total = jnp.zeros_like(rhs)
    weight = jnp.zeros_like(rhs)
    for off_x, off_z, off_y in ((0, 1, 1), (2, 1, 1), (1, 0, 1), (1, 2, 1), (1, 1, 0), (1, 1, 2)):
        next_p = press_pad[off_x : off_x + rows_all, off_z : off_z + cols_all, off_y : off_y + beam]
        next_rho = dens_pad[
            off_x : off_x + rows_all, off_z : off_z + cols_all, off_y : off_y + beam
        ]
        coeff = 2.0 / (own_rho + next_rho)
        total = total + coeff * next_p
        weight = weight + coeff
    return (total - rhs) / weight


def body(alpha, vel_x, vel_z, divergence, press_guess, panel_records, panel_dest, panel_segment):
    slabs = lax.axis_size("slab")
    depths = lax.axis_size("depth")
    devices = slabs * depths
    panel_count = panel_records.shape[0]
    capacity = 2 * panel_count // devices
    cells_x, cells_z, beam = alpha.shape
    blocks = beam // 128
    target = panel_dest[:, 0]
    onehot = (target[:, None] == jnp.arange(devices, dtype=jnp.int32)[None, :]).astype(jnp.int32)
    before = jnp.cumsum(onehot, axis=0) - onehot
    slot = jnp.sum(before * onehot, axis=1)
    place = target * capacity + slot
    send_rec = jnp.zeros((devices * capacity, 128), jnp.bfloat16).at[place].set(panel_records)
    send_seg = jnp.zeros((devices * capacity,), jnp.int32).at[place].set(panel_segment[:, 0])
    got_rec, got_seg = (
        lax.all_to_all(send_rec, ("slab", "depth"), split_axis=0, concat_axis=0, tiled=True),
        lax.all_to_all(send_seg, ("slab", "depth"), split_axis=0, concat_axis=0, tiled=True),
    )
    hull = (
        jnp.zeros((cells_x * cells_z * blocks, 128), jnp.float32)
        .at[got_seg]
        .add(got_rec.astype(jnp.float32))
    )
    hull = hull.reshape(cells_x, cells_z, beam)
    stacked = jnp.stack([alpha, vel_x, vel_z])
    padded = with_halo(stacked, (("slab", 1), ("depth", 2)), 1)
    alpha_next = advect_core(padded[0], padded[1], padded[2])
    density = 1.0 + 9.0 * alpha_next
    rhs = divergence + hull
    dens_pad = with_halo(density, (("slab", 0), ("depth", 1)), 1)
    pressure = press_guess
    for sweep_number in range(3):
        press_pad = with_halo(pressure, (("slab", 0), ("depth", 1)), 1)
        pressure = sweep(press_pad, dens_pad, rhs)
    wall_rows = pressure.reshape(-1, 128).astype(jnp.bfloat16)[got_seg]
    returned = lax.all_to_all(wall_rows, ("slab", "depth"), split_axis=0, concat_axis=0, tiled=True)
    panel_pressure = returned[place]
    return (pressure, alpha_next, panel_pressure)


def solution(mesh):
    in_specs = (
        P("slab", "depth", None),
        P("slab", "depth", None),
        P("slab", "depth", None),
        P("slab", "depth", None),
        P("slab", "depth", None),
        P(("slab", "depth"), None),
        P(("slab", "depth"), None),
        P(("slab", "depth"), None),
    )
    out_specs = (P("slab", "depth", None), P("slab", "depth", None), P(("slab", "depth"), None))
    return jax.shard_map(body, mesh=mesh, in_specs=in_specs, out_specs=out_specs, check_vma=False)
```

profile of v0, /device:TPU:0, one launch (start us, length us, event | category | flops | bytes accessed | tf_op | source)
XLA Modules:
  0.0 180.7 jit_solution(9752607152570612587)
XLA Ops:
  0.6 2.1 %pad_maximum_fusion.31 = (f32[3,1,64,512]{3,2,1,0:T(8,128)}, f32[3,1,64,512]{3,2,1,0:T(8,128)S(1)}) fusion(f32[1,16,64,512]{3,2,1,0:T(8,128)} %bitcast.41, f32[1,16,64,512]{3,2,1,0:T(8,128)} %bitcast.44, f32[1,16,64,512]{3,2,1,0:T(8,128)} %bitcast.47), kind=kLoop, calls=%fused_computation.120 | loop fusion | flops 393216 | bytes 7077888 | tf_op jit(solution)/shard_map/slice | solution.py:15
  2.8 4.9 %collective-permute-start = (f32[3,1,64,512]{3,2,1,0:T(8,128)}, f32[3,1,64,512]{3,2,1,0:T(8,128)S(1)}, u32[]{:S(2)}, u32[]{:S(2)}) collective-permute-start(f32[3,1,64,512]{3,2,1,0:T(8,128)} %get-tuple-element.14), channel_id=1, source_target_pairs={{0,4},{4,8},{8,12},{12,16},{16,20},{20,24},{24,28},{1,5},{5,9},{9,... | collective-permute-start | bytes 1179656 | tf_op jit(solution)/shard_map/ppermute | solution.py:14
  12.2 7.0 %all-to-all-start = ((s32[32,16,1]{1,2,0:T(1,128)}), s32[32,16,1]{1,2,0:T(1,128)S(1)}, u32[]{:S(2)}, u32[]{:S(2)}) async-start(s32[32,16,1]{1,2,0:T(1,128)} %bitcast.12), calls=%async_computation | async-start | bytes 32768 | tf_op jit(solution)/shard_map/all_to_all | solution.py:70
  20.9 3.7 %collective-permute-start.5 = (f32[1,64,512]{2,1,0:T(8,128)}, f32[1,64,512]{2,1,0:T(8,128)S(1)}, u32[]{:S(2)}, u32[]{:S(2)}) collective-permute-start(f32[1,64,512]{2,1,0:T(8,128)} %get-tuple-element.31), channel_id=1, source_target_pairs={{0,4},{4,8},{8,12},{12,16},{16,20},{20,24},{24,28},{1,5},{5,9},{9,... | collective-permute-start | bytes 393224 | tf_op jit(solution)/shard_map/ppermute | solution.py:14
  25.9 2.1 %scatter_custom_fusion.1 = bf16[512,128]{1,0:T(8,128)(2,1)} fusion(s32[256]{0:T(256)} %bitcast.56, bf16[256,128]{1,0:T(8,128)(2,1)} %param.13, bf16[]{:T(256)} %constant.8.clone.1), kind=kCustom, calls=%fused_computation.127 | custom fusion | bytes 131584 | tf_op jit(solution)/shard_map/scatter | solution.py:66
  28.0 6.8 %all-to-all-start.1 = ((bf16[32,16,128]{2,1,0:T(8,128)(2,1)}), bf16[32,16,128]{2,1,0:T(8,128)(2,1)}, u32[]{:S(2)}, u32[]{:S(2)}) async-start(bf16[32,16,128]{2,1,0:T(8,128)(2,1)} %bitcast.14), calls=%async_computation.1 | async-start | bytes 262144 | tf_op jit(solution)/shard_map/all_to_all | solution.py:69
  37.4 1.9 %constant_dynamic-update-slice_fusion.1 = f32[18,64,512]{2,1,0:T(8,128)S(1)} fusion(f32[18,64,512]{2,1,0:T(8,128)S(1)} %constant_dynamic-update-slice_fusion.2, f32[16,64,512]{2,1,0:T(8,128)} %param.12), kind=kLoop, calls=%fused_computation.149 | loop fusion | bytes 4194304
  40.5 2.1 %collective-permute-start.2 = (f32[3,18,1,512]{3,2,1,0:T(1,128)S(1)}, f32[3,18,1,512]{3,2,1,0:T(1,128)S(1)}, u32[]{:S(2)}, u32[]{:S(2)}) collective-permute-start(f32[3,18,1,512]{3,2,1,0:T(1,128)S(1)} %get-tuple-element.12), channel_id=1, source_target_pairs={{0,1},{1,2},{2,3},{4,5},{5,6},{6,7},{8,9},{9,10},{10,11},{12,13},{... | collective-permute-start | bytes 331784 | tf_op jit(solution)/shard_map/ppermute | solution.py:14
  43.9 3.0 %collective-permute-done.3 = f32[3,18,1,512]{3,2,1,0:T(1,128)S(1)} collective-permute-done((f32[3,18,1,512]{3,2,1,0:T(1,128)S(1)}, f32[3,18,1,512]{3,2,1,0:T(1,128)S(1)}, u32[]{:S(2)}, u32[]{:S(2)}) %collective-permute-start.3) | collective-permute-done | bytes 110624 | tf_op jit(solution)/shard_map/ppermute | solution.py:17
  50.8 2.2 %multiply_add_fusion = (f32[16,64,512]{2,1,0:T(8,128)S(1)}, f32[16,64,512]{2,1,0:T(8,128)}) fusion(f32[16,65,512]{2,1,0:T(8,128)S(1)} %fusion.1, f32[17,64,512]{2,1,0:T(8,128)S(1)} %fusion.2, f32[18,66,512]{2,1,0:T(8,128)S(1)} %get-tuple-element.11), kind=kLoop, calls=%fused_computation.115 | loop fusion | flops 3670016 | bytes 14680064 | tf_op jit(solution)/shard_map/add | solution.py:81
  53.1 3.4 %collective-permute-start.4 = (f32[1,64,512]{2,1,0:T(8,128)S(1)}, f32[1,64,512]{2,1,0:T(8,128)S(1)}, u32[]{:S(2)}, u32[]{:S(2)}) collective-permute-start(f32[1,64,512]{2,1,0:T(8,128)S(1)} %get-tuple-element.29), channel_id=1, source_target_pairs={{0,4},{4,8},{8,12},{12,16},{16,20},{20,24},{24,28},{1,5},{5,9},{9,... | collective-permute-start | bytes 393224 | tf_op jit(solution)/shard_map/ppermute | solution.py:14
  59.1 5.6 %collective-permute-start.9 = (f32[18,1,512]{2,1,0:T(1,128)S(1)}, f32[18,1,512]{2,1,0:T(1,128)S(1)}, u32[]{:S(2)}, u32[]{:S(2)}) collective-permute-start(f32[18,1,512]{2,1,0:T(1,128)S(1)} %get-tuple-element.22), channel_id=1, source_target_pairs={{0,1},{1,2},{2,3},{4,5},{5,6},{6,7},{8,9},{9,10},{10,11},{12,13},{... | collective-permute-start | bytes 110600 | tf_op jit(solution)/shard_map/ppermute | solution.py:14
  66.1 4.3 %collective-permute-start.8 = (f32[18,1,512]{2,1,0:T(1,128)S(1)}, f32[18,1,512]{2,1,0:T(1,128)S(1)}, u32[]{:S(2)}, u32[]{:S(2)}) collective-permute-start(f32[18,1,512]{2,1,0:T(1,128)S(1)} %get-tuple-element.21), channel_id=1, source_target_pairs={{0,1},{1,2},{2,3},{4,5},{5,6},{6,7},{8,9},{9,10},{10,11},{12,13},{... | collective-permute-start | bytes 110600 | tf_op jit(solution)/shard_map/ppermute | solution.py:14
  70.4 3.0 %select_maximum_fusion.8 = f32[18,66,514]{2,1,0:T(8,128)} fusion(f32[18,1,512]{2,1,0:T(1,128)S(1)} %collective-permute-done.11, f32[18,64,512]{2,1,0:T(8,128)S(1)} %constant_dynamic-update-slice_fusion, f32[18,1,512]{2,1,0:T(1,128)S(1)} %collective-permute-done.9), kind=kLoop, calls=%fused_computation.16 | loop fusion | flops 4885056 | bytes 4875552 | tf_op jit(solution)/shard_map/concatenate | solution.py:18
  73.5 4.3 %scatter_custom_fusion.2 = f32[4096,128]{1,0:T(8,128)} fusion(s32[512]{0:T(512)S(1)} %bitcast.53, f32[]{:T(128)} %constant.11.clone.1, bf16[512,128]{1,0:T(8,128)(2,1)} %bitcast.18), kind=kCustom, calls=%fused_computation.116 | custom fusion | flops 131072 | bytes 2228228 | tf_op jit(solution)/shard_map/scatter-add | solution.py:75
  77.8 2.7 %reshape.65 = f32[16,64,512]{2,1,0:T(8,128)} reshape(f32[4096,128]{1,0:T(8,128)} %scatter_custom_fusion.2) | data formatting | bytes 4194304 | tf_op jit(solution)/shard_map/reshape | solution.py:77
  80.6 3.0 %select_maximum_fusion.10 = f32[18,66,514]{2,1,0:T(8,128)S(1)} fusion(f32[18,1,512]{2,1,0:T(1,128)S(1)} %collective-permute-done.10, f32[18,1,512]{2,1,0:T(1,128)S(1)} %collective-permute-done.8, f32[1,64,512]{2,1,0:T(8,128)S(1)} %collective-permute-done.6, f32[16,64,512]{2,1,0:T(8,128)S(1)} %get-tuple-element.7, f32[1,64,512]{2,1,0:T(8,128)S(1)} %collective-permute-done.4), kind=kLoop, calls=%fused_computation.18 | loop fusion | flops 7327584 | bytes 4875552 | tf_op jit(solution)/shard_map/concatenate | solution.py:18
  83.6 12.7 %fusion.27 = (f32[16,64,512]{2,1,0:T(8,128)S(1)}, f32[16,64,512]{2,1,0:T(8,128)}) fusion(f32[18,66,514]{2,1,0:T(8,128)} %select_maximum_fusion.8, f32[18,1,512]{2,1,0:T(1,128)S(1)} %collective-permute-done.11, f32[18,64,512]{2,1,0:T(8,128)} %copy-done.6, f32[18,1,512]{2,1,0:T(1,128)S(1)} %collective-permute-done.9, ...), kind=kLoop, calls=%fused_computation.75 | loop fusion | flops 23592960 | bytes 26099712 | tf_op jit(solution)/shard_map/div | solution.py:50
  96.3 4.8 %collective-permute-start.12 = (f32[1,64,512]{2,1,0:T(8,128)S(1)}, f32[1,64,512]{2,1,0:T(8,128)S(1)}, u32[]{:S(2)}, u32[]{:S(2)}) collective-permute-start(f32[1,64,512]{2,1,0:T(8,128)S(1)} %get-tuple-element.26), channel_id=1, source_target_pairs={{0,4},{4,8},{8,12},{12,16},{16,20},{20,24},{24,28},{1,5},{5,9},{9,... | collective-permute-start | bytes 393224 | tf_op jit(solution)/shard_map/ppermute | solution.py:14
  102.5 2.5 %collective-permute-done.12 = f32[1,64,512]{2,1,0:T(8,128)S(1)} collective-permute-done((f32[1,64,512]{2,1,0:T(8,128)S(1)}, f32[1,64,512]{2,1,0:T(8,128)S(1)}, u32[]{:S(2)}, u32[]{:S(2)}) %collective-permute-start.12) | collective-permute-done | bytes 131104 | tf_op jit(solution)/shard_map/ppermute | solution.py:14
  104.9 4.3 %collective-permute-done.13 = f32[1,64,512]{2,1,0:T(8,128)S(1)} collective-permute-done((f32[1,64,512]{2,1,0:T(8,128)S(1)}, f32[1,64,512]{2,1,0:T(8,128)S(1)}, u32[]{:S(2)}, u32[]{:S(2)}) %collective-permute-start.13) | collective-permute-done | bytes 131104 | tf_op jit(solution)/shard_map/ppermute | solution.py:17
  109.3 2.4 %collective-permute-start.14 = (f32[18,1,512]{2,1,0:T(1,128)S(1)}, f32[18,1,512]{2,1,0:T(1,128)S(1)}, u32[]{:S(2)}, u32[]{:S(2)}) collective-permute-start(f32[18,1,512]{2,1,0:T(1,128)S(1)} %get-tuple-element.18), channel_id=1, source_target_pairs={{0,1},{1,2},{2,3},{4,5},{5,6},{6,7},{8,9},{9,10},{10,11},{12,13},{... | collective-permute-start | bytes 110600 | tf_op jit(solution)/shard_map/ppermute | solution.py:14
  115.0 4.1 %select_maximum_fusion.4 = f32[18,66,514]{2,1,0:T(8,128)} fusion(f32[18,1,512]{2,1,0:T(1,128)S(1)} %collective-permute-done.15, f32[18,1,512]{2,1,0:T(1,128)S(1)} %collective-permute-done.14, f32[1,64,512]{2,1,0:T(8,128)S(1)} %collective-permute-done.13, f32[16,64,512]{2,1,0:T(8,128)S(1)} %get-tuple-element.5, f32[1,64,512]{2,1,0:T(8,128)S(1)} %collective-permute-done.12), kind=kLoop, calls=%fused_computation.12 | loop fusion | flops 7327584 | bytes 4875552 | tf_op jit(solution)/shard_map/concatenate | solution.py:18
  119.2 9.6 %fusion.16 = f32[16,64,512]{2,1,0:T(8,128)S(1)} fusion(f32[16,64,512]{2,1,0:T(8,128)S(1)} %copy-done.4, f32[18,66,514]{2,1,0:T(8,128)} %select_maximum_fusion.4, f32[18,1,512]{2,1,0:T(1,128)S(1)} %collective-permute-done.15, f32[1,64,512]{2,1,0:T(8,128)S(1)} %collective-permute-done.13, f32[16,64,512]{2,1,0:T(8,128)S(1)} %get-tuple-element.5, ...), kind=kLoop, calls=%fused_computation.54 | loop fusion | flops 25165824 | bytes 19546112 | tf_op jit(solution)/shard_map/div | solution.py:50
  128.8 4.8 %collective-permute-start.16 = (f32[1,64,512]{2,1,0:T(8,128)S(1)}, f32[1,64,512]{2,1,0:T(8,128)S(1)}, u32[]{:S(2)}, u32[]{:S(2)}) collective-permute-start(f32[1,64,512]{2,1,0:T(8,128)S(1)} %get-tuple-element.24), channel_id=1, source_target_pairs={{0,4},{4,8},{8,12},{12,16},{16,20},{20,24},{24,28},{1,5},{5,9},{9,... | collective-permute-start | bytes 393224 | tf_op jit(solution)/shard_map/ppermute | solution.py:14
  136.2 4.4 %collective-permute-done.17 = f32[1,64,512]{2,1,0:T(8,128)S(1)} collective-permute-done((f32[1,64,512]{2,1,0:T(8,128)S(1)}, f32[1,64,512]{2,1,0:T(8,128)S(1)}, u32[]{:S(2)}, u32[]{:S(2)}) %collective-permute-start.17) | collective-permute-done | bytes 131104 | tf_op jit(solution)/shard_map/ppermute | solution.py:17
  140.6 3.1 %collective-permute-start.18 = (f32[18,1,512]{2,1,0:T(1,128)S(1)}, f32[18,1,512]{2,1,0:T(1,128)S(1)}, u32[]{:S(2)}, u32[]{:S(2)}) collective-permute-start(f32[18,1,512]{2,1,0:T(1,128)S(1)} %get-tuple-element.16), channel_id=1, source_target_pairs={{0,1},{1,2},{2,3},{4,5},{5,6},{6,7},{8,9},{9,10},{10,11},{12,13},{... | collective-permute-start | bytes 110600 | tf_op jit(solution)/shard_map/ppermute | solution.py:14
  145.3 2.5 %collective-permute-done.19 = f32[18,1,512]{2,1,0:T(1,128)S(1)} collective-permute-done((f32[18,1,512]{2,1,0:T(1,128)S(1)}, f32[18,1,512]{2,1,0:T(1,128)S(1)}, u32[]{:S(2)}, u32[]{:S(2)}) %collective-permute-start.19) | collective-permute-done | bytes 36896 | tf_op jit(solution)/shard_map/ppermute | solution.py:17
  147.8 4.1 %select_maximum_fusion = f32[18,66,514]{2,1,0:T(8,128)} fusion(f32[18,1,512]{2,1,0:T(1,128)S(1)} %collective-permute-done.19, f32[18,1,512]{2,1,0:T(1,128)S(1)} %collective-permute-done.18, f32[1,64,512]{2,1,0:T(8,128)S(1)} %collective-permute-done.17, f32[16,64,512]{2,1,0:T(8,128)S(1)} %fusion.16, f32[1,64,512]{2,1,0:T(8,128)S(1)} %collective-permute-done.16), kind=kLoop, calls=%fused_computation.8 | loop fusion | flops 7327584 | bytes 4875552 | tf_op jit(solution)/shard_map/concatenate | solution.py:18
  151.9 10.4 %fusion.59 = (bf16[16,64,512]{2,1,0:T(8,128)(2,1)S(1)}, f32[16,64,512]{2,1,0:T(8,128)}) fusion(f32[16,64,512]{2,1,0:T(8,128)S(1)} %copy-done.5, f32[18,66,514]{2,1,0:T(8,128)} %select_maximum_fusion, f32[18,66,514]{2,1,0:T(8,128)S(1)} %select_maximum_fusion.10, f32[16,64,512]{2,1,0:T(8,128)S(1)} %copy-done, f32[18,1,512]{2,1,0:T(1,128)S(1)} %collective-permute-done.19, ...), kind=kLoop, calls=%fused_computation.156 | loop fusion | flops 25690112 | bytes 20594688 | tf_op jit(solution)/shard_map/convert_element_type | solution.py:88
  164.9 6.1 %all-to-all-start.2 = ((bf16[32,16,128]{2,1,0:T(8,128)(2,1)}), bf16[32,16,128]{2,1,0:T(8,128)(2,1)S(1)}, u32[]{:S(2)}, u32[]{:S(2)}) async-start(bf16[32,16,128]{2,1,0:T(8,128)(2,1)} %bitcast.16), calls=%async_computation.2 | async-start | bytes 262144 | tf_op jit(solution)/shard_map/all_to_all | solution.py:89
  171.0 8.2 %all-to-all-done.2 = bf16[32,16,128]{2,1,0:T(8,128)(2,1)S(1)} async-done(((bf16[32,16,128]{2,1,0:T(8,128)(2,1)}), bf16[32,16,128]{2,1,0:T(8,128)(2,1)S(1)}, u32[]{:S(2)}, u32[]{:S(2)}) %all-to-all-start.2) | async-done | bytes 131104 | tf_op jit(solution)/shard_map/all_to_all | solution.py:89
  (82 shorter events, 33.2 us)
Async XLA Ops:
  0.6 8.4 %copy-start.8 = (s32[256,1]{0,1:T(1,128)S(1)}, s32[256,1]{0,1:T(1,128)}, u32[]{:S(2)}) copy-start(s32[256,1]{0,1:T(1,128)} %param.14) | copy-start | bytes 3076
  0.6 38.8 %copy-start.3 = (f32[16,64,512]{2,1,0:T(8,128)S(1)}, f32[16,64,512]{2,1,0:T(8,128)}, u32[]{:S(2)}) copy-start(f32[16,64,512]{2,1,0:T(8,128)} %param.8) | copy-start | bytes 6291460
  2.8 36.6 %collective-permute-start = (f32[3,1,64,512]{3,2,1,0:T(8,128)}, f32[3,1,64,512]{3,2,1,0:T(8,128)S(1)}, u32[]{:S(2)}, u32[]{:S(2)}) collective-permute-start(f32[3,1,64,512]{3,2,1,0:T(8,128)} %get-tuple-element.14), channel_id=1, source_target_pairs={{0,4},{4,8},{8,12},{12,16},{16,20},{20,24},{24,28},{1,5},{5,9},{9,... | collective-permute-start | bytes 1179656 | tf_op jit(solution)/shard_map/ppermute | solution.py:14
  7.7 31.7 %collective-permute-start.1 = (f32[3,1,64,512]{3,2,1,0:T(8,128)S(1)}, f32[3,1,64,512]{3,2,1,0:T(8,128)S(1)}, u32[]{:S(2)}, u32[]{:S(2)}) collective-permute-start(f32[3,1,64,512]{3,2,1,0:T(8,128)S(1)} %get-tuple-element.15), channel_id=1, source_target_pairs={{4,0},{8,4},{12,8},{16,12},{20,16},{24,20},{28,24},{5,1},{9,5},{13... | collective-permute-start | bytes 1179656 | tf_op jit(solution)/shard_map/ppermute | solution.py:17
  9.9 10.9 %copy-start.9 = (s32[256,1]{0,1:T(1,128)}, s32[256,1]{0,1:T(1,128)S(1)}, u32[]{:S(2)}) copy-start(s32[256,1]{0,1:T(1,128)S(1)} %compare_select_fusion.1) | copy-start | bytes 3076
  12.2 15.8 %all-to-all-start = ((s32[32,16,1]{1,2,0:T(1,128)}), s32[32,16,1]{1,2,0:T(1,128)S(1)}, u32[]{:S(2)}, u32[]{:S(2)}) async-start(s32[32,16,1]{1,2,0:T(1,128)} %bitcast.12), calls=%async_computation | async-start | bytes 32768 | tf_op jit(solution)/shard_map/all_to_all | solution.py:70
  20.9 16.5 %collective-permute-start.5 = (f32[1,64,512]{2,1,0:T(8,128)}, f32[1,64,512]{2,1,0:T(8,128)S(1)}, u32[]{:S(2)}, u32[]{:S(2)}) collective-permute-start(f32[1,64,512]{2,1,0:T(8,128)} %get-tuple-element.31), channel_id=1, source_target_pairs={{0,4},{4,8},{8,12},{12,16},{16,20},{20,24},{24,28},{1,5},{5,9},{9,... | collective-permute-start | bytes 393224 | tf_op jit(solution)/shard_map/ppermute | solution.py:14
  24.6 19.3 %collective-permute-start.7 = (f32[1,64,512]{2,1,0:T(8,128)}, f32[1,64,512]{2,1,0:T(8,128)S(1)}, u32[]{:S(2)}, u32[]{:S(2)}) collective-permute-start(f32[1,64,512]{2,1,0:T(8,128)} %get-tuple-element.30), channel_id=1, source_target_pairs={{4,0},{8,4},{12,8},{16,12},{20,16},{24,20},{28,24},{5,1},{9,5},{13... | collective-permute-start | bytes 393224 | tf_op jit(solution)/shard_map/ppermute | solution.py:17
  28.0 45.5 %all-to-all-start.1 = ((bf16[32,16,128]{2,1,0:T(8,128)(2,1)}), bf16[32,16,128]{2,1,0:T(8,128)(2,1)}, u32[]{:S(2)}, u32[]{:S(2)}) async-start(bf16[32,16,128]{2,1,0:T(8,128)(2,1)} %bitcast.14), calls=%async_computation.1 | async-start | bytes 262144 | tf_op jit(solution)/shard_map/all_to_all | solution.py:69
  40.5 3.4 %collective-permute-start.2 = (f32[3,18,1,512]{3,2,1,0:T(1,128)S(1)}, f32[3,18,1,512]{3,2,1,0:T(1,128)S(1)}, u32[]{:S(2)}, u32[]{:S(2)}) collective-permute-start(f32[3,18,1,512]{3,2,1,0:T(1,128)S(1)} %get-tuple-element.12), channel_id=1, source_target_pairs={{0,1},{1,2},{2,3},{4,5},{5,6},{6,7},{8,9},{9,10},{10,11},{12,13},{... | collective-permute-start | bytes 331784 | tf_op jit(solution)/shard_map/ppermute | solution.py:14
  42.6 4.3 %collective-permute-start.3 = (f32[3,18,1,512]{3,2,1,0:T(1,128)S(1)}, f32[3,18,1,512]{3,2,1,0:T(1,128)S(1)}, u32[]{:S(2)}, u32[]{:S(2)}) collective-permute-start(f32[3,18,1,512]{3,2,1,0:T(1,128)S(1)} %get-tuple-element.13), channel_id=1, source_target_pairs={{1,0},{2,1},{3,2},{5,4},{6,5},{7,6},{9,8},{10,9},{11,10},{13,12},{... | collective-permute-start | bytes 331784 | tf_op jit(solution)/shard_map/ppermute | solution.py:17
  43.9 26.5 %copy-start.6 = (f32[18,64,512]{2,1,0:T(8,128)}, f32[18,64,512]{2,1,0:T(8,128)S(1)}, u32[]{:S(2)}) copy-start(f32[18,64,512]{2,1,0:T(8,128)S(1)} %constant_dynamic-update-slice_fusion) | copy-start | bytes 7077892
  53.1 11.7 %collective-permute-start.4 = (f32[1,64,512]{2,1,0:T(8,128)S(1)}, f32[1,64,512]{2,1,0:T(8,128)S(1)}, u32[]{:S(2)}, u32[]{:S(2)}) collective-permute-start(f32[1,64,512]{2,1,0:T(8,128)S(1)} %get-tuple-element.29), channel_id=1, source_target_pairs={{0,4},{4,8},{8,12},{12,16},{16,20},{20,24},{24,28},{1,5},{5,9},{9,... | collective-permute-start | bytes 393224 | tf_op jit(solution)/shard_map/ppermute | solution.py:14
  56.5 8.3 %collective-permute-start.6 = (f32[1,64,512]{2,1,0:T(8,128)S(1)}, f32[1,64,512]{2,1,0:T(8,128)S(1)}, u32[]{:S(2)}, u32[]{:S(2)}) collective-permute-start(f32[1,64,512]{2,1,0:T(8,128)S(1)} %get-tuple-element.28), channel_id=1, source_target_pairs={{4,0},{8,4},{12,8},{16,12},{20,16},{24,20},{28,24},{5,1},{9,5},{13... | collective-permute-start | bytes 393224 | tf_op jit(solution)/shard_map/ppermute | solution.py:17
  57.8 12.6 %collective-permute-start.11 = (f32[18,1,512]{2,1,0:T(1,128)S(1)}, f32[18,1,512]{2,1,0:T(1,128)S(1)}, u32[]{:S(2)}, u32[]{:S(2)}) collective-permute-start(f32[18,1,512]{2,1,0:T(1,128)S(1)} %get-tuple-element.23), channel_id=1, source_target_pairs={{1,0},{2,1},{3,2},{5,4},{6,5},{7,6},{9,8},{10,9},{11,10},{13,12},{... | collective-permute-start | bytes 110600 | tf_op jit(solution)/shard_map/ppermute | solution.py:17
  59.1 11.3 %collective-permute-start.9 = (f32[18,1,512]{2,1,0:T(1,128)S(1)}, f32[18,1,512]{2,1,0:T(1,128)S(1)}, u32[]{:S(2)}, u32[]{:S(2)}) collective-permute-start(f32[18,1,512]{2,1,0:T(1,128)S(1)} %get-tuple-element.22), channel_id=1, source_target_pairs={{0,1},{1,2},{2,3},{4,5},{5,6},{6,7},{8,9},{9,10},{10,11},{12,13},{... | collective-permute-start | bytes 110600 | tf_op jit(solution)/shard_map/ppermute | solution.py:14
  64.8 15.7 %collective-permute-start.10 = (f32[18,1,512]{2,1,0:T(1,128)S(1)}, f32[18,1,512]{2,1,0:T(1,128)S(1)}, u32[]{:S(2)}, u32[]{:S(2)}) collective-permute-start(f32[18,1,512]{2,1,0:T(1,128)S(1)} %get-tuple-element.20), channel_id=1, source_target_pairs={{1,0},{2,1},{3,2},{5,4},{6,5},{7,6},{9,8},{10,9},{11,10},{13,12},{... | collective-permute-start | bytes 110600 | tf_op jit(solution)/shard_map/ppermute | solution.py:17
  66.1 14.4 %collective-permute-start.8 = (f32[18,1,512]{2,1,0:T(1,128)S(1)}, f32[18,1,512]{2,1,0:T(1,128)S(1)}, u32[]{:S(2)}, u32[]{:S(2)}) collective-permute-start(f32[18,1,512]{2,1,0:T(1,128)S(1)} %get-tuple-element.21), channel_id=1, source_target_pairs={{0,1},{1,2},{2,3},{4,5},{5,6},{6,7},{8,9},{9,10},{10,11},{12,13},{... | collective-permute-start | bytes 110600 | tf_op jit(solution)/shard_map/ppermute | solution.py:14
  80.5 3.0 %copy-start = (f32[16,64,512]{2,1,0:T(8,128)S(1)}, f32[16,64,512]{2,1,0:T(8,128)}, u32[]{:S(2)}) copy-start(f32[16,64,512]{2,1,0:T(8,128)} %get-tuple-element.8) | copy-start | bytes 6291460
  80.5 3.0 %copy-start.7 = (f32[16,64,512]{2,1,0:T(8,128)S(1)}, f32[16,64,512]{2,1,0:T(8,128)}, u32[]{:S(2)}) copy-start(f32[16,64,512]{2,1,0:T(8,128)} %param.12) | copy-start | bytes 6291460
  96.3 8.6 %collective-permute-start.12 = (f32[1,64,512]{2,1,0:T(8,128)S(1)}, f32[1,64,512]{2,1,0:T(8,128)S(1)}, u32[]{:S(2)}, u32[]{:S(2)}) collective-permute-start(f32[1,64,512]{2,1,0:T(8,128)S(1)} %get-tuple-element.26), channel_id=1, source_target_pairs={{0,4},{4,8},{8,12},{12,16},{16,20},{20,24},{24,28},{1,5},{5,9},{9,... | collective-permute-start | bytes 393224 | tf_op jit(solution)/shard_map/ppermute | solution.py:14
  101.2 8.1 %collective-permute-start.13 = (f32[1,64,512]{2,1,0:T(8,128)S(1)}, f32[1,64,512]{2,1,0:T(8,128)S(1)}, u32[]{:S(2)}, u32[]{:S(2)}) collective-permute-start(f32[1,64,512]{2,1,0:T(8,128)S(1)} %get-tuple-element.27), channel_id=1, source_target_pairs={{4,0},{8,4},{12,8},{16,12},{20,16},{24,20},{28,24},{5,1},{9,5},{13... | collective-permute-start | bytes 393224 | tf_op jit(solution)/shard_map/ppermute | solution.py:17
  109.3 3.8 %collective-permute-start.14 = (f32[18,1,512]{2,1,0:T(1,128)S(1)}, f32[18,1,512]{2,1,0:T(1,128)S(1)}, u32[]{:S(2)}, u32[]{:S(2)}) collective-permute-start(f32[18,1,512]{2,1,0:T(1,128)S(1)} %get-tuple-element.18), channel_id=1, source_target_pairs={{0,1},{1,2},{2,3},{4,5},{5,6},{6,7},{8,9},{9,10},{10,11},{12,13},{... | collective-permute-start | bytes 110600 | tf_op jit(solution)/shard_map/ppermute | solution.py:14
  111.7 7.5 %copy-start.4 = (f32[16,64,512]{2,1,0:T(8,128)S(1)}, f32[16,64,512]{2,1,0:T(8,128)}, u32[]{:S(2)}) copy-start(f32[16,64,512]{2,1,0:T(8,128)} %get-tuple-element.6) | copy-start | bytes 6291460
  111.7 3.3 %collective-permute-start.15 = (f32[18,1,512]{2,1,0:T(1,128)S(1)}, f32[18,1,512]{2,1,0:T(1,128)S(1)}, u32[]{:S(2)}, u32[]{:S(2)}) collective-permute-start(f32[18,1,512]{2,1,0:T(1,128)S(1)} %get-tuple-element.19), channel_id=1, source_target_pairs={{1,0},{2,1},{3,2},{5,4},{6,5},{7,6},{9,8},{10,9},{11,10},{13,12},{... | collective-permute-start | bytes 110600 | tf_op jit(solution)/shard_map/ppermute | solution.py:17
  128.8 7.3 %collective-permute-start.16 = (f32[1,64,512]{2,1,0:T(8,128)S(1)}, f32[1,64,512]{2,1,0:T(8,128)S(1)}, u32[]{:S(2)}, u32[]{:S(2)}) collective-permute-start(f32[1,64,512]{2,1,0:T(8,128)S(1)} %get-tuple-element.24), channel_id=1, source_target_pairs={{0,4},{4,8},{8,12},{12,16},{16,20},{20,24},{24,28},{1,5},{5,9},{9,... | collective-permute-start | bytes 393224 | tf_op jit(solution)/shard_map/ppermute | solution.py:14
  133.7 6.9 %collective-permute-start.17 = (f32[1,64,512]{2,1,0:T(8,128)S(1)}, f32[1,64,512]{2,1,0:T(8,128)S(1)}, u32[]{:S(2)}, u32[]{:S(2)}) collective-permute-start(f32[1,64,512]{2,1,0:T(8,128)S(1)} %get-tuple-element.25), channel_id=1, source_target_pairs={{4,0},{8,4},{12,8},{16,12},{20,16},{24,20},{28,24},{5,1},{9,5},{13... | collective-permute-start | bytes 393224 | tf_op jit(solution)/shard_map/ppermute | solution.py:17
  140.6 4.7 %collective-permute-start.18 = (f32[18,1,512]{2,1,0:T(1,128)S(1)}, f32[18,1,512]{2,1,0:T(1,128)S(1)}, u32[]{:S(2)}, u32[]{:S(2)}) collective-permute-start(f32[18,1,512]{2,1,0:T(1,128)S(1)} %get-tuple-element.16), channel_id=1, source_target_pairs={{0,1},{1,2},{2,3},{4,5},{5,6},{6,7},{8,9},{9,10},{10,11},{12,13},{... | collective-permute-start | bytes 110600 | tf_op jit(solution)/shard_map/ppermute | solution.py:14
  143.8 4.0 %collective-permute-start.19 = (f32[18,1,512]{2,1,0:T(1,128)S(1)}, f32[18,1,512]{2,1,0:T(1,128)S(1)}, u32[]{:S(2)}, u32[]{:S(2)}) collective-permute-start(f32[18,1,512]{2,1,0:T(1,128)S(1)} %get-tuple-element.17), channel_id=1, source_target_pairs={{1,0},{2,1},{3,2},{5,4},{6,5},{7,6},{9,8},{10,9},{11,10},{13,12},{... | collective-permute-start | bytes 110600 | tf_op jit(solution)/shard_map/ppermute | solution.py:17
  145.3 6.6 %copy-start.5 = (f32[16,64,512]{2,1,0:T(8,128)S(1)}, f32[16,64,512]{2,1,0:T(8,128)}, u32[]{:S(2)}) copy-start(f32[16,64,512]{2,1,0:T(8,128)} %get-tuple-element.6) | copy-start | bytes 6291460
  162.3 8.6 %copy-start.10 = (s32[256,1]{0,1:T(1,128)S(1)}, s32[256,1]{0,1:T(1,128)}, u32[]{:S(2)}) copy-start(s32[256,1]{0,1:T(1,128)} %copy-done.9) | copy-start | bytes 3076
  164.9 14.3 %all-to-all-start.2 = ((bf16[32,16,128]{2,1,0:T(8,128)(2,1)}), bf16[32,16,128]{2,1,0:T(8,128)(2,1)S(1)}, u32[]{:S(2)}, u32[]{:S(2)}) async-start(bf16[32,16,128]{2,1,0:T(8,128)(2,1)} %bitcast.16), calls=%async_computation.2 | async-start | bytes 262144 | tf_op jit(solution)/shard_map/all_to_all | solution.py:89
  (2 other events, 5.1 us)
where the time goes:
time: 182 us; the launch traced here: 181 us
  starting transfers between devices  72.2 us (40%)
  other arithmetic  61 us (34%)
  waiting for transfers between devices  27.9 us (15%)
  local copies, waits for them, and re-layouts  18.3 us (10%)
    ppermute x10, starting transfers between devices, with_halo(): lax.ppermute(lax.slice_in_dim(block, block.shape[dim] - width, None, axis...  39.1 us
    div x2, other arithmetic, sweep(): return (total - rhs) / weight  22.4 us
    ppermute x10, waiting for transfers between devices, with_halo(): lax.ppermute(lax.slice_in_dim(block, 0, width, axis=dim), axis, backward)  16.1 us
    concatenate x6, other arithmetic, with_halo(): block = jnp.concatenate([low, block, high], axis=dim)  16 us
    ppermute x10, starting transfers between devices, with_halo(): lax.ppermute(lax.slice_in_dim(block, 0, width, axis=dim), axis, backward)  13.3 us
    convert_element_type x1, other arithmetic, body(): wall_rows = pressure.reshape(-1, 128).astype(jnp.bfloat16)[got_seg]  10.4 us
    all_to_all x1, waiting for transfers between devices, body(): lax.all_to_all(wall_rows, ('slab', 'depth'), split_axis=0, concat_axis=0,...  8.18 us
    all_to_all x1, starting transfers between devices, body(): lax.all_to_all(send_seg, ('slab', 'depth'), split_axis=0, concat_axis=0,...  7 us
  transfers between devices with their start and end apart: 23, of which 8 were waited for; matrix products, arithmetic and copies ran while one was open for 15% of the time, Pallas kernels for 0%

commit v1 on v0

v1 whole, which is shorter than its diff:
```python
import functools

import jax
import jax.numpy as jnp
from jax import lax
from jax.experimental import pallas as pl
from jax.experimental.pallas import tpu as pltpu
from jax.sharding import PartitionSpec as P

COURANT = 0.2
LANES = 128
SUB = 8
DIGIT = 256
MIB = 1 << 20
F32 = jnp.float32
BF16 = jnp.bfloat16

WHOLE = pl.BlockSpec(memory_space=pltpu.VMEM)
FAR = pl.BlockSpec(memory_space=pltpu.HBM)
DMA = pltpu.SemaphoreType.DMA


def call(kernel, outs, *args, aliases=None, far_in=(), far_out=(), in_specs=None, scratch=(), limit=12 * MIB, name=None):
    specs = [FAR if n in far_in else WHOLE for n in range(len(args))]
    for n, spec in (in_specs or {}).items():
        specs[n] = spec
    shapes = [o if n in far_out else pltpu.VMEM(o.shape, o.dtype) for n, o in enumerate(outs)]
    return pl.pallas_call(
        kernel,
        out_shape=shapes,
        in_specs=specs,
        out_specs=[FAR if n in far_out else WHOLE for n in range(len(outs))],
        scratch_shapes=list(scratch),
        input_output_aliases=aliases or {},
        compiler_params=pltpu.CompilerParams(vmem_limit_bytes=limit),
        name=name,
    )(*(pltpu.with_memory_space_constraint(a, pltpu.HBM) if n in far_in else a for n, a in enumerate(args)))


def shape(dims, dtype=F32):
    return jax.ShapeDtypeStruct(tuple(dims), dtype)


def even(axis):
    return lax.rem(lax.axis_index(axis), 2) == 0


def swap(block, axis, odd):
    count = lax.axis_size(axis)
    pairs = []
    for i in range(odd, count - 1, 2):
        pairs += [(i, i + 1), (i + 1, i)]
    if not pairs:
        return jnp.zeros_like(block)
    return lax.ppermute(block, axis, pairs)


def row_is(rows, index):
    return lax.broadcasted_iota(jnp.int32, rows, 0) == index


def z_tiles(ref):
    last = ref.shape[1] // SUB - 1
    return [ref.at[:, pl.ds(0, SUB), :], ref.at[:, pl.ds(last * SUB, SUB), :]]


def x_planes(ref):
    return [ref.at[0], ref.at[ref.shape[0] - 1]]


def fetch(sources, targets, sems):
    copies = []
    for n, (source, target) in enumerate(zip(sources, targets)):
        copies.append(pltpu.make_async_copy(source, target, sems.at[n]))
        copies[-1].start()
    return copies


def pack_first(alpha, vx, vz, xe, xo, ze, zo, a0, a1, az0, az1, vx0, vz0, sems):
    sources = x_planes(alpha) + z_tiles(alpha) + x_planes(vx)[:1] + z_tiles(vz)[:1]
    for copy in fetch(sources, [a0, a1, az0, az1, vx0, vz0], sems):
        copy.wait()
    ev_x = even("slab")
    ev_z = even("depth")

    def fold(v, a):
        return jnp.where(v > 0, v, v * a)

    for k in range(a0.shape[0] // SUB):
        at = pl.ds(k * SUB, SUB)
        up = a1[at, :]
        down = fold(vx0[at, :], a0[at, :])
        xe[at, :] = jnp.where(ev_x, up, down).astype(BF16)
        xo[at, :] = jnp.where(ev_x, down, up).astype(BF16)
    for x in range(az0.shape[0]):
        up = az1[x, SUB - 1:SUB, :]
        down = fold(vz0[x, 0:1, :], az0[x, 0:1, :])
        ze[x:x + 1, :] = jnp.where(ev_z, up, down)
        zo[x:x + 1, :] = jnp.where(ev_z, down, up)


def route(capacity, rows, devices, dest, seg, rec, send, slot_out):
    panels = dest.shape[1]
    d = dest[...]
    s = seg[...]
    hot = lax.broadcasted_iota(jnp.int32, (devices, panels), 0) == d
    hot_f = jnp.where(hot, 1.0, 0.0)
    before_me = lax.broadcasted_iota(jnp.int32, (panels, panels), 0) < lax.broadcasted_iota(
        jnp.int32, (panels, panels), 1
    )
    before = jnp.dot(
        hot_f.astype(BF16), jnp.where(before_me, 1.0, 0.0).astype(BF16), preferred_element_type=F32
    )
    slot = jnp.sum(before * hot_f, axis=0, keepdims=True).astype(jnp.int32)
    place = d * rows + slot
    pick = lax.broadcasted_iota(jnp.int32, (devices * rows, panels), 0) == place
    records = jnp.dot(jnp.where(pick, 1.0, 0.0).astype(BF16), rec[...], preferred_element_type=F32)
    high = (s // DIGIT).astype(F32)
    low = (s % DIGIT).astype(F32)
    lane = lax.broadcasted_iota(jnp.int32, (LANES, panels), 0)
    at_high = jnp.where(lane == slot, 1.0, 0.0).astype(BF16)
    at_low = jnp.where(lane == slot + capacity, 1.0, 0.0).astype(BF16)
    contract = (((1,), (1,)), ((), ()))
    digits = lax.dot_general(
        (hot_f * high).astype(BF16), at_high, contract, preferred_element_type=F32
    ) + lax.dot_general((hot_f * low).astype(BF16), at_low, contract, preferred_element_type=F32)
    records = records.reshape(devices, rows, LANES)
    is_digit = lax.broadcasted_iota(jnp.int32, records.shape, 1) >= capacity
    send[...] = jnp.where(is_digit, digits[:, None, :], records).astype(BF16)
    slot_out[...] = d * capacity + slot


def parts_of(cells_x):
    step = max(1, cells_x // 4)
    return [(first, min(step, cells_x - first)) for first in range(0, cells_x, step)]


def fetch_field(source, target, sems, row):
    copies = []
    for n, (first, count) in enumerate(parts_of(target.shape[0])):
        planes = pl.ds(first, count)
        copies.append(pltpu.make_async_copy(source.at[planes], target.at[planes], sems.at[row, n]))
        copies[-1].start()
    return copies


def advect(
    alpha_h, vx_h, vz_h, p_h, xe_in, xo_in, ze_in, zo_in,
    out_h, xe, xo, ze, zo,
    alpha, vx, vz, out, p0, p1, pz0, pz1, sems, p_sems,
):
    cells_x, cells_z, beam = alpha.shape
    chunks = cells_z // SUB
    ev_x = even("slab")
    ev_z = even("depth")
    top = row_is((SUB, beam), 0)
    bottom = row_is((SUB, beam), SUB - 1)
    parts = parts_of(cells_x)
    ins = [fetch_field(h, v, sems, n) for n, (h, v) in enumerate(((alpha_h, alpha), (vx_h, vx), (vz_h, vz)))]
    p_ins = fetch(x_planes(p_h) + z_tiles(p_h), [p0, p1, pz0, pz1], p_sems)
    outs = [
        pltpu.make_async_copy(out.at[pl.ds(f, c)], out_h.at[pl.ds(f, c)], sems.at[len(ins), n])
        for n, (f, c) in enumerate(parts)
    ]

    def at(k):
        return pl.ds(k * SUB, SUB)

    def plane(x, first, last):
        zlo = jnp.where(ev_z, zo_in[pl.ds(x, 1), :], ze_in[pl.ds(x, 1), :])
        zhi = jnp.where(ev_z, ze_in[pl.ds(x, 1), :], zo_in[pl.ds(x, 1), :])
        above = None
        for k in reversed(range(chunks)):
            a = alpha[x, at(k), :]
            v = vx[x, at(k), :]
            if first:
                am = jnp.where(ev_x, xo_in[at(k), :], xe_in[at(k), :]).astype(F32)
            else:
                am = alpha[x - 1, at(k), :]
            fx = v * jnp.where(v > 0, am, a)
            if last:
                q = jnp.where(ev_x, xe_in[at(k), :], xo_in[at(k), :]).astype(F32)
                fxn = jnp.where(q > 0, q * a, q)
            else:
                vn = vx[x + 1, at(k), :]
                fxn = vn * jnp.where(vn > 0, a, alpha[x + 1, at(k), :])
            w = vz[x, at(k), :]
            if k == 0:
                edge = jnp.broadcast_to(zlo, a.shape)
            else:
                edge = pltpu.roll(alpha[x, at(k - 1), :], 1, 0)
            ad = jnp.where(top, edge, pltpu.roll(a, 1, 0))
            fz = w * jnp.where(w > 0, ad, a)
            up = pltpu.roll(fz, SUB - 1, 0)
            if above is None:
                q = jnp.broadcast_to(zhi, a.shape)
                fzn = jnp.where(bottom, jnp.where(q > 0, q * a, q), up)
            else:
                fzn = jnp.where(bottom, above, up)
            above = up
            new = a - COURANT * (fxn - fx + fzn - fz)
            out[x, at(k), :] = new
            if k == chunks - 1:
                z_up = new[SUB - 1:SUB, :] - 0.5
            if k == 0:
                z_down = new[0:1, :] - 0.5
        ze[0, pl.ds(x, 1), :] = jnp.where(ev_z, z_up, z_down)
        zo[0, pl.ds(x, 1), :] = jnp.where(ev_z, z_down, z_up)

    for n, (first, count) in enumerate(parts):
        for copies in ins:
            copies[n].wait()
        begin = max(first - 1, 0)
        end = first + count - 1
        if begin == 0:
            plane(0, True, end == begin and cells_x == 1)
            begin = 1

        @pl.loop(begin, end)
        def _(x):
            plane(x, False, False)

        if n == len(parts) - 1:
            plane(cells_x - 1, False, True)
        if n > 0:
            outs[n - 1].start()
    outs[-1].start()

    for copy in p_ins:
        copy.wait()
    for k in range(chunks):
        for which, up, down in ((0, out[cells_x - 1, at(k), :] - 0.5, out[0, at(k), :] - 0.5), (1, p1[at(k), :], p0[at(k), :])):
            xe[which, at(k), :] = jnp.where(ev_x, up, down).astype(BF16)
            xo[which, at(k), :] = jnp.where(ev_x, down, up).astype(BF16)
    for x in range(cells_x):
        up = pz1[x, SUB - 1:SUB, :]
        down = pz0[x, 0:1, :]
        ze[1, x:x + 1, :] = jnp.where(ev_z, up, down)
        zo[1, x:x + 1, :] = jnp.where(ev_z, down, up)
    for copy in outs:
        copy.wait()


def coefficients(alpha_h, after, alpha, cx, cz, cy, inverse, sems):
    del after
    cells_x, cells_z, beam = alpha.shape
    chunks = cells_z // SUB
    top = row_is((SUB, beam), 0)
    bottom = row_is((SUB, beam), SUB - 1)
    lane = lax.broadcasted_iota(jnp.int32, (SUB, beam), 1)
    ins = fetch_field(alpha_h, alpha, sems, 0)
    cx[0] = jnp.zeros((cells_z, beam), F32)

    def at(k):
        return pl.ds(k * SUB, SUB)

    def plane(x):
        inside = jnp.where(x < cells_x - 1, 2.0, 0.0)
        nxt = jnp.minimum(x + 1, cells_x - 1)
        above = jnp.zeros((SUB, beam), F32)
        for k in reversed(range(chunks)):
            rho = 1.0 + 9.0 * alpha[x, at(k), :]
            rho_x = 1.0 + 9.0 * alpha[nxt, at(k), :]
            hx = inside / (rho + rho_x)
            cx[x + 1, at(k), :] = hx
            rolled = pltpu.roll(rho, 1, 0)
            if k == 0:
                hz = jnp.where(top, 0.0, 2.0 / (rho + rolled))
            else:
                below = pltpu.roll(1.0 + 9.0 * alpha[x, at(k - 1), :], 1, 0)
                hz = 2.0 / (rho + jnp.where(top, below, rolled))
            cz[x, at(k), :] = hz
            up = pltpu.roll(hz, SUB - 1, 0)
            hz_up = jnp.where(bottom, above, up)
            above = up
            hy_all = 2.0 / (rho + jnp.where(lane == 0, 0.0, pltpu.roll(rho, 1, 1)))
            hy = jnp.where(lane == 0, 0.0, hy_all)
            cy[x, at(k), :] = hy
            far = rho[:, beam - LANES:]
            edge = jnp.where(lane[:, beam - LANES:] == beam - 1, 2.0 / far, 0.0)
            hy_up = pltpu.roll(hy, beam - 1, 1)
            hy_up = jnp.concatenate(
                [hy_up[:, : beam - LANES], hy_up[:, beam - LANES:] + edge], axis=1
            )
            inverse[x, at(k), :] = 1.0 / (cx[x, at(k), :] + hx + hz + hz_up + hy_all + hy_up)

    parts = parts_of(cells_x)
    for n, (first, count) in enumerate(parts):
        ins[n].wait()
        end = cells_x if n == len(parts) - 1 else first + count - 1

        @pl.loop(max(first - 1, 0), end)
        def _(x):
            plane(x)


def close(
    p_in, inverse_in, alpha, xe_in, xo_in, ze_in, zo_in,
    p, inverse, gx, gz, xe, xo, ze, zo,
    wx,
):
    del p_in, inverse_in
    cells_x, cells_z, beam = alpha.shape
    chunks = cells_z // SUB
    i, j = lax.axis_index("slab"), lax.axis_index("depth")
    ev_x, ev_z = even("slab"), even("depth")
    has = [
        [jnp.where(i > 0, 1.0, 0.0), jnp.where(i < lax.axis_size("slab") - 1, 1.0, 0.0)],
        [jnp.where(j > 0, 1.0, 0.0), jnp.where(j < lax.axis_size("depth") - 1, 1.0, 0.0)],
    ]

    def at(k):
        return pl.ds(k * SUB, SUB)

    for side, x in ((0, 0), (1, cells_x - 1)):
        for k in range(chunks):
            a, b = xe_in[:, at(k), :], xo_in[:, at(k), :]
            v = (jnp.where(ev_x, a, b) if side else jnp.where(ev_x, b, a)).astype(F32)
            halo = has[0][side] * (9.0 * v[0] + 5.5)
            c = 2.0 / (1.0 + 9.0 * alpha[x, at(k), :] + halo)
            w = 1.0 / inverse[x, at(k), :]
            p[x, at(k), :] = p[x, at(k), :] * w + c * v[1]
            gx[side, at(k), :] = c
            wx[side, at(k), :] = w + c

    def rows(x, plane):
        faces = []
        for side, k in ((0, 0), (1, chunks - 1)):
            here = row_is((SUB, beam), 0 if side == 0 else SUB - 1)
            a, b = ze_in[:, pl.ds(x, 1), :], zo_in[:, pl.ds(x, 1), :]
            v = jnp.where(ev_z, a, b) if side else jnp.where(ev_z, b, a)
            halo = jnp.broadcast_to(has[1][side] * (9.0 * v[0] + 5.5), (SUB, beam))
            c = jnp.where(here, 2.0 / (1.0 + 9.0 * alpha[x, at(k), :] + halo), 0.0)
            add = c * jnp.broadcast_to(v[1], (SUB, beam))
            if plane is None:
                w = 1.0 / inverse[x, at(k), :]
                total = p[x, at(k), :] * w + add
                inv = 1.0 / (w + c)
                inverse[x, at(k), :] = inv
                new = total * inv
                p[x, at(k), :] = new
            else:
                w = wx[plane, at(k), :] + c
                wx[plane, at(k), :] = w
                inv = 1.0 / w
                total = p[x, at(k), :] + add
                p[x, at(k), :] = total
                new = total * inv
            g = inv * c
            r = slice(0, 1) if side == 0 else slice(SUB - 1, SUB)
            gz[side, pl.ds(x, 1), :] = g[r, :]
            faces.append(new[r, :])
        ze[pl.ds(x, 1), :] = jnp.where(ev_z, faces[1], faces[0])
        zo[pl.ds(x, 1), :] = jnp.where(ev_z, faces[0], faces[1])

    rows(0, 0)
    rows(cells_x - 1, 1)

    @pl.loop(1, cells_x - 1)
    def _(x):
        rows(x, None)

    for k in range(chunks):
        new = []
        for side, x in ((0, 0), (1, cells_x - 1)):
            inv = 1.0 / wx[side, at(k), :]
            inverse[x, at(k), :] = inv
            gx[side, at(k), :] = gx[side, at(k), :] * inv
            new.append(p[x, at(k), :] * inv)
            p[x, at(k), :] = new[side]
        xe[at(k), :] = jnp.where(ev_x, new[1], new[0]).astype(BF16)
        xo[at(k), :] = jnp.where(ev_x, new[0], new[1]).astype(BF16)


def by_lanes(ref):
    cells_x, cells_z, beam = ref.shape
    blocks = beam // LANES
    for b in range(blocks):
        yield b, pl.ds(b * LANES, LANES)


def scatter(capacity, got, div_h, rhs, row_out, rec32, row_v, row_s, hull, div, sems, sem):
    devices, rows, _ = got.shape
    cells_x, cells_z, beam = rhs.shape
    blocks = beam // LANES
    ins = fetch_field(div_h, div, sems, 0)
    digits = got[:, rows - 1, :].astype(F32)
    seg = (digits * float(DIGIT) + pltpu.roll(digits, LANES - capacity, 1)).astype(jnp.int32)
    across = seg // blocks
    row = ((across // cells_z) * blocks + seg % blocks) * cells_z + across % cells_z
    row_v[...] = row
    row_out[...] = row
    copy = pltpu.make_async_copy(row_v, row_s, sem)
    copy.start()
    rec32[...] = got[...].astype(F32).reshape(devices * rows, LANES)
    hull[...] = jnp.zeros_like(hull)
    copy.wait()

    @pl.loop(0, devices)
    def _(d):
        for s in range(capacity):
            n = row_s[d, s]
            hull[pl.ds(n, 1), :] += rec32[pl.ds(d * rows + s, 1), :]

    for copy in ins:
        copy.wait()

    @pl.loop(0, cells_x)
    def _(x):
        for b, lanes in by_lanes(rhs):
            first = pl.multiple_of((x * blocks + b) * cells_z, SUB)
            rhs[x, :, lanes] = div[x, :, lanes] + hull[pl.ds(first, cells_z), :]


def sweep(p, cx, cz, cy, inverse, rhs, out):
    cells_x, cells_z, beam = p.shape
    chunks = cells_z // SUB
    top = row_is((SUB, beam), 0)
    bottom = row_is((SUB, beam), SUB - 1)

    def at(k):
        return pl.ds(k * SUB, SUB)

    @pl.loop(0, cells_x)
    def _(x):
        prv = jnp.maximum(x - 1, 0)
        nxt = jnp.minimum(x + 1, cells_x - 1)
        above = jnp.zeros((SUB, beam), F32)
        rolled = pltpu.roll(p[x, at(chunks - 1), :], 1, 0)
        for k in reversed(range(chunks)):
            here = p[x, at(k), :]
            hz = cz[x, at(k), :]
            hy = cy[x, at(k), :]
            total = cx[x, at(k), :] * p[prv, at(k), :] + cx[x + 1, at(k), :] * p[nxt, at(k), :]
            if k > 0:
                below = pltpu.roll(p[x, at(k - 1), :], 1, 0)
                down = jnp.where(top, below, rolled)
                rolled = below
            else:
                down = rolled
            up = pltpu.roll(hz * here, SUB - 1, 0)
            total = total + (hz * down + jnp.where(bottom, above, up))
            above = up
            total = total + (hy * pltpu.roll(here, 1, 1) + pltpu.roll(hy * here, beam - 1, 1))
            out[x, at(k), :] = (total - rhs[x, at(k), :]) * inverse[x, at(k), :]


def add_borders(p_in, xe_in, xo_in, ze_in, zo_in, gx, gz, p, send=None):
    del p_in
    cells_x, cells_z, beam = p.shape
    chunks = cells_z // SUB
    ev_x, ev_z = even("slab"), even("depth")

    def at(k):
        return pl.ds(k * SUB, SUB)

    for side, x in ((0, 0), (1, cells_x - 1)):
        for k in range(chunks):
            a, b = xe_in[at(k), :], xo_in[at(k), :]
            v = jnp.where(ev_x, a, b) if side else jnp.where(ev_x, b, a)
            p[x, at(k), :] = p[x, at(k), :] + gx[side, at(k), :] * v.astype(F32)

    @pl.loop(0, cells_x)
    def _(x):
        faces = []
        for side, k in ((0, 0), (1, chunks - 1)):
            here = row_is((SUB, beam), 0 if side == 0 else SUB - 1)
            a, b = ze_in[pl.ds(x, 1), :], zo_in[pl.ds(x, 1), :]
            v = jnp.where(ev_z, a, b) if side else jnp.where(ev_z, b, a)
            add = jnp.broadcast_to(gz[side, pl.ds(x, 1), :] * v, (SUB, beam))
            new = p[x, at(k), :] + jnp.where(here, add, 0.0)
            p[x, at(k), :] = new
            faces.append(new[0:1, :] if side == 0 else new[SUB - 1:SUB, :])
        if send is not None:
            send[2][pl.ds(x, 1), :] = jnp.where(ev_z, faces[1], faces[0])
            send[3][pl.ds(x, 1), :] = jnp.where(ev_z, faces[0], faces[1])

    if send is not None:
        for k in range(chunks):
            lo, hi = p[0, at(k), :], p[cells_x - 1, at(k), :]
            send[0][at(k), :] = jnp.where(ev_x, hi, lo).astype(BF16)
            send[1][at(k), :] = jnp.where(ev_x, lo, hi).astype(BF16)


def fix_and_send(p_in, xe_in, xo_in, ze_in, zo_in, gx, gz, p, xe, xo, ze, zo):
    add_borders(p_in, xe_in, xo_in, ze_in, zo_in, gx, gz, p, (xe, xo, ze, zo))


def fix_and_gather(
    capacity, p_in, xe_in, xo_in, ze_in, zo_in, gx, gz, row, p_h, back, p, split, rows32, sems
):
    cells_x, cells_z, beam = p.shape
    p[...] = p_in[...]
    add_borders(p_in, xe_in, xo_in, ze_in, zo_in, gx, gz, p)
    blocks = beam // LANES
    devices = back.shape[0]
    out = pltpu.make_async_copy(p, p_h, sems)
    out.start()

    @pl.loop(0, cells_x)
    def _(x):
        for b, lanes in by_lanes(p):
            first = pl.multiple_of((x * blocks + b) * cells_z, SUB)
            split[pl.ds(first, cells_z), :] = p[x, :, lanes]

    @pl.loop(0, devices)
    def _(d):
        for s in range(capacity):
            rows32[pl.ds(d * capacity + s, 1), :] = split[pl.ds(row[d, s], 1), :]

    back[...] = rows32[...].astype(BF16).reshape(back.shape)
    out.wait()


def unroute(back, slot, out):
    rows = back.shape[0] * back.shape[1]
    panels = out.shape[0]
    pick = lax.broadcasted_iota(jnp.int32, (rows, panels), 0) == slot[...]
    out[...] = lax.dot_general(
        jnp.where(pick, 1.0, 0.0).astype(BF16),
        back[...].reshape(rows, LANES),
        (((0,), (0,)), ((), ())),
        preferred_element_type=F32,
    ).astype(BF16)


def body(alpha, vel_x, vel_z, divergence, press_guess, panel_records, panel_dest, panel_segment):
    devices = lax.axis_size("slab") * lax.axis_size("depth")
    panels = panel_records.shape[0]
    capacity = 2 * panels // devices
    cells_x, cells_z, beam = alpha.shape
    field = shape(alpha.shape)
    rows = -(-(capacity + 1) // SUB) * SUB
    axes = ("slab", "depth")

    xs, zs = (cells_z, beam), (cells_x, beam)
    tile = (cells_x, SUB, beam)
    faces = [shape(xs, BF16)] * 2 + [shape(zs)] * 2
    two_faces = [shape((2,) + xs, BF16)] * 2 + [shape((2,) + zs)] * 2
    parts = len(parts_of(cells_x))
    lines = (cells_x * cells_z * beam // LANES, LANES)

    def near(dims, dtype=F32):
        return pltpu.VMEM(tuple(dims), dtype)

    def swaps(xe, xo, ze, zo):
        return swap(xe, "slab", 0), swap(xo, "slab", 1), swap(ze, "depth", 0), swap(zo, "depth", 1)

    send, slot = call(
        functools.partial(route, capacity, rows, devices),
        [shape((devices, rows, LANES), BF16), shape((1, panels), jnp.int32)],
        panel_dest.reshape(1, panels), panel_segment.reshape(1, panels), panel_records,
        name="route",
    )
    got = lax.all_to_all(send, axes, split_axis=0, concat_axis=0, tiled=True)

    packed = call(
        pack_first, faces, alpha, vel_x, vel_z,
        far_in=(0, 1, 2),
        scratch=[near(xs), near(xs), near(tile), near(tile), near(xs), near(tile), DMA((6,))],
        name="pack_first",
    )
    alpha_next, *packed = call(
        advect, [field] + two_faces, alpha, vel_x, vel_z, press_guess, *swaps(*packed),
        far_in=(0, 1, 2, 3), far_out=(0,),
        scratch=[near(alpha.shape)] * 4 + [near(xs), near(xs), near(tile), near(tile), DMA((4, parts)), DMA((4,))],
        name="advect",
    )
    halo = swaps(*packed)
    near_alpha, cx, cz, cy, inverse = call(
        coefficients,
        [field, shape((cells_x + 1,) + xs), field, field, field],
        alpha_next, got,
        far_in=(0,),
        in_specs={1: pl.BlockSpec(memory_space=pl.ANY)},
        scratch=[DMA((1, parts))],
        name="coefficients",
    )
    rhs, row = call(
        functools.partial(scatter, capacity),
        [field, shape((devices, LANES), jnp.int32)],
        got, divergence,
        far_in=(1,),
        scratch=[
            near((devices * rows, LANES)),
            near((devices, LANES), jnp.int32),
            pltpu.SMEM((devices, LANES), jnp.int32),
            near(lines),
            near(alpha.shape),
            DMA((1, parts)),
            DMA,
        ],
        name="scatter",
    )
    (pressure,) = call(sweep, [field], press_guess, cx, cz, cy, inverse, rhs, name="sweep")
    pressure, inverse, gx, gz, *packed = call(
        close,
        [field, field, shape((2,) + xs), shape((2,) + zs)] + faces,
        pressure, inverse, near_alpha, *halo,
        aliases={0: 0, 1: 1},
        scratch=[near((2,) + xs)],
        name="close",
    )
    halo = swaps(*packed)
    (pressure,) = call(sweep, [field], pressure, cx, cz, cy, inverse, rhs, name="sweep")
    pressure, *packed = call(
        fix_and_send, [field] + faces, pressure, *halo, gx, gz, aliases={0: 0}, name="fix"
    )
    halo = swaps(*packed)
    (pressure,) = call(sweep, [field], pressure, cx, cz, cy, inverse, rhs, name="sweep")
    pressure, back = call(
        functools.partial(fix_and_gather, capacity),
        [field, shape((devices, capacity, LANES), BF16)],
        pressure, *halo, gx, gz, row,
        far_out=(0,),
        in_specs={7: pl.BlockSpec(memory_space=pltpu.SMEM)},
        scratch=[near(alpha.shape), near(lines), near((devices * capacity, LANES)), DMA],
        name="gather",
    )
    returned = lax.all_to_all(back, axes, split_axis=0, concat_axis=0, tiled=True)
    panel_pressure = pl.pallas_call(
        unroute,
        out_shape=shape((panels, LANES), BF16),
        in_specs=[WHOLE] * 2,
        out_specs=WHOLE,
        name="unroute",
    )(returned, slot)
    return (pressure, alpha_next, panel_pressure)


def solution(mesh):
    in_specs = (
        P("slab", "depth", None),
        P("slab", "depth", None),
        P("slab", "depth", None),
        P("slab", "depth", None),
        P("slab", "depth", None),
        P(("slab", "depth"), None),
        P(("slab", "depth"), None),
        P(("slab", "depth"), None),
    )
    out_specs = (P("slab", "depth", None), P("slab", "depth", None), P(("slab", "depth"), None))
    return jax.shard_map(body, mesh=mesh, in_specs=in_specs, out_specs=out_specs, check_vma=False)
```

time: 182 us -> 83.9 us (0.46)
  other arithmetic: 61 us -> 0 us
  starting transfers between devices: 72.2 us -> 36 us
  Pallas kernels: 0 us -> 26.8 us
  waiting for transfers between devices: 27.9 us -> 1.83 us
  local copies, waits for them, and re-layouts: 18.3 us -> 2.78 us
  blocking collectives: 0 us -> 15 us
    pallas_call x0 -> x12, Pallas kernels: none -> 26.8 us  [the longest x11 25 us: call(): pl.pallas_call(kernel, out_shape=shapes, in_specs=specs, out_specs=[FAR i...]
    ppermute x20 -> x16, starting transfers between devices: 52.3 us -> 28.7 us  [swap(): return lax.ppermute(block, axis, pairs)]
    div x2 -> x0, other arithmetic: 22.4 us -> none  [sweep(): return (total - rhs) / weight]
    ppermute x20 -> x16, waiting for transfers between devices: 19.7 us -> 1.83 us  [swap(): return lax.ppermute(block, axis, pairs)]
    concatenate x6 -> x0, other arithmetic: 16 us -> none  [with_halo(): block = jnp.concatenate([low, block, high], axis=dim)]
    all_to_all x0 -> x1, blocking collectives: none -> 15 us  [body(): lax.all_to_all(back, axes, split_axis=0, concat_axis=0, tiled=True)]
    all_to_all x3 -> x1, starting transfers between devices: 19.9 us -> 7.32 us  [body(): got = lax.all_to_all(send, axes, split_axis=0, concat_axis=0, tiled=True)]
    convert_element_type x2 -> x0, other arithmetic: 10.4 us -> none  [the longest x1 10.4 us: body(): wall_rows = pressure.reshape(-1, 128).astype(jnp.bfloat16)[got_seg]]
  transfers between devices with their start and end apart: 23 -> 17, of which waited for: 8 -> 2; matrix products, arithmetic and copies ran while one was open for 15% -> 0% of each run, Pallas kernels for 0% -> 24%
where the time goes in v1:
time: 83.9 us; the launch traced here: 83.3 us
  starting transfers between devices  36 us (43%)
  Pallas kernels  26.8 us (32%)
  blocking collectives  15 us (18%)
  local copies, waits for them, and re-layouts  2.78 us (3%)
  waiting for transfers between devices  1.83 us (2%)
  between operations  0.91 us (1%)
    ppermute x16, starting transfers between devices, swap(): return lax.ppermute(block, axis, pairs)  28.7 us
    pallas_call x11, Pallas kernels, call(): pl.pallas_call(kernel, out_shape=shapes, in_specs=specs, out_specs=[FAR i...  25 us
    all_to_all x1, blocking collectives, body(): lax.all_to_all(back, axes, split_axis=0, concat_axis=0, tiled=True)  15 us
    all_to_all x1, starting transfers between devices, body(): got = lax.all_to_all(send, axes, split_axis=0, concat_axis=0, tiled=True)  7.32 us
    unnamed x10, local copies, waits for them, and re-layouts  2.78 us
    ppermute x16, waiting for transfers between devices, swap(): return lax.ppermute(block, axis, pairs)  1.83 us
    pallas_call x1, Pallas kernels, body(): pl.pallas_call(unroute, out_shape=shape((panels, LANES), BF16), in_specs=...  1.82 us
  transfers between devices with their start and end apart: 17, of which 2 were waited for; matrix products, arithmetic and copies ran while one was open for 0% of the time, Pallas kernels for 24%

profile of v1, /device:TPU:0, one launch (start us, length us, event | category | flops | bytes accessed | tf_op | source)
XLA Modules:
  0.0 83.3 jit_solution(145121825937875669)
XLA Ops:
  0.6 0.8 copy-done.1
  1.5 0.7 copy-done.2
  2.2 0.7 copy-done.3
  2.8 1.1 %route.1 = (bf16[32,24,128]{2,1,0:T(8,128)(2,1)}, s32[1,256]{1,0:T(1,128)S(1)}) custom-call(s32[1,256]{1,0:T(1,128)S(1)} %bitcast.2, s32[1,256]{1,0:T(1,128)S(1)} %bitcast.3, bf16[256,128]{1,0:T(8,128)(2,1)S(1)} %copy-done.1), custom_call_target="tpu_custom_call" | custom-call | tf_op jit(solution)/shard_map/route/pallas_call | solution.py:28
  4.5 7.3 %all-to-all-start = ((bf16[32,24,128]{2,1,0:T(8,128)(2,1)}), bf16[32,24,128]{2,1,0:T(8,128)(2,1)S(1)}, u32[]{:S(2)}, u32[]{:S(2)}) async-start(bf16[32,24,128]{2,1,0:T(8,128)(2,1)} %get-tuple-element.41), calls=%async_computation | async-start | bytes 393216 | tf_op jit(solution)/shard_map/all_to_all | solution.py:555
  11.9 1.4 %pack_first.1 = (bf16[64,512]{1,0:T(8,128)(2,1)S(1)}, bf16[64,512]{1,0:T(8,128)(2,1)S(1)}, f32[16,512]{1,0:T(8,128)S(1)}, f32[16,512]{1,0:T(8,128)S(1)}) custom-call(f32[16,64,512]{2,1,0:T(8,128)} %alpha_h.1, f32[16,64,512]{2,1,0:T(8,128)} %vx_h.1, f32[16,64,512]{2,1,0:T(8,128)} %vz_h.1), custom_call_target="tpu_custom_call" | custom-call | tf_op jit(solution)/shard_map/pack_first/pallas_call | solution.py:28
  13.3 1.8 %collective-permute-start = (bf16[64,512]{1,0:T(8,128)(2,1)S(1)}, bf16[64,512]{1,0:T(8,128)(2,1)S(1)}, u32[]{:S(2)}, u32[]{:S(2)}) collective-permute-start(bf16[64,512]{1,0:T(8,128)(2,1)S(1)} %get-tuple-element.36), channel_id=1, source_target_pairs={{0,4},{4,0},{8,12},{12,8},{16,20},{20,16},{24,28},{28,24},{1,5},{5... | collective-permute-start | bytes 196616 | tf_op jit(solution)/shard_map/ppermute | solution.py:55
  15.1 0.7 collective-permute-start.1
  15.8 0.7 collective-permute-start.3
  17.0 1.3 %collective-permute-done.xe_in = bf16[64,512]{1,0:T(8,128)(2,1)S(1)} collective-permute-done((bf16[64,512]{1,0:T(8,128)(2,1)S(1)}, bf16[64,512]{1,0:T(8,128)(2,1)S(1)}, u32[]{:S(2)}, u32[]{:S(2)}) %collective-permute-start) | collective-permute-done | bytes 65568 | tf_op jit(solution)/shard_map/ppermute | solution.py:55
  18.3 5.0 %advect.1 = (f32[16,64,512]{2,1,0:T(8,128)}, bf16[2,64,512]{2,1,0:T(8,128)(2,1)S(1)}, bf16[2,64,512]{2,1,0:T(8,128)(2,1)S(1)}, f32[2,16,512]{2,1,0:T(8,128)S(1)}, f32[2,16,512]{2,1,0:T(8,128)S(1)}) custom-call(f32[16,64,512]{2,1,0:T(8,128)} %alpha_h.1, f32[16,64,512]{2,1,0:T(8,128)} %vx_h.1, f32[16,64,512]{2,1,0:T(8,128)} %vz_h.1, f32[16,64,512]{2,1,0:T(8,128)} %p.1, ...), custom_call_target="tpu_custom_call" | custom-call | tf_op jit(solution)/shard_map/advect/pallas_call | solution.py:28
  23.3 4.2 %collective-permute-start.4 = (bf16[2,64,512]{2,1,0:T(8,128)(2,1)S(1)}, bf16[2,64,512]{2,1,0:T(8,128)(2,1)S(1)}, u32[]{:S(2)}, u32[]{:S(2)}) collective-permute-start(bf16[2,64,512]{2,1,0:T(8,128)(2,1)S(1)} %get-tuple-element.48), channel_id=1, source_target_pairs={{0,4},{4,0},{8,12},{12,8},{16,20},{20,16},{24,28},{28,24},{1,5},{5... | collective-permute-start | bytes 393224 | tf_op jit(solution)/shard_map/ppermute | solution.py:55
  27.5 0.7 collective-permute-start.5
  28.1 3.1 %collective-permute-start.6 = (f32[2,16,512]{2,1,0:T(8,128)S(1)}, f32[2,16,512]{2,1,0:T(8,128)S(1)}, u32[]{:S(2)}, u32[]{:S(2)}) collective-permute-start(f32[2,16,512]{2,1,0:T(8,128)S(1)} %get-tuple-element.50), channel_id=1, source_target_pairs={{0,1},{1,0},{2,3},{3,2},{4,5},{5,4},{6,7},{7,6},{8,9},{9,8},{10,11... | collective-permute-start | bytes 196616 | tf_op jit(solution)/shard_map/ppermute | solution.py:55
  31.2 0.8 collective-permute-start.7
  32.0 2.6 %scatter.1 = (f32[16,64,512]{2,1,0:T(8,128)S(1)}, s32[32,128]{1,0:T(8,128)S(1)}) custom-call(bf16[32,24,128]{2,1,0:T(8,128)(2,1)S(1)} %all-to-all-done.after.got, f32[16,64,512]{2,1,0:T(8,128)} %div_h.1), custom_call_target="tpu_custom_call" | custom-call | tf_op jit(solution)/shard_map/scatter/pallas_call | solution.py:28
  34.7 4.6 %coefficients.1 = (f32[16,64,512]{2,1,0:T(8,128)S(1)}, f32[17,64,512]{2,1,0:T(8,128)S(1)}, f32[16,64,512]{2,1,0:T(8,128)S(1)}, f32[16,64,512]{2,1,0:T(8,128)S(1)}, f32[16,64,512]{2,1,0:T(8,128)S(1)}) custom-call(f32[16,64,512]{2,1,0:T(8,128)} %get-tuple-element.34.alpha_h, bf16[32,24,128]{2,1,0:T(8,128)(2,1)S(1)} %all-to-all-done.after.got), custom_call_target="tpu_custom_call" | custom-call | tf_op jit(solution)/shard_map/coefficients/pallas_call | solution.py:28
  39.3 2.2 %sweep.3.p_in = f32[16,64,512]{2,1,0:T(8,128)S(1)} custom-call(f32[16,64,512]{2,1,0:T(8,128)S(1)} %copy-done, f32[17,64,512]{2,1,0:T(8,128)S(1)} %get-tuple-element.42.cx, f32[16,64,512]{2,1,0:T(8,128)S(1)} %get-tuple-element.43.cz, f32[16,64,512]{2,1,0:T(8,128)S(1)} %get-tuple-element.44.cy, f32[16,64,512]{2,1,0:T(8,128)S(1)} %get-tuple-element.45.inverse.inverse_in, ...), custom_call_target="tpu_custom_call" | custom-call | tf_op jit(solution)/shard_map/sweep/pallas_call | solution.py:28
  41.6 0.8 close.1
  42.3 5.4 %collective-permute-start.8 = (bf16[64,512]{1,0:T(8,128)(2,1)S(1)}, bf16[64,512]{1,0:T(8,128)(2,1)S(1)}, u32[]{:S(2)}, u32[]{:S(2)}) collective-permute-start(bf16[64,512]{1,0:T(8,128)(2,1)S(1)} %get-tuple-element.54), channel_id=1, source_target_pairs={{0,4},{4,0},{8,12},{12,8},{16,20},{20,16},{24,28},{28,24},{1,5},{5... | collective-permute-start | bytes 196616 | tf_op jit(solution)/shard_map/ppermute | solution.py:55
  47.8 0.7 collective-permute-start.9
  48.4 2.4 %collective-permute-start.10 = (f32[16,512]{1,0:T(8,128)S(1)}, f32[16,512]{1,0:T(8,128)S(1)}, u32[]{:S(2)}, u32[]{:S(2)}) collective-permute-start(f32[16,512]{1,0:T(8,128)S(1)} %get-tuple-element.56), channel_id=1, source_target_pairs={{0,1},{1,0},{2,3},{3,2},{4,5},{5,4},{6,7},{7,6},{8,9},{9,8},{10,11... | collective-permute-start | bytes 98312 | tf_op jit(solution)/shard_map/ppermute | solution.py:55
  50.8 0.7 collective-permute-start.11
  51.5 2.2 %sweep.4.p_in = f32[16,64,512]{2,1,0:T(8,128)S(1)} custom-call(f32[16,64,512]{2,1,0:T(8,128)S(1)} %get-tuple-element.52.p, f32[17,64,512]{2,1,0:T(8,128)S(1)} %get-tuple-element.42.cx, f32[16,64,512]{2,1,0:T(8,128)S(1)} %get-tuple-element.43.cz, f32[16,64,512]{2,1,0:T(8,128)S(1)} %get-tuple-element.44.cy, f32[16,64,512]{2,1,0:T(8,128)S(1)} %get-tuple-element.53.inverse, ...), custom_call_target="tpu_custom_call" | custom-call | tf_op jit(solution)/shard_map/sweep/pallas_call | solution.py:28
  54.1 4.2 %collective-permute-start.12 = (bf16[64,512]{1,0:T(8,128)(2,1)S(1)}, bf16[64,512]{1,0:T(8,128)(2,1)S(1)}, u32[]{:S(2)}, u32[]{:S(2)}) collective-permute-start(bf16[64,512]{1,0:T(8,128)(2,1)S(1)} %get-tuple-element.61), channel_id=1, source_target_pairs={{0,4},{4,0},{8,12},{12,8},{16,20},{20,16},{24,28},{28,24},{1,5},{5... | collective-permute-start | bytes 196616 | tf_op jit(solution)/shard_map/ppermute | solution.py:55
  58.3 0.7 collective-permute-start.13
  59.0 2.1 %collective-permute-start.14 = (f32[16,512]{1,0:T(8,128)S(1)}, f32[16,512]{1,0:T(8,128)S(1)}, u32[]{:S(2)}, u32[]{:S(2)}) collective-permute-start(f32[16,512]{1,0:T(8,128)S(1)} %get-tuple-element.63), channel_id=1, source_target_pairs={{0,1},{1,0},{2,3},{3,2},{4,5},{5,4},{6,7},{7,6},{8,9},{9,8},{10,11... | collective-permute-start | bytes 98312 | tf_op jit(solution)/shard_map/ppermute | solution.py:55
  61.1 0.7 collective-permute-start.15
  61.7 2.2 %sweep.5.p_in = f32[16,64,512]{2,1,0:T(8,128)S(1)} custom-call(f32[16,64,512]{2,1,0:T(8,128)S(1)} %get-tuple-element.60.p, f32[17,64,512]{2,1,0:T(8,128)S(1)} %get-tuple-element.42.cx, f32[16,64,512]{2,1,0:T(8,128)S(1)} %get-tuple-element.43.cz, f32[16,64,512]{2,1,0:T(8,128)S(1)} %get-tuple-element.44.cy, f32[16,64,512]{2,1,0:T(8,128)S(1)} %get-tuple-element.53.inverse, ...), custom_call_target="tpu_custom_call" | custom-call | tf_op jit(solution)/shard_map/sweep/pallas_call | solution.py:28
  64.0 2.5 %gather.1 = (f32[16,64,512]{2,1,0:T(8,128)}, bf16[32,16,128]{2,1,0:T(8,128)(2,1)S(1)}) custom-call(f32[16,64,512]{2,1,0:T(8,128)S(1)} %sweep.5.p_in, bf16[64,512]{1,0:T(8,128)(2,1)S(1)} %collective-permute-done.12.xe_in, bf16[64,512]{1,0:T(8,128)(2,1)S(1)} %collective-permute-done.13.xo_in, f32[16,512]{1,0:T(8,128)S(1)} %collective-permute-done.14.ze_in, ...), custom_call_target="tpu_custom_call" | custom-call | tf_op jit(solution)/shard_map/gather/pallas_call | solution.py:28
  66.5 15.0 %all_to_all.10.back = bf16[32,16,128]{2,1,0:T(8,128)(2,1)} all-to-all(bf16[32,16,128]{2,1,0:T(8,128)(2,1)S(1)} %get-tuple-element.67), channel_id=1, replica_groups=mesh['slab'=8,'depth'=4] {'slab','depth'}, dimensions={0} | all-to-all | bytes 262144 | tf_op jit(solution)/shard_map/all_to_all | solution.py:620
  81.5 1.8 %unroute.1 = bf16[256,128]{1,0:T(8,128)(2,1)} custom-call(bf16[32,16,128]{2,1,0:T(8,128)(2,1)} %all_to_all.10.back, s32[1,256]{1,0:T(1,128)} %copy-done.4), custom_call_target="tpu_custom_call" | custom-call | tf_op jit(solution)/shard_map/unroute/pallas_call | solution.py:621
  (25 shorter events, 1.6 us)
Async XLA Ops:
  0.6 0.8 %copy-start.1 = (bf16[256,128]{1,0:T(8,128)(2,1)S(1)}, bf16[256,128]{1,0:T(8,128)(2,1)}, u32[]{:S(2)}) copy-start(bf16[256,128]{1,0:T(8,128)(2,1)} %rec.1) | copy-start | bytes 196612
  1.5 0.7 copy-start.2
  2.2 0.7 copy-start.3
  4.0 0.6 copy-start.4
  4.5 27.5 %all-to-all-start = ((bf16[32,24,128]{2,1,0:T(8,128)(2,1)}), bf16[32,24,128]{2,1,0:T(8,128)(2,1)S(1)}, u32[]{:S(2)}, u32[]{:S(2)}) async-start(bf16[32,24,128]{2,1,0:T(8,128)(2,1)} %get-tuple-element.41), calls=%async_computation | async-start | bytes 393216 | tf_op jit(solution)/shard_map/all_to_all | solution.py:555
  13.3 5.0 %collective-permute-start = (bf16[64,512]{1,0:T(8,128)(2,1)S(1)}, bf16[64,512]{1,0:T(8,128)(2,1)S(1)}, u32[]{:S(2)}, u32[]{:S(2)}) collective-permute-start(bf16[64,512]{1,0:T(8,128)(2,1)S(1)} %get-tuple-element.36), channel_id=1, source_target_pairs={{0,4},{4,0},{8,12},{12,8},{16,20},{20,16},{24,28},{28,24},{1,5},{5... | collective-permute-start | bytes 196616 | tf_op jit(solution)/shard_map/ppermute | solution.py:55
  15.1 3.2 %collective-permute-start.1 = (bf16[64,512]{1,0:T(8,128)(2,1)S(1)}, bf16[64,512]{1,0:T(8,128)(2,1)S(1)}, u32[]{:S(2)}, u32[]{:S(2)}) collective-permute-start(bf16[64,512]{1,0:T(8,128)(2,1)S(1)} %get-tuple-element.37), channel_id=1, source_target_pairs={{4,8},{8,4},{12,16},{16,12},{20,24},{24,20},{5,9},{9,5},{13,17},{1... | collective-permute-start | bytes 196616 | tf_op jit(solution)/shard_map/ppermute | solution.py:55
  15.8 1.3 %collective-permute-start.2 = (f32[16,512]{1,0:T(8,128)S(1)}, f32[16,512]{1,0:T(8,128)S(1)}, u32[]{:S(2)}, u32[]{:S(2)}) collective-permute-start(f32[16,512]{1,0:T(8,128)S(1)} %get-tuple-element.38), channel_id=1, source_target_pairs={{0,1},{1,0},{2,3},{3,2},{4,5},{5,4},{6,7},{7,6},{8,9},{9,8},{10,11... | collective-permute-start | bytes 98312 | tf_op jit(solution)/shard_map/ppermute | solution.py:55
  15.8 1.2 %collective-permute-start.3 = (f32[16,512]{1,0:T(8,128)S(1)}, f32[16,512]{1,0:T(8,128)S(1)}, u32[]{:S(2)}, u32[]{:S(2)}) collective-permute-start(f32[16,512]{1,0:T(8,128)S(1)} %get-tuple-element.39), channel_id=1, source_target_pairs={{1,2},{2,1},{5,6},{6,5},{9,10},{10,9},{13,14},{14,13},{17,18},{18,... | collective-permute-start | bytes 98312 | tf_op jit(solution)/shard_map/ppermute | solution.py:55
  23.3 18.3 %collective-permute-start.4 = (bf16[2,64,512]{2,1,0:T(8,128)(2,1)S(1)}, bf16[2,64,512]{2,1,0:T(8,128)(2,1)S(1)}, u32[]{:S(2)}, u32[]{:S(2)}) collective-permute-start(bf16[2,64,512]{2,1,0:T(8,128)(2,1)S(1)} %get-tuple-element.48), channel_id=1, source_target_pairs={{0,4},{4,0},{8,12},{12,8},{16,20},{20,16},{24,28},{28,24},{1,5},{5... | collective-permute-start | bytes 393224 | tf_op jit(solution)/shard_map/ppermute | solution.py:55
  27.5 14.1 %collective-permute-start.5 = (bf16[2,64,512]{2,1,0:T(8,128)(2,1)S(1)}, bf16[2,64,512]{2,1,0:T(8,128)(2,1)S(1)}, u32[]{:S(2)}, u32[]{:S(2)}) collective-permute-start(bf16[2,64,512]{2,1,0:T(8,128)(2,1)S(1)} %get-tuple-element.49), channel_id=1, source_target_pairs={{4,8},{8,4},{12,16},{16,12},{20,24},{24,20},{5,9},{9,5},{13,17},{1... | collective-permute-start | bytes 393224 | tf_op jit(solution)/shard_map/ppermute | solution.py:55
  28.1 13.4 %collective-permute-start.6 = (f32[2,16,512]{2,1,0:T(8,128)S(1)}, f32[2,16,512]{2,1,0:T(8,128)S(1)}, u32[]{:S(2)}, u32[]{:S(2)}) collective-permute-start(f32[2,16,512]{2,1,0:T(8,128)S(1)} %get-tuple-element.50), channel_id=1, source_target_pairs={{0,1},{1,0},{2,3},{3,2},{4,5},{5,4},{6,7},{7,6},{8,9},{9,8},{10,11... | collective-permute-start | bytes 196616 | tf_op jit(solution)/shard_map/ppermute | solution.py:55
  31.2 8.0 %copy-start = (f32[16,64,512]{2,1,0:T(8,128)S(1)}, f32[16,64,512]{2,1,0:T(8,128)}, u32[]{:S(2)}) copy-start(f32[16,64,512]{2,1,0:T(8,128)} %p.1) | copy-start | bytes 6291460
  31.2 10.3 %collective-permute-start.7 = (f32[2,16,512]{2,1,0:T(8,128)S(1)}, f32[2,16,512]{2,1,0:T(8,128)S(1)}, u32[]{:S(2)}, u32[]{:S(2)}) collective-permute-start(f32[2,16,512]{2,1,0:T(8,128)S(1)} %get-tuple-element.51), channel_id=1, source_target_pairs={{1,2},{2,1},{5,6},{6,5},{9,10},{10,9},{13,14},{14,13},{17,18},{18,... | collective-permute-start | bytes 196616 | tf_op jit(solution)/shard_map/ppermute | solution.py:55
  42.3 11.4 %collective-permute-start.8 = (bf16[64,512]{1,0:T(8,128)(2,1)S(1)}, bf16[64,512]{1,0:T(8,128)(2,1)S(1)}, u32[]{:S(2)}, u32[]{:S(2)}) collective-permute-start(bf16[64,512]{1,0:T(8,128)(2,1)S(1)} %get-tuple-element.54), channel_id=1, source_target_pairs={{0,4},{4,0},{8,12},{12,8},{16,20},{20,16},{24,28},{28,24},{1,5},{5... | collective-permute-start | bytes 196616 | tf_op jit(solution)/shard_map/ppermute | solution.py:55
  47.8 6.0 %collective-permute-start.9 = (bf16[64,512]{1,0:T(8,128)(2,1)S(1)}, bf16[64,512]{1,0:T(8,128)(2,1)S(1)}, u32[]{:S(2)}, u32[]{:S(2)}) collective-permute-start(bf16[64,512]{1,0:T(8,128)(2,1)S(1)} %get-tuple-element.55), channel_id=1, source_target_pairs={{4,8},{8,4},{12,16},{16,12},{20,24},{24,20},{5,9},{9,5},{13,17},{1... | collective-permute-start | bytes 196616 | tf_op jit(solution)/shard_map/ppermute | solution.py:55
  48.4 5.3 %collective-permute-start.10 = (f32[16,512]{1,0:T(8,128)S(1)}, f32[16,512]{1,0:T(8,128)S(1)}, u32[]{:S(2)}, u32[]{:S(2)}) collective-permute-start(f32[16,512]{1,0:T(8,128)S(1)} %get-tuple-element.56), channel_id=1, source_target_pairs={{0,1},{1,0},{2,3},{3,2},{4,5},{5,4},{6,7},{7,6},{8,9},{9,8},{10,11... | collective-permute-start | bytes 98312 | tf_op jit(solution)/shard_map/ppermute | solution.py:55
  50.8 2.9 %collective-permute-start.11 = (f32[16,512]{1,0:T(8,128)S(1)}, f32[16,512]{1,0:T(8,128)S(1)}, u32[]{:S(2)}, u32[]{:S(2)}) collective-permute-start(f32[16,512]{1,0:T(8,128)S(1)} %get-tuple-element.57), channel_id=1, source_target_pairs={{1,2},{2,1},{5,6},{6,5},{9,10},{10,9},{13,14},{14,13},{17,18},{18,... | collective-permute-start | bytes 98312 | tf_op jit(solution)/shard_map/ppermute | solution.py:55
  54.1 9.8 %collective-permute-start.12 = (bf16[64,512]{1,0:T(8,128)(2,1)S(1)}, bf16[64,512]{1,0:T(8,128)(2,1)S(1)}, u32[]{:S(2)}, u32[]{:S(2)}) collective-permute-start(bf16[64,512]{1,0:T(8,128)(2,1)S(1)} %get-tuple-element.61), channel_id=1, source_target_pairs={{0,4},{4,0},{8,12},{12,8},{16,20},{20,16},{24,28},{28,24},{1,5},{5... | collective-permute-start | bytes 196616 | tf_op jit(solution)/shard_map/ppermute | solution.py:55
  58.3 5.7 %collective-permute-start.13 = (bf16[64,512]{1,0:T(8,128)(2,1)S(1)}, bf16[64,512]{1,0:T(8,128)(2,1)S(1)}, u32[]{:S(2)}, u32[]{:S(2)}) collective-permute-start(bf16[64,512]{1,0:T(8,128)(2,1)S(1)} %get-tuple-element.62), channel_id=1, source_target_pairs={{4,8},{8,4},{12,16},{16,12},{20,24},{24,20},{5,9},{9,5},{13,17},{1... | collective-permute-start | bytes 196616 | tf_op jit(solution)/shard_map/ppermute | solution.py:55
  59.0 5.0 %collective-permute-start.14 = (f32[16,512]{1,0:T(8,128)S(1)}, f32[16,512]{1,0:T(8,128)S(1)}, u32[]{:S(2)}, u32[]{:S(2)}) collective-permute-start(f32[16,512]{1,0:T(8,128)S(1)} %get-tuple-element.63), channel_id=1, source_target_pairs={{0,1},{1,0},{2,3},{3,2},{4,5},{5,4},{6,7},{7,6},{8,9},{9,8},{10,11... | collective-permute-start | bytes 98312 | tf_op jit(solution)/shard_map/ppermute | solution.py:55
  61.1 2.9 %collective-permute-start.15 = (f32[16,512]{1,0:T(8,128)S(1)}, f32[16,512]{1,0:T(8,128)S(1)}, u32[]{:S(2)}, u32[]{:S(2)}) collective-permute-start(f32[16,512]{1,0:T(8,128)S(1)} %get-tuple-element.64), channel_id=1, source_target_pairs={{1,2},{2,1},{5,6},{6,5},{9,10},{10,9},{13,14},{14,13},{17,18},{18,... | collective-permute-start | bytes 98312 | tf_op jit(solution)/shard_map/ppermute | solution.py:55

commit v2 on v1

--- a/solution.py
+++ b/solution.py
@@ -20,11 +20,11 @@
 DMA = pltpu.SemaphoreType.DMA
 
 
-def call(kernel, outs, *args, aliases=None, far_in=(), far_out=(), in_specs=None, scratch=(), limit=12 * MIB, name=None):
+def call(kernel, outs, *args, aliases=None, far_in=(), far_out=(), free_out=(), in_specs=None, scratch=(), limit=12 * MIB, name=None):
     specs = [FAR if n in far_in else WHOLE for n in range(len(args))]
     for n, spec in (in_specs or {}).items():
         specs[n] = spec
-    shapes = [o if n in far_out else pltpu.VMEM(o.shape, o.dtype) for n, o in enumerate(outs)]
+    shapes = [o if n in far_out or n in free_out else pltpu.VMEM(o.shape, o.dtype) for n, o in enumerate(outs)]
     return pl.pallas_call(
         kernel,
         out_shape=shapes,
@@ -46,13 +46,24 @@
 
 
 def swap(block, axis, odd):
-    count = lax.axis_size(axis)
+    slabs, depths = lax.axis_size("slab"), lax.axis_size("depth")
     pairs = []
-    for i in range(odd, count - 1, 2):
-        pairs += [(i, i + 1), (i + 1, i)]
-    if not pairs:
-        return jnp.zeros_like(block)
-    return lax.ppermute(block, axis, pairs)
+    for i in range(slabs):
+        for j in range(depths):
+            own, count, other = (i, slabs, depths) if axis == "slab" else (j, depths, slabs)
+            partner = own + 1 if own % 2 == odd else own - 1
+            target = (partner, j) if axis == "slab" else (i, partner)
+            if not 0 <= partner < count:
+                if other % 2:
+                    continue
+                target = (i, j ^ 1) if axis == "slab" else (i ^ 1, j)
+            pairs.append((i * depths + j, target[0] * depths + target[1]))
+    return lax.ppermute(block, ("slab", "depth"), pairs)
+
+
+def inner(axis):
+    i = lax.axis_index(axis)
+    return [jnp.where(i > 0, 1.0, 0.0), jnp.where(i < lax.axis_size(axis) - 1, 1.0, 0.0)]
 
 
 def row_is(rows, index):
@@ -99,8 +110,11 @@
         zo[x:x + 1, :] = jnp.where(ev_z, down, up)
 
 
-def route(capacity, rows, devices, dest, seg, rec, send, slot_out):
+def route(capacity, rows, devices, dest_h, seg_h, rec_h, send, slot_h, dest, seg, rec, slot_v, sems):
     panels = dest.shape[1]
+    dest_in, seg_in, rec_in = fetch([dest_h, seg_h, rec_h], [dest, seg, rec], sems)
+    dest_in.wait()
+    seg_in.wait()
     d = dest[...]
     s = seg[...]
     hot = lax.broadcasted_iota(jnp.int32, (devices, panels), 0) == d
@@ -112,8 +126,12 @@
         hot_f.astype(BF16), jnp.where(before_me, 1.0, 0.0).astype(BF16), preferred_element_type=F32
     )
     slot = jnp.sum(before * hot_f, axis=0, keepdims=True).astype(jnp.int32)
+    slot_v[...] = d * capacity + slot
+    slot_out = pltpu.make_async_copy(slot_v, slot_h, sems.at[3])
+    slot_out.start()
     place = d * rows + slot
     pick = lax.broadcasted_iota(jnp.int32, (devices * rows, panels), 0) == place
+    rec_in.wait()
     records = jnp.dot(jnp.where(pick, 1.0, 0.0).astype(BF16), rec[...], preferred_element_type=F32)
     high = (s // DIGIT).astype(F32)
     low = (s % DIGIT).astype(F32)
@@ -127,7 +145,7 @@
     records = records.reshape(devices, rows, LANES)
     is_digit = lax.broadcasted_iota(jnp.int32, records.shape, 1) >= capacity
     send[...] = jnp.where(is_digit, digits[:, None, :], records).astype(BF16)
-    slot_out[...] = d * capacity + slot
+    slot_out.wait()
 
 
 def parts_of(cells_x):
@@ -145,9 +163,9 @@
 
 
 def advect(
-    alpha_h, vx_h, vz_h, p_h, xe_in, xo_in, ze_in, zo_in,
+    alpha, vx, vz, p_h, xe_in, xo_in, ze_in, zo_in,
     out_h, xe, xo, ze, zo,
-    alpha, vx, vz, out, p0, p1, pz0, pz1, sems, p_sems,
+    out, p0, p1, pz0, pz1, sems, p_sems,
 ):
     cells_x, cells_z, beam = alpha.shape
     chunks = cells_z // SUB
@@ -156,30 +174,31 @@
     top = row_is((SUB, beam), 0)
     bottom = row_is((SUB, beam), SUB - 1)
     parts = parts_of(cells_x)
-    ins = [fetch_field(h, v, sems, n) for n, (h, v) in enumerate(((alpha_h, alpha), (vx_h, vx), (vz_h, vz)))]
     p_ins = fetch(x_planes(p_h) + z_tiles(p_h), [p0, p1, pz0, pz1], p_sems)
     outs = [
-        pltpu.make_async_copy(out.at[pl.ds(f, c)], out_h.at[pl.ds(f, c)], sems.at[len(ins), n])
+        pltpu.make_async_copy(out.at[pl.ds(f, c)], out_h.at[pl.ds(f, c)], sems.at[n])
         for n, (f, c) in enumerate(parts)
     ]
 
     def at(k):
         return pl.ds(k * SUB, SUB)
 
+    has_x, has_z = inner("slab"), inner("depth")
+
     def plane(x, first, last):
-        zlo = jnp.where(ev_z, zo_in[pl.ds(x, 1), :], ze_in[pl.ds(x, 1), :])
-        zhi = jnp.where(ev_z, ze_in[pl.ds(x, 1), :], zo_in[pl.ds(x, 1), :])
+        zlo = has_z[0] * jnp.where(ev_z, zo_in[pl.ds(x, 1), :], ze_in[pl.ds(x, 1), :])
+        zhi = has_z[1] * jnp.where(ev_z, ze_in[pl.ds(x, 1), :], zo_in[pl.ds(x, 1), :])
         above = None
         for k in reversed(range(chunks)):
             a = alpha[x, at(k), :]
             v = vx[x, at(k), :]
             if first:
-                am = jnp.where(ev_x, xo_in[at(k), :], xe_in[at(k), :]).astype(F32)
+                am = has_x[0] * jnp.where(ev_x, xo_in[at(k), :], xe_in[at(k), :]).astype(F32)
             else:
                 am = alpha[x - 1, at(k), :]
             fx = v * jnp.where(v > 0, am, a)
             if last:
-                q = jnp.where(ev_x, xe_in[at(k), :], xo_in[at(k), :]).astype(F32)
+                q = has_x[1] * jnp.where(ev_x, xe_in[at(k), :], xo_in[at(k), :]).astype(F32)
                 fxn = jnp.where(q > 0, q * a, q)
             else:
                 vn = vx[x + 1, at(k), :]
@@ -208,8 +227,6 @@
         zo[0, pl.ds(x, 1), :] = jnp.where(ev_z, z_down, z_up)
 
     for n, (first, count) in enumerate(parts):
-        for copies in ins:
-            copies[n].wait()
         begin = max(first - 1, 0)
         end = first + count - 1
         if begin == 0:
@@ -302,12 +319,8 @@
     del p_in, inverse_in
     cells_x, cells_z, beam = alpha.shape
     chunks = cells_z // SUB
-    i, j = lax.axis_index("slab"), lax.axis_index("depth")
     ev_x, ev_z = even("slab"), even("depth")
-    has = [
-        [jnp.where(i > 0, 1.0, 0.0), jnp.where(i < lax.axis_size("slab") - 1, 1.0, 0.0)],
-        [jnp.where(j > 0, 1.0, 0.0), jnp.where(j < lax.axis_size("depth") - 1, 1.0, 0.0)],
-    ]
+    has = [inner("slab"), inner("depth")]
 
     def at(k):
         return pl.ds(k * SUB, SUB)
@@ -319,8 +332,9 @@
             halo = has[0][side] * (9.0 * v[0] + 5.5)
             c = 2.0 / (1.0 + 9.0 * alpha[x, at(k), :] + halo)
             w = 1.0 / inverse[x, at(k), :]
-            p[x, at(k), :] = p[x, at(k), :] * w + c * v[1]
-            gx[side, at(k), :] = c
+            open_c = has[0][side] * c
+            p[x, at(k), :] = p[x, at(k), :] * w + open_c * v[1]
+            gx[side, at(k), :] = open_c
             wx[side, at(k), :] = w + c
 
     def rows(x, plane):
@@ -331,7 +345,8 @@
             v = jnp.where(ev_z, a, b) if side else jnp.where(ev_z, b, a)
             halo = jnp.broadcast_to(has[1][side] * (9.0 * v[0] + 5.5), (SUB, beam))
             c = jnp.where(here, 2.0 / (1.0 + 9.0 * alpha[x, at(k), :] + halo), 0.0)
-            add = c * jnp.broadcast_to(v[1], (SUB, beam))
+            open_c = has[1][side] * c
+            add = open_c * jnp.broadcast_to(v[1], (SUB, beam))
             if plane is None:
                 w = 1.0 / inverse[x, at(k), :]
                 total = p[x, at(k), :] * w + add
@@ -346,7 +361,7 @@
                 total = p[x, at(k), :] + add
                 p[x, at(k), :] = total
                 new = total * inv
-            g = inv * c
+            g = inv * open_c
             r = slice(0, 1) if side == 0 else slice(SUB - 1, SUB)
             gz[side, pl.ds(x, 1), :] = g[r, :]
             faces.append(new[r, :])
@@ -550,6 +565,14 @@
         functools.partial(route, capacity, rows, devices),
         [shape((devices, rows, LANES), BF16), shape((1, panels), jnp.int32)],
         panel_dest.reshape(1, panels), panel_segment.reshape(1, panels), panel_records,
+        far_in=(0, 1, 2), free_out=(0,), far_out=(1,),
+        scratch=[
+            near((1, panels), jnp.int32),
+            near((1, panels), jnp.int32),
+            near((panels, LANES), BF16),
+            near((1, panels), jnp.int32),
+            DMA((4,)),
+        ],
         name="route",
     )
     got = lax.all_to_all(send, axes, split_axis=0, concat_axis=0, tiled=True)
@@ -562,8 +585,8 @@
     )
     alpha_next, *packed = call(
         advect, [field] + two_faces, alpha, vel_x, vel_z, press_guess, *swaps(*packed),
-        far_in=(0, 1, 2, 3), far_out=(0,),
-        scratch=[near(alpha.shape)] * 4 + [near(xs), near(xs), near(tile), near(tile), DMA((4, parts)), DMA((4,))],
+        far_in=(3,), far_out=(0,),
+        scratch=[near(alpha.shape), near(xs), near(xs), near(tile), near(tile), DMA((parts,)), DMA((4,))],
         name="advect",
     )
     halo = swaps(*packed)

time: 83.9 us -> 66.7 us (0.79)
  starting transfers between devices: 36 us -> 24.2 us
  blocking collectives: 15 us -> 11.2 us
  local copies, waits for them, and re-layouts: 2.78 us -> 0.61 us
    ppermute x16, starting transfers between devices: 28.7 us -> 16.9 us  [swap(): return lax.ppermute(block, ('slab', 'depth'), pairs)]
    all_to_all x1, blocking collectives: 15 us -> 11.2 us  [body(): lax.all_to_all(back, axes, split_axis=0, concat_axis=0, tiled=True)]
    unnamed x10, local copies, waits for them, and re-layouts: 2.78 us -> 0.61 us
  transfers between devices with their start and end apart: 17 -> 17, of which waited for: 2 -> 2; matrix products, arithmetic and copies ran while one was open for 0% -> 0% of each run, Pallas kernels for 24% -> 29%
where the time goes in v2:
time: 66.7 us; the launch traced here: 66.1 us
  Pallas kernels  26.9 us (40%)
  starting transfers between devices  24.2 us (36%)
  blocking collectives  11.2 us (17%)
  waiting for transfers between devices  2.39 us (4%)
  between operations  0.88 us (1%)
    pallas_call x11, Pallas kernels, call(): pl.pallas_call(kernel, out_shape=shapes, in_specs=specs, out_specs=[FAR i...  25 us
    ppermute x16, starting transfers between devices, swap(): return lax.ppermute(block, ('slab', 'depth'), pairs)  16.9 us
    all_to_all x1, blocking collectives, body(): lax.all_to_all(back, axes, split_axis=0, concat_axis=0, tiled=True)  11.2 us
    all_to_all x1, starting transfers between devices, body(): got = lax.all_to_all(send, axes, split_axis=0, concat_axis=0, tiled=True)  7.33 us
    ppermute x16, waiting for transfers between devices, swap(): return lax.ppermute(block, ('slab', 'depth'), pairs)  2.39 us
    pallas_call x1, Pallas kernels, body(): pl.pallas_call(unroute, out_shape=shape((panels, LANES), BF16), in_specs=...  1.82 us
  transfers between devices with their start and end apart: 17, of which 2 were waited for; matrix products, arithmetic and copies ran while one was open for 0% of the time, Pallas kernels for 29%

profile of v2, /device:TPU:0, one launch (start us, length us, event | category | flops | bytes accessed | tf_op | source)
XLA Modules:
  0.0 66.1 jit_solution(9464985349061087641)
XLA Ops:
  0.6 2.0 %route.1 = (bf16[32,24,128]{2,1,0:T(8,128)(2,1)}, s32[1,256]{1,0:T(1,128)S(1)}) custom-call(s32[1,256]{1,0:T(1,128)} %bitcast.2, s32[1,256]{1,0:T(1,128)} %bitcast.3, bf16[256,128]{1,0:T(8,128)(2,1)} %rec_h.1), custom_call_target="tpu_custom_call" | custom-call | tf_op jit(solution)/shard_map/route/pallas_call | solution.py:28
  2.6 0.6 copy-done.4
  3.2 7.3 %all-to-all-start = ((bf16[32,24,128]{2,1,0:T(8,128)(2,1)}), bf16[32,24,128]{2,1,0:T(8,128)(2,1)S(1)}, u32[]{:S(2)}, u32[]{:S(2)}) async-start(bf16[32,24,128]{2,1,0:T(8,128)(2,1)} %get-tuple-element.41), calls=%async_computation | async-start | bytes 393216 | tf_op jit(solution)/shard_map/all_to_all | solution.py:578
  10.6 0.0 copy-start.1
  10.6 0.0 copy-start.2
  10.6 1.5 %pack_first.1 = (bf16[64,512]{1,0:T(8,128)(2,1)S(1)}, bf16[64,512]{1,0:T(8,128)(2,1)S(1)}, f32[16,512]{1,0:T(8,128)S(1)}, f32[16,512]{1,0:T(8,128)S(1)}) custom-call(f32[16,64,512]{2,1,0:T(8,128)} %alpha.3, f32[16,64,512]{2,1,0:T(8,128)} %vx.3, f32[16,64,512]{2,1,0:T(8,128)} %vz.3), custom_call_target="tpu_custom_call" | custom-call | tf_op jit(solution)/shard_map/pack_first/pallas_call | solution.py:28
  12.1 1.8 %collective-permute-start = (bf16[64,512]{1,0:T(8,128)(2,1)S(1)}, bf16[64,512]{1,0:T(8,128)(2,1)S(1)}, u32[]{:S(2)}, u32[]{:S(2)}) collective-permute-start(bf16[64,512]{1,0:T(8,128)(2,1)S(1)} %get-tuple-element.36), channel_id=1, source_target_pairs={{0,4},{1,5},{2,6},{3,7},{4,0},{5,1},{6,2},{7,3},{8,12},{9,13},{10,... | collective-permute-start | bytes 196616 | tf_op jit(solution)/shard_map/ppermute | solution.py:61
  14.0 0.5 collective-permute-start.2
  14.5 2.4 %collective-permute-start.3 = (f32[16,512]{1,0:T(8,128)S(1)}, f32[16,512]{1,0:T(8,128)S(1)}, u32[]{:S(2)}, u32[]{:S(2)}) collective-permute-start(f32[16,512]{1,0:T(8,128)S(1)} %get-tuple-element.39), channel_id=1, source_target_pairs={{0,4},{1,2},{2,1},{3,7},{4,0},{5,6},{6,5},{7,3},{8,12},{9,10},{10,... | collective-permute-start | bytes 98312 | tf_op jit(solution)/shard_map/ppermute | solution.py:61
  16.9 2.1 %collective-permute-done.3.zo_in = f32[16,512]{1,0:T(8,128)S(1)} collective-permute-done((f32[16,512]{1,0:T(8,128)S(1)}, f32[16,512]{1,0:T(8,128)S(1)}, u32[]{:S(2)}, u32[]{:S(2)}) %collective-permute-start.3) | collective-permute-done | bytes 32800 | tf_op jit(solution)/shard_map/ppermute | solution.py:61
  19.0 2.6 %advect.1 = (f32[16,64,512]{2,1,0:T(8,128)}, bf16[2,64,512]{2,1,0:T(8,128)(2,1)S(1)}, bf16[2,64,512]{2,1,0:T(8,128)(2,1)S(1)}, f32[2,16,512]{2,1,0:T(8,128)S(1)}, f32[2,16,512]{2,1,0:T(8,128)S(1)}) custom-call(f32[16,64,512]{2,1,0:T(8,128)S(1)} %copy-done, f32[16,64,512]{2,1,0:T(8,128)S(1)} %copy-done.1, f32[16,64,512]{2,1,0:T(8,128)S(1)} %copy-done.2, ...), custom_call_target="tpu_custom_call" | custom-call | tf_op jit(solution)/shard_map/advect/pallas_call | solution.py:28
  21.6 1.9 %collective-permute-start.4 = (bf16[2,64,512]{2,1,0:T(8,128)(2,1)S(1)}, bf16[2,64,512]{2,1,0:T(8,128)(2,1)S(1)}, u32[]{:S(2)}, u32[]{:S(2)}) collective-permute-start(bf16[2,64,512]{2,1,0:T(8,128)(2,1)S(1)} %get-tuple-element.48), channel_id=1, source_target_pairs={{0,4},{1,5},{2,6},{3,7},{4,0},{5,1},{6,2},{7,3},{8,12},{9,13},{10,... | collective-permute-start | bytes 393224 | tf_op jit(solution)/shard_map/ppermute | solution.py:61
  23.5 0.5 collective-permute-start.6
  24.0 2.4 %collective-permute-start.7 = (f32[2,16,512]{2,1,0:T(8,128)S(1)}, f32[2,16,512]{2,1,0:T(8,128)S(1)}, u32[]{:S(2)}, u32[]{:S(2)}) collective-permute-start(f32[2,16,512]{2,1,0:T(8,128)S(1)} %get-tuple-element.51), channel_id=1, source_target_pairs={{0,4},{1,2},{2,1},{3,7},{4,0},{5,6},{6,5},{7,3},{8,12},{9,10},{10,... | collective-permute-start | bytes 196616 | tf_op jit(solution)/shard_map/ppermute | solution.py:61
  26.4 4.1 %scatter.1 = (f32[16,64,512]{2,1,0:T(8,128)S(1)}, s32[32,128]{1,0:T(8,128)S(1)}) custom-call(bf16[32,24,128]{2,1,0:T(8,128)(2,1)S(1)} %all-to-all-done.after.got, f32[16,64,512]{2,1,0:T(8,128)} %div_h.1), custom_call_target="tpu_custom_call" | custom-call | tf_op jit(solution)/shard_map/scatter/pallas_call | solution.py:28
  30.5 4.6 %coefficients.1 = (f32[16,64,512]{2,1,0:T(8,128)S(1)}, f32[17,64,512]{2,1,0:T(8,128)S(1)}, f32[16,64,512]{2,1,0:T(8,128)S(1)}, f32[16,64,512]{2,1,0:T(8,128)S(1)}, f32[16,64,512]{2,1,0:T(8,128)S(1)}) custom-call(f32[16,64,512]{2,1,0:T(8,128)} %get-tuple-element.34.alpha_h, bf16[32,24,128]{2,1,0:T(8,128)(2,1)S(1)} %all-to-all-done.after.got), custom_call_target="tpu_custom_call" | custom-call | tf_op jit(solution)/shard_map/coefficients/pallas_call | solution.py:28
  35.1 2.2 %sweep.3.p_in = f32[16,64,512]{2,1,0:T(8,128)S(1)} custom-call(f32[16,64,512]{2,1,0:T(8,128)S(1)} %copy-done.3, f32[17,64,512]{2,1,0:T(8,128)S(1)} %get-tuple-element.42.cx, f32[16,64,512]{2,1,0:T(8,128)S(1)} %get-tuple-element.43.cz, f32[16,64,512]{2,1,0:T(8,128)S(1)} %get-tuple-element.44.cy, f32[16,64,512]{2,1,0:T(8,128)S(1)} %get-tuple-element.45.inverse.inverse_in, ...), custom_call_target="tpu_custom_call" | custom-call | tf_op jit(solution)/shard_map/sweep/pallas_call | solution.py:28
  37.4 0.8 %close.1 = (f32[16,64,512]{2,1,0:T(8,128)S(1)}, f32[16,64,512]{2,1,0:T(8,128)S(1)}, f32[2,64,512]{2,1,0:T(8,128)S(1)}, f32[2,16,512]{2,1,0:T(8,128)S(1)}, bf16[6...) custom-call(f32[16,64,512]{2,1,0:T(8,128)S(1)} %sweep.3.p_in, ...), custom_call_target="tpu_custom_call", output_to_operand_aliasing={{0}: (0, {}), {1}: (1, {})} | custom-call | tf_op jit(solution)/shard_map/close/pallas_call | solution.py:28
  38.2 0.1 collective-permute-start.8
  38.2 0.1 collective-permute-start.9
  38.3 0.5 collective-permute-start.10
  38.8 2.8 %collective-permute-start.11 = (f32[16,512]{1,0:T(8,128)S(1)}, f32[16,512]{1,0:T(8,128)S(1)}, u32[]{:S(2)}, u32[]{:S(2)}) collective-permute-start(f32[16,512]{1,0:T(8,128)S(1)} %get-tuple-element.57), channel_id=1, source_target_pairs={{0,4},{1,2},{2,1},{3,7},{4,0},{5,6},{6,5},{7,3},{8,12},{9,10},{10,... | collective-permute-start | bytes 98312 | tf_op jit(solution)/shard_map/ppermute | solution.py:61
  41.7 2.2 %sweep.4.p_in = f32[16,64,512]{2,1,0:T(8,128)S(1)} custom-call(f32[16,64,512]{2,1,0:T(8,128)S(1)} %get-tuple-element.52.p, f32[17,64,512]{2,1,0:T(8,128)S(1)} %get-tuple-element.42.cx, f32[16,64,512]{2,1,0:T(8,128)S(1)} %get-tuple-element.43.cz, f32[16,64,512]{2,1,0:T(8,128)S(1)} %get-tuple-element.44.cy, f32[16,64,512]{2,1,0:T(8,128)S(1)} %get-tuple-element.53.inverse, ...), custom_call_target="tpu_custom_call" | custom-call | tf_op jit(solution)/shard_map/sweep/pallas_call | solution.py:28
  43.9 0.4 fix.1
  44.3 1.9 %collective-permute-start.12 = (bf16[64,512]{1,0:T(8,128)(2,1)S(1)}, bf16[64,512]{1,0:T(8,128)(2,1)S(1)}, u32[]{:S(2)}, u32[]{:S(2)}) collective-permute-start(bf16[64,512]{1,0:T(8,128)(2,1)S(1)} %get-tuple-element.61), channel_id=1, source_target_pairs={{0,4},{1,5},{2,6},{3,7},{4,0},{5,1},{6,2},{7,3},{8,12},{9,13},{10,... | collective-permute-start | bytes 196616 | tf_op jit(solution)/shard_map/ppermute | solution.py:61
  46.2 0.5 collective-permute-start.14
  46.7 1.4 %collective-permute-start.15 = (f32[16,512]{1,0:T(8,128)S(1)}, f32[16,512]{1,0:T(8,128)S(1)}, u32[]{:S(2)}, u32[]{:S(2)}) collective-permute-start(f32[16,512]{1,0:T(8,128)S(1)} %get-tuple-element.64), channel_id=1, source_target_pairs={{0,4},{1,2},{2,1},{3,7},{4,0},{5,6},{6,5},{7,3},{8,12},{9,10},{10,... | collective-permute-start | bytes 98312 | tf_op jit(solution)/shard_map/ppermute | solution.py:61
  48.1 2.2 %sweep.5.p_in = f32[16,64,512]{2,1,0:T(8,128)S(1)} custom-call(f32[16,64,512]{2,1,0:T(8,128)S(1)} %get-tuple-element.60.p, f32[17,64,512]{2,1,0:T(8,128)S(1)} %get-tuple-element.42.cx, f32[16,64,512]{2,1,0:T(8,128)S(1)} %get-tuple-element.43.cz, f32[16,64,512]{2,1,0:T(8,128)S(1)} %get-tuple-element.44.cy, f32[16,64,512]{2,1,0:T(8,128)S(1)} %get-tuple-element.53.inverse, ...), custom_call_target="tpu_custom_call" | custom-call | tf_op jit(solution)/shard_map/sweep/pallas_call | solution.py:28
  50.3 0.3 collective-permute-done.15.zo_in
  50.6 2.5 %gather.1 = (f32[16,64,512]{2,1,0:T(8,128)}, bf16[32,16,128]{2,1,0:T(8,128)(2,1)S(1)}) custom-call(f32[16,64,512]{2,1,0:T(8,128)S(1)} %sweep.5.p_in, bf16[64,512]{1,0:T(8,128)(2,1)S(1)} %collective-permute-done.12.xe_in, bf16[64,512]{1,0:T(8,128)(2,1)S(1)} %collective-permute-done.13.xo_in, f32[16,512]{1,0:T(8,128)S(1)} %collective-permute-done.14.ze_in, ...), custom_call_target="tpu_custom_call" | custom-call | tf_op jit(solution)/shard_map/gather/pallas_call | solution.py:28
  53.1 11.2 %all_to_all.10.back = bf16[32,16,128]{2,1,0:T(8,128)(2,1)} all-to-all(bf16[32,16,128]{2,1,0:T(8,128)(2,1)S(1)} %get-tuple-element.67), channel_id=1, replica_groups=mesh['slab'=8,'depth'=4] {'slab','depth'}, dimensions={0} | all-to-all | bytes 262144 | tf_op jit(solution)/shard_map/all_to_all | solution.py:643
  64.3 1.8 %unroute.1 = bf16[256,128]{1,0:T(8,128)(2,1)} custom-call(bf16[32,16,128]{2,1,0:T(8,128)(2,1)} %all_to_all.10.back, s32[1,256]{1,0:T(1,128)} %copy-done.4), custom_call_target="tpu_custom_call" | custom-call | tf_op jit(solution)/shard_map/unroute/pallas_call | solution.py:644
  (25 shorter events, 0.1 us)
Async XLA Ops:
  2.6 0.6 copy-start.4
  3.2 23.2 %all-to-all-start = ((bf16[32,24,128]{2,1,0:T(8,128)(2,1)}), bf16[32,24,128]{2,1,0:T(8,128)(2,1)S(1)}, u32[]{:S(2)}, u32[]{:S(2)}) async-start(bf16[32,24,128]{2,1,0:T(8,128)(2,1)} %get-tuple-element.41), calls=%async_computation | async-start | bytes 393216 | tf_op jit(solution)/shard_map/all_to_all | solution.py:578
  10.5 8.4 %copy-start = (f32[16,64,512]{2,1,0:T(8,128)S(1)}, f32[16,64,512]{2,1,0:T(8,128)}, u32[]{:S(2)}) copy-start(f32[16,64,512]{2,1,0:T(8,128)} %alpha.3) | copy-start | bytes 6291460
  10.6 8.4 %copy-start.1 = (f32[16,64,512]{2,1,0:T(8,128)S(1)}, f32[16,64,512]{2,1,0:T(8,128)}, u32[]{:S(2)}) copy-start(f32[16,64,512]{2,1,0:T(8,128)} %vx.3) | copy-start | bytes 6291460
  10.6 8.4 %copy-start.2 = (f32[16,64,512]{2,1,0:T(8,128)S(1)}, f32[16,64,512]{2,1,0:T(8,128)}, u32[]{:S(2)}) copy-start(f32[16,64,512]{2,1,0:T(8,128)} %vz.3) | copy-start | bytes 6291460
  12.1 6.8 %collective-permute-start = (bf16[64,512]{1,0:T(8,128)(2,1)S(1)}, bf16[64,512]{1,0:T(8,128)(2,1)S(1)}, u32[]{:S(2)}, u32[]{:S(2)}) collective-permute-start(bf16[64,512]{1,0:T(8,128)(2,1)S(1)} %get-tuple-element.36), channel_id=1, source_target_pairs={{0,4},{1,5},{2,6},{3,7},{4,0},{5,1},{6,2},{7,3},{8,12},{9,13},{10,... | collective-permute-start | bytes 196616 | tf_op jit(solution)/shard_map/ppermute | solution.py:61
  14.0 5.0 %collective-permute-start.1 = (bf16[64,512]{1,0:T(8,128)(2,1)S(1)}, bf16[64,512]{1,0:T(8,128)(2,1)S(1)}, u32[]{:S(2)}, u32[]{:S(2)}) collective-permute-start(bf16[64,512]{1,0:T(8,128)(2,1)S(1)} %get-tuple-element.37), channel_id=1, source_target_pairs={{0,1},{1,0},{2,3},{3,2},{4,8},{5,9},{6,10},{7,11},{8,4},{9,5},{10,... | collective-permute-start | bytes 196616 | tf_op jit(solution)/shard_map/ppermute | solution.py:61
  14.0 2.9 %collective-permute-start.2 = (f32[16,512]{1,0:T(8,128)S(1)}, f32[16,512]{1,0:T(8,128)S(1)}, u32[]{:S(2)}, u32[]{:S(2)}) collective-permute-start(f32[16,512]{1,0:T(8,128)S(1)} %get-tuple-element.38), channel_id=1, source_target_pairs={{0,1},{1,0},{2,3},{3,2},{4,5},{5,4},{6,7},{7,6},{8,9},{9,8},{10,11... | collective-permute-start | bytes 98312 | tf_op jit(solution)/shard_map/ppermute | solution.py:61
  14.5 4.5 %collective-permute-start.3 = (f32[16,512]{1,0:T(8,128)S(1)}, f32[16,512]{1,0:T(8,128)S(1)}, u32[]{:S(2)}, u32[]{:S(2)}) collective-permute-start(f32[16,512]{1,0:T(8,128)S(1)} %get-tuple-element.39), channel_id=1, source_target_pairs={{0,4},{1,2},{2,1},{3,7},{4,0},{5,6},{6,5},{7,3},{8,12},{9,10},{10,... | collective-permute-start | bytes 98312 | tf_op jit(solution)/shard_map/ppermute | solution.py:61
  21.6 15.8 %collective-permute-start.4 = (bf16[2,64,512]{2,1,0:T(8,128)(2,1)S(1)}, bf16[2,64,512]{2,1,0:T(8,128)(2,1)S(1)}, u32[]{:S(2)}, u32[]{:S(2)}) collective-permute-start(bf16[2,64,512]{2,1,0:T(8,128)(2,1)S(1)} %get-tuple-element.48), channel_id=1, source_target_pairs={{0,4},{1,5},{2,6},{3,7},{4,0},{5,1},{6,2},{7,3},{8,12},{9,13},{10,... | collective-permute-start | bytes 393224 | tf_op jit(solution)/shard_map/ppermute | solution.py:61
  23.5 13.9 %collective-permute-start.5 = (bf16[2,64,512]{2,1,0:T(8,128)(2,1)S(1)}, bf16[2,64,512]{2,1,0:T(8,128)(2,1)S(1)}, u32[]{:S(2)}, u32[]{:S(2)}) collective-permute-start(bf16[2,64,512]{2,1,0:T(8,128)(2,1)S(1)} %get-tuple-element.49), channel_id=1, source_target_pairs={{0,1},{1,0},{2,3},{3,2},{4,8},{5,9},{6,10},{7,11},{8,4},{9,5},{10,... | collective-permute-start | bytes 393224 | tf_op jit(solution)/shard_map/ppermute | solution.py:61
  23.5 13.8 %collective-permute-start.6 = (f32[2,16,512]{2,1,0:T(8,128)S(1)}, f32[2,16,512]{2,1,0:T(8,128)S(1)}, u32[]{:S(2)}, u32[]{:S(2)}) collective-permute-start(f32[2,16,512]{2,1,0:T(8,128)S(1)} %get-tuple-element.50), channel_id=1, source_target_pairs={{0,1},{1,0},{2,3},{3,2},{4,5},{5,4},{6,7},{7,6},{8,9},{9,8},{10,11... | collective-permute-start | bytes 196616 | tf_op jit(solution)/shard_map/ppermute | solution.py:61
  24.0 11.1 %copy-start.3 = (f32[16,64,512]{2,1,0:T(8,128)S(1)}, f32[16,64,512]{2,1,0:T(8,128)}, u32[]{:S(2)}) copy-start(f32[16,64,512]{2,1,0:T(8,128)} %p.1) | copy-start | bytes 6291460
  24.0 13.3 %collective-permute-start.7 = (f32[2,16,512]{2,1,0:T(8,128)S(1)}, f32[2,16,512]{2,1,0:T(8,128)S(1)}, u32[]{:S(2)}, u32[]{:S(2)}) collective-permute-start(f32[2,16,512]{2,1,0:T(8,128)S(1)} %get-tuple-element.51), channel_id=1, source_target_pairs={{0,4},{1,2},{2,1},{3,7},{4,0},{5,6},{6,5},{7,3},{8,12},{9,10},{10,... | collective-permute-start | bytes 196616 | tf_op jit(solution)/shard_map/ppermute | solution.py:61
  38.2 5.8 %collective-permute-start.8 = (bf16[64,512]{1,0:T(8,128)(2,1)S(1)}, bf16[64,512]{1,0:T(8,128)(2,1)S(1)}, u32[]{:S(2)}, u32[]{:S(2)}) collective-permute-start(bf16[64,512]{1,0:T(8,128)(2,1)S(1)} %get-tuple-element.54), channel_id=1, source_target_pairs={{0,4},{1,5},{2,6},{3,7},{4,0},{5,1},{6,2},{7,3},{8,12},{9,13},{10,... | collective-permute-start | bytes 196616 | tf_op jit(solution)/shard_map/ppermute | solution.py:61
  38.2 5.7 %collective-permute-start.9 = (bf16[64,512]{1,0:T(8,128)(2,1)S(1)}, bf16[64,512]{1,0:T(8,128)(2,1)S(1)}, u32[]{:S(2)}, u32[]{:S(2)}) collective-permute-start(bf16[64,512]{1,0:T(8,128)(2,1)S(1)} %get-tuple-element.55), channel_id=1, source_target_pairs={{0,1},{1,0},{2,3},{3,2},{4,8},{5,9},{6,10},{7,11},{8,4},{9,5},{10,... | collective-permute-start | bytes 196616 | tf_op jit(solution)/shard_map/ppermute | solution.py:61
  38.3 5.6 %collective-permute-start.10 = (f32[16,512]{1,0:T(8,128)S(1)}, f32[16,512]{1,0:T(8,128)S(1)}, u32[]{:S(2)}, u32[]{:S(2)}) collective-permute-start(f32[16,512]{1,0:T(8,128)S(1)} %get-tuple-element.56), channel_id=1, source_target_pairs={{0,1},{1,0},{2,3},{3,2},{4,5},{5,4},{6,7},{7,6},{8,9},{9,8},{10,11... | collective-permute-start | bytes 98312 | tf_op jit(solution)/shard_map/ppermute | solution.py:61
  38.8 5.1 %collective-permute-start.11 = (f32[16,512]{1,0:T(8,128)S(1)}, f32[16,512]{1,0:T(8,128)S(1)}, u32[]{:S(2)}, u32[]{:S(2)}) collective-permute-start(f32[16,512]{1,0:T(8,128)S(1)} %get-tuple-element.57), channel_id=1, source_target_pairs={{0,4},{1,2},{2,1},{3,7},{4,0},{5,6},{6,5},{7,3},{8,12},{9,10},{10,... | collective-permute-start | bytes 98312 | tf_op jit(solution)/shard_map/ppermute | solution.py:61
  44.3 6.3 %collective-permute-start.12 = (bf16[64,512]{1,0:T(8,128)(2,1)S(1)}, bf16[64,512]{1,0:T(8,128)(2,1)S(1)}, u32[]{:S(2)}, u32[]{:S(2)}) collective-permute-start(bf16[64,512]{1,0:T(8,128)(2,1)S(1)} %get-tuple-element.61), channel_id=1, source_target_pairs={{0,4},{1,5},{2,6},{3,7},{4,0},{5,1},{6,2},{7,3},{8,12},{9,13},{10,... | collective-permute-start | bytes 196616 | tf_op jit(solution)/shard_map/ppermute | solution.py:61
  46.2 4.4 %collective-permute-start.13 = (bf16[64,512]{1,0:T(8,128)(2,1)S(1)}, bf16[64,512]{1,0:T(8,128)(2,1)S(1)}, u32[]{:S(2)}, u32[]{:S(2)}) collective-permute-start(bf16[64,512]{1,0:T(8,128)(2,1)S(1)} %get-tuple-element.62), channel_id=1, source_target_pairs={{0,1},{1,0},{2,3},{3,2},{4,8},{5,9},{6,10},{7,11},{8,4},{9,5},{10,... | collective-permute-start | bytes 196616 | tf_op jit(solution)/shard_map/ppermute | solution.py:61
  46.2 4.1 %collective-permute-start.14 = (f32[16,512]{1,0:T(8,128)S(1)}, f32[16,512]{1,0:T(8,128)S(1)}, u32[]{:S(2)}, u32[]{:S(2)}) collective-permute-start(f32[16,512]{1,0:T(8,128)S(1)} %get-tuple-element.63), channel_id=1, source_target_pairs={{0,1},{1,0},{2,3},{3,2},{4,5},{5,4},{6,7},{7,6},{8,9},{9,8},{10,11... | collective-permute-start | bytes 98312 | tf_op jit(solution)/shard_map/ppermute | solution.py:61
  46.7 3.9 %collective-permute-start.15 = (f32[16,512]{1,0:T(8,128)S(1)}, f32[16,512]{1,0:T(8,128)S(1)}, u32[]{:S(2)}, u32[]{:S(2)}) collective-permute-start(f32[16,512]{1,0:T(8,128)S(1)} %get-tuple-element.64), channel_id=1, source_target_pairs={{0,4},{1,2},{2,1},{3,7},{4,0},{5,6},{6,5},{7,3},{8,12},{9,10},{10,... | collective-permute-start | bytes 98312 | tf_op jit(solution)/shard_map/ppermute | solution.py:61

commit v3 on v2

--- a/solution.py
+++ b/solution.py
@@ -6,6 +6,7 @@
 from jax.experimental import pallas as pl
 from jax.experimental.pallas import tpu as pltpu
 from jax.sharding import PartitionSpec as P
+
 
 COURANT = 0.2
 LANES = 128
@@ -20,7 +21,7 @@
 DMA = pltpu.SemaphoreType.DMA
 
 
-def call(kernel, outs, *args, aliases=None, far_in=(), far_out=(), free_out=(), in_specs=None, scratch=(), limit=12 * MIB, name=None):
+def call(kernel, outs, *args, aliases=None, far_in=(), far_out=(), free_out=(), in_specs=None, scratch=(), limit=12 * MIB):
     specs = [FAR if n in far_in else WHOLE for n in range(len(args))]
     for n, spec in (in_specs or {}).items():
         specs[n] = spec
@@ -33,7 +34,6 @@
         scratch_shapes=list(scratch),
         input_output_aliases=aliases or {},
         compiler_params=pltpu.CompilerParams(vmem_limit_bytes=limit),
-        name=name,
     )(*(pltpu.with_memory_space_constraint(a, pltpu.HBM) if n in far_in else a for n, a in enumerate(args)))
 
 
@@ -66,6 +66,11 @@
     return [jnp.where(i > 0, 1.0, 0.0), jnp.where(i < lax.axis_size(axis) - 1, 1.0, 0.0)]
 
 
+def unrolled(begin, end, most=4):
+    count = end - begin
+    return pl.loop(begin, end, unroll=next(n for n in range(most, 0, -1) if count % n == 0))
+
+
 def row_is(rows, index):
     return lax.broadcasted_iota(jnp.int32, rows, 0) == index
 
@@ -87,10 +92,7 @@
     return copies
 
 
-def pack_first(alpha, vx, vz, xe, xo, ze, zo, a0, a1, az0, az1, vx0, vz0, sems):
-    sources = x_planes(alpha) + z_tiles(alpha) + x_planes(vx)[:1] + z_tiles(vz)[:1]
-    for copy in fetch(sources, [a0, a1, az0, az1, vx0, vz0], sems):
-        copy.wait()
+def pack_first(a0, a1, az0, az1, vx0, vz0, xe, xo, ze, zo):
     ev_x = even("slab")
     ev_z = even("depth")
 
@@ -110,11 +112,18 @@
         zo[x:x + 1, :] = jnp.where(ev_z, down, up)
 
 
-def route(capacity, rows, devices, dest_h, seg_h, rec_h, send, slot_h, dest, seg, rec, slot_v, sems):
+def enter(
+    capacity, rows, devices,
+    alpha, vx, vz, dest_h, seg_h, rec_h,
+    xe, xo, ze, zo, send_h, slot_h,
+    a0, a1, az0, az1, vx0, vz0, dest, seg, rec, slot_v, send, sems,
+):
+    sources = x_planes(alpha) + z_tiles(alpha) + x_planes(vx)[:1] + z_tiles(vz)[:1]
+    borders = [a0, a1, az0, az1, vx0, vz0]
+    copies = fetch([dest_h, seg_h, rec_h] + sources, [dest, seg, rec] + borders, sems)
     panels = dest.shape[1]
-    dest_in, seg_in, rec_in = fetch([dest_h, seg_h, rec_h], [dest, seg, rec], sems)
-    dest_in.wait()
-    seg_in.wait()
+    copies[0].wait()
+    copies[1].wait()
     d = dest[...]
     s = seg[...]
     hot = lax.broadcasted_iota(jnp.int32, (devices, panels), 0) == d
@@ -127,13 +136,13 @@
     )
     slot = jnp.sum(before * hot_f, axis=0, keepdims=True).astype(jnp.int32)
     slot_v[...] = d * capacity + slot
-    slot_out = pltpu.make_async_copy(slot_v, slot_h, sems.at[3])
+    slot_out = pltpu.make_async_copy(slot_v, slot_h, sems.at[9])
     slot_out.start()
     place = d * rows + slot
     pick = lax.broadcasted_iota(jnp.int32, (devices * rows, panels), 0) == place
-    rec_in.wait()
+    copies[2].wait()
     records = jnp.dot(jnp.where(pick, 1.0, 0.0).astype(BF16), rec[...], preferred_element_type=F32)
-    high = (s // DIGIT).astype(F32)
+    high = (s // DIGIT + 1).astype(F32)
     low = (s % DIGIT).astype(F32)
     lane = lax.broadcasted_iota(jnp.int32, (LANES, panels), 0)
     at_high = jnp.where(lane == slot, 1.0, 0.0).astype(BF16)
@@ -145,27 +154,35 @@
     records = records.reshape(devices, rows, LANES)
     is_digit = lax.broadcasted_iota(jnp.int32, records.shape, 1) >= capacity
     send[...] = jnp.where(is_digit, digits[:, None, :], records).astype(BF16)
+    send_out = pltpu.make_async_copy(send, send_h, sems.at[10])
+    send_out.start()
+    for copy in copies[3:]:
+        copy.wait()
+    pack_first(*borders, xe, xo, ze, zo)
     slot_out.wait()
+    send_out.wait()
 
 
 def parts_of(cells_x):
-    step = max(1, cells_x // 4)
+    step = max(1, cells_x // 8)
     return [(first, min(step, cells_x - first)) for first in range(0, cells_x, step)]
 
 
-def fetch_field(source, target, sems, row):
-    copies = []
-    for n, (first, count) in enumerate(parts_of(target.shape[0])):
+def fetch_fields(fields, sems):
+    copies = [[] for _ in fields]
+    for n, (first, count) in enumerate(parts_of(fields[0][1].shape[0])):
         planes = pl.ds(first, count)
-        copies.append(pltpu.make_async_copy(source.at[planes], target.at[planes], sems.at[row, n]))
-        copies[-1].start()
+        for row, (source, target) in enumerate(fields):
+            copy = pltpu.make_async_copy(source.at[planes], target.at[planes], sems.at[row, n])
+            copy.start()
+            copies[row].append(copy)
     return copies
 
 
 def advect(
-    alpha, vx, vz, p_h, xe_in, xo_in, ze_in, zo_in,
+    alpha_h, vx_h, vz_h, p_h, xe_in, xo_in, ze_in, zo_in,
     out_h, xe, xo, ze, zo,
-    out, p0, p1, pz0, pz1, sems, p_sems,
+    alpha, vx, vz, out, p0, p1, pz0, pz1, sems, p_sems,
 ):
     cells_x, cells_z, beam = alpha.shape
     chunks = cells_z // SUB
@@ -174,9 +191,11 @@
     top = row_is((SUB, beam), 0)
     bottom = row_is((SUB, beam), SUB - 1)
     parts = parts_of(cells_x)
+    fields = ((alpha_h, alpha), (vx_h, vx), (vz_h, vz))
+    ins = fetch_fields(fields, sems)
     p_ins = fetch(x_planes(p_h) + z_tiles(p_h), [p0, p1, pz0, pz1], p_sems)
     outs = [
-        pltpu.make_async_copy(out.at[pl.ds(f, c)], out_h.at[pl.ds(f, c)], sems.at[n])
+        pltpu.make_async_copy(out.at[pl.ds(f, c)], out_h.at[pl.ds(f, c)], sems.at[len(fields), n])
         for n, (f, c) in enumerate(parts)
     ]
 
@@ -227,6 +246,8 @@
         zo[0, pl.ds(x, 1), :] = jnp.where(ev_z, z_down, z_up)
 
     for n, (first, count) in enumerate(parts):
+        for copies in ins:
+            copies[n].wait()
         begin = max(first - 1, 0)
         end = first + count - 1
         if begin == 0:
@@ -258,66 +279,66 @@
         copy.wait()
 
 
-def coefficients(alpha_h, after, alpha, cx, cz, cy, inverse, sems):
-    del after
-    cells_x, cells_z, beam = alpha.shape
+def coefficients(half, cx, cz, cy, inverse, arrived):
+    cells_x, cells_z, beam = half.shape
     chunks = cells_z // SUB
     top = row_is((SUB, beam), 0)
     bottom = row_is((SUB, beam), SUB - 1)
     lane = lax.broadcasted_iota(jnp.int32, (SUB, beam), 1)
-    ins = fetch_field(alpha_h, alpha, sems, 0)
-    cx[0] = jnp.zeros((cells_z, beam), F32)
+    end_lane = lane[:, beam - LANES:] == beam - 1
+    none = jnp.zeros((cells_z, beam), F32)
+    cx[0] = none
+    cx[cells_x] = none
 
     def at(k):
         return pl.ds(k * SUB, SUB)
 
-    def plane(x):
-        inside = jnp.where(x < cells_x - 1, 2.0, 0.0)
-        nxt = jnp.minimum(x + 1, cells_x - 1)
+    def plane(x, last):
         above = jnp.zeros((SUB, beam), F32)
         for k in reversed(range(chunks)):
-            rho = 1.0 + 9.0 * alpha[x, at(k), :]
-            rho_x = 1.0 + 9.0 * alpha[nxt, at(k), :]
-            hx = inside / (rho + rho_x)
-            cx[x + 1, at(k), :] = hx
-            rolled = pltpu.roll(rho, 1, 0)
+            r = half[x, at(k), :]
+            total = cx[x, at(k), :]
+            if not last:
+                hx = 1.0 / (r + half[x + 1, at(k), :])
+                cx[x + 1, at(k), :] = hx
+                total = total + hx
+            rolled = pltpu.roll(r, 1, 0)
             if k == 0:
-                hz = jnp.where(top, 0.0, 2.0 / (rho + rolled))
+                hz = jnp.where(top, 0.0, 1.0 / (r + rolled))
             else:
-                below = pltpu.roll(1.0 + 9.0 * alpha[x, at(k - 1), :], 1, 0)
-                hz = 2.0 / (rho + jnp.where(top, below, rolled))
+                below = pltpu.roll(half[x, at(k - 1), :], 1, 0)
+                hz = 1.0 / (r + jnp.where(top, below, rolled))
             cz[x, at(k), :] = hz
             up = pltpu.roll(hz, SUB - 1, 0)
-            hz_up = jnp.where(bottom, above, up)
+            total = total + (hz + jnp.where(bottom, above, up))
             above = up
-            hy_all = 2.0 / (rho + jnp.where(lane == 0, 0.0, pltpu.roll(rho, 1, 1)))
+            hy_all = 1.0 / (r + jnp.where(lane == 0, 0.0, pltpu.roll(r, 1, 1)))
             hy = jnp.where(lane == 0, 0.0, hy_all)
             cy[x, at(k), :] = hy
-            far = rho[:, beam - LANES:]
-            edge = jnp.where(lane[:, beam - LANES:] == beam - 1, 2.0 / far, 0.0)
+            edge = jnp.where(end_lane, 1.0 / r[:, beam - LANES:], 0.0)
             hy_up = pltpu.roll(hy, beam - 1, 1)
             hy_up = jnp.concatenate(
                 [hy_up[:, : beam - LANES], hy_up[:, beam - LANES:] + edge], axis=1
             )
-            inverse[x, at(k), :] = 1.0 / (cx[x, at(k), :] + hx + hz + hz_up + hy_all + hy_up)
-
-    parts = parts_of(cells_x)
-    for n, (first, count) in enumerate(parts):
-        ins[n].wait()
-        end = cells_x if n == len(parts) - 1 else first + count - 1
-
-        @pl.loop(max(first - 1, 0), end)
+            inverse[x, at(k), :] = 1.0 / (total + (hy_all + hy_up))
+
+    begin = 0
+    for stop in arrived():
+        @unrolled(begin, stop - 1, 3)
         def _(x):
-            plane(x)
+            plane(x, False)
+
+        begin = stop - 1
+    plane(cells_x - 1, True)
 
 
 def close(
-    p_in, inverse_in, alpha, xe_in, xo_in, ze_in, zo_in,
+    p_in, inverse_in, half, xe_in, xo_in, ze_in, zo_in,
     p, inverse, gx, gz, xe, xo, ze, zo,
     wx,
 ):
     del p_in, inverse_in
-    cells_x, cells_z, beam = alpha.shape
+    cells_x, cells_z, beam = half.shape
     chunks = cells_z // SUB
     ev_x, ev_z = even("slab"), even("depth")
     has = [inner("slab"), inner("depth")]
@@ -329,8 +350,8 @@
         for k in range(chunks):
             a, b = xe_in[:, at(k), :], xo_in[:, at(k), :]
             v = (jnp.where(ev_x, a, b) if side else jnp.where(ev_x, b, a)).astype(F32)
-            halo = has[0][side] * (9.0 * v[0] + 5.5)
-            c = 2.0 / (1.0 + 9.0 * alpha[x, at(k), :] + halo)
+            halo = has[0][side] * (4.5 * v[0] + 2.75)
+            c = 1.0 / (half[x, at(k), :] + halo)
             w = 1.0 / inverse[x, at(k), :]
             open_c = has[0][side] * c
             p[x, at(k), :] = p[x, at(k), :] * w + open_c * v[1]
@@ -343,8 +364,8 @@
             here = row_is((SUB, beam), 0 if side == 0 else SUB - 1)
             a, b = ze_in[:, pl.ds(x, 1), :], zo_in[:, pl.ds(x, 1), :]
             v = jnp.where(ev_z, a, b) if side else jnp.where(ev_z, b, a)
-            halo = jnp.broadcast_to(has[1][side] * (9.0 * v[0] + 5.5), (SUB, beam))
-            c = jnp.where(here, 2.0 / (1.0 + 9.0 * alpha[x, at(k), :] + halo), 0.0)
+            halo = jnp.broadcast_to(has[1][side] * (4.5 * v[0] + 2.75), (SUB, beam))
+            c = jnp.where(here, 1.0 / (half[x, at(k), :] + halo), 0.0)
             open_c = has[1][side] * c
             add = open_c * jnp.broadcast_to(v[1], (SUB, beam))
             if plane is None:
@@ -388,27 +409,55 @@
 
 
 def by_lanes(ref):
-    cells_x, cells_z, beam = ref.shape
+    _, _, beam = ref.shape
     blocks = beam // LANES
     for b in range(blocks):
         yield b, pl.ds(b * LANES, LANES)
 
 
-def scatter(capacity, got, div_h, rhs, row_out, rec32, row_v, row_s, hull, div, sems, sem):
+def middle(
+    capacity, got, alpha_h, div_h, p_h,
+    half, cx, cz, cy, inverse, rhs, p, row_out,
+    rec32, row_v, row_s, hull, div, p0, sems, sem,
+):
     devices, rows, _ = got.shape
     cells_x, cells_z, beam = rhs.shape
     blocks = beam // LANES
-    ins = fetch_field(div_h, div, sems, 0)
     digits = got[:, rows - 1, :].astype(F32)
-    seg = (digits * float(DIGIT) + pltpu.roll(digits, LANES - capacity, 1)).astype(jnp.int32)
+    seg = (digits * float(DIGIT) + pltpu.roll(digits, LANES - capacity, 1)).astype(jnp.int32) - DIGIT
     across = seg // blocks
     row = ((across // cells_z) * blocks + seg % blocks) * cells_z + across % cells_z
+    slots = lax.broadcasted_iota(jnp.int32, seg.shape, 0) * capacity
+    slots = slots + lax.broadcasted_iota(jnp.int32, seg.shape, 1)
+    row = jnp.where(seg < 0, slots % hull.shape[0], row)
     row_v[...] = row
     row_out[...] = row
     copy = pltpu.make_async_copy(row_v, row_s, sem)
     copy.start()
+    cut = max(1, cells_x // 4)
+    parts = [(0, cut), (cut, cells_x)]
+    alpha_in = fetch(
+        [alpha_h.at[pl.ds(i, j - i)] for i, j in parts], [half.at[pl.ds(i, j - i)] for i, j in parts], sems
+    )
+    rest = [
+        pltpu.make_async_copy(h, v, sems.at[2 + n]) for n, (h, v) in enumerate(((div_h, div), (p_h, p0)))
+    ]
+    for other in rest:
+        other.start()
     rec32[...] = got[...].astype(F32).reshape(devices * rows, LANES)
     hull[...] = jnp.zeros_like(hull)
+
+    def arrived():
+        for (i, j), part in zip(parts, alpha_in):
+            part.wait()
+
+            @unrolled(i, j)
+            def _(x):
+                half[x] = 0.5 + 4.5 * half[x]
+
+            yield j
+
+    coefficients(half, cx, cz, cy, inverse, arrived)
     copy.wait()
 
     @pl.loop(0, devices)
@@ -417,17 +466,22 @@
             n = row_s[d, s]
             hull[pl.ds(n, 1), :] += rec32[pl.ds(d * rows + s, 1), :]
 
-    for copy in ins:
-        copy.wait()
-
-    @pl.loop(0, cells_x)
-    def _(x):
+    for other in rest:
+        other.wait()
+
+    def source(x, at):
+        parts = []
         for b, lanes in by_lanes(rhs):
-            first = pl.multiple_of((x * blocks + b) * cells_z, SUB)
-            rhs[x, :, lanes] = div[x, :, lanes] + hull[pl.ds(first, cells_z), :]
-
-
-def sweep(p, cx, cz, cy, inverse, rhs, out):
+            first = pl.multiple_of((x * blocks + b) * cells_z + at.start, SUB)
+            parts.append(div[x, at, lanes] + hull[pl.ds(first, SUB), :])
+        value = jnp.concatenate(parts, axis=1)
+        rhs[x, at, :] = value
+        return value
+
+    sweep(p0, cx, cz, cy, inverse, source, p)
+
+
+def sweep(p, cx, cz, cy, inverse, source, out, start=0, stop=None):
     cells_x, cells_z, beam = p.shape
     chunks = cells_z // SUB
     top = row_is((SUB, beam), 0)
@@ -436,7 +490,7 @@
     def at(k):
         return pl.ds(k * SUB, SUB)
 
-    @pl.loop(0, cells_x)
+    @unrolled(start, cells_x if stop is None else stop)
     def _(x):
         prv = jnp.maximum(x - 1, 0)
         nxt = jnp.minimum(x + 1, cells_x - 1)
@@ -457,7 +511,11 @@
             total = total + (hz * down + jnp.where(bottom, above, up))
             above = up
             total = total + (hy * pltpu.roll(here, 1, 1) + pltpu.roll(hy * here, beam - 1, 1))
-            out[x, at(k), :] = (total - rhs[x, at(k), :]) * inverse[x, at(k), :]
+            out[x, at(k), :] = (total - source(x, at(k))) * inverse[x, at(k), :]
+
+
+def next_sweep(p, cx, cz, cy, inverse, rhs, out):
+    sweep(p, cx, cz, cy, inverse, lambda x, at: rhs[x, at, :], out)
 
 
 def add_borders(p_in, xe_in, xo_in, ze_in, zo_in, gx, gz, p, send=None):
@@ -501,16 +559,46 @@
     add_borders(p_in, xe_in, xo_in, ze_in, zo_in, gx, gz, p, (xe, xo, ze, zo))
 
 
+def inner_part(ref, count):
+    return ref.at[pl.ds(1, count), pl.ds(SUB, ref.shape[1] - 2 * SUB), :]
+
+
+def border_parts(ref, count):
+    cells_x, cells_z, _ = ref.shape
+    planes = pl.ds(1, count)
+    return [
+        ref.at[0],
+        ref.at[pl.ds(count + 1, cells_x - count - 1)],
+        ref.at[planes, pl.ds(0, SUB), :],
+        ref.at[planes, pl.ds(cells_z - SUB, SUB), :],
+    ]
+
+
+def early_planes(cells_x):
+    return max(1, cells_x * 3 // 4 - 1)
+
+
+def last_sweep(p, cx, cz, cy, inverse, rhs, out, out_h, sem):
+    count = early_planes(p.shape[0])
+    copy = pltpu.make_async_copy(inner_part(out, count), inner_part(out_h, count), sem)
+    sweep(p, cx, cz, cy, inverse, lambda x, at: rhs[x, at, :], out, stop=count + 1)
+    copy.start()
+    sweep(p, cx, cz, cy, inverse, lambda x, at: rhs[x, at, :], out, start=count + 1)
+    copy.wait()
+
+
 def fix_and_gather(
-    capacity, p_in, xe_in, xo_in, ze_in, zo_in, gx, gz, row, p_h, back, p, split, rows32, sems
+    capacity, p_in, xe_in, xo_in, ze_in, zo_in, gx, gz, row_v, out_in, p, back, out_h, split, rows32, row, sem, sems
 ):
+    del out_in
     cells_x, cells_z, beam = p.shape
-    p[...] = p_in[...]
+    row_copy = pltpu.make_async_copy(row_v, row, sem)
+    row_copy.start()
     add_borders(p_in, xe_in, xo_in, ze_in, zo_in, gx, gz, p)
+    count = early_planes(cells_x)
+    outs = fetch(border_parts(p, count), border_parts(out_h, count), sems)
     blocks = beam // LANES
     devices = back.shape[0]
-    out = pltpu.make_async_copy(p, p_h, sems)
-    out.start()
 
     @pl.loop(0, cells_x)
     def _(x):
@@ -518,16 +606,19 @@
             first = pl.multiple_of((x * blocks + b) * cells_z, SUB)
             split[pl.ds(first, cells_z), :] = p[x, :, lanes]
 
+    row_copy.wait()
+
     @pl.loop(0, devices)
     def _(d):
         for s in range(capacity):
             rows32[pl.ds(d * capacity + s, 1), :] = split[pl.ds(row[d, s], 1), :]
 
     back[...] = rows32[...].astype(BF16).reshape(back.shape)
-    out.wait()
-
-
-def unroute(back, slot, out):
+    for copy in outs:
+        copy.wait()
+
+
+def leave(back, slot, out):
     rows = back.shape[0] * back.shape[1]
     panels = out.shape[0]
     pick = lax.broadcasted_iota(jnp.int32, (rows, panels), 0) == slot[...]
@@ -561,93 +652,74 @@
     def swaps(xe, xo, ze, zo):
         return swap(xe, "slab", 0), swap(xo, "slab", 1), swap(ze, "depth", 0), swap(zo, "depth", 1)
 
-    send, slot = call(
-        functools.partial(route, capacity, rows, devices),
-        [shape((devices, rows, LANES), BF16), shape((1, panels), jnp.int32)],
+    *packed, send, slot = call(
+        functools.partial(enter, capacity, rows, devices),
+        faces + [shape((devices, rows, LANES), BF16), shape((1, panels), jnp.int32)],
+        alpha, vel_x, vel_z,
         panel_dest.reshape(1, panels), panel_segment.reshape(1, panels), panel_records,
-        far_in=(0, 1, 2), free_out=(0,), far_out=(1,),
+        far_in=(0, 1, 2, 3, 4, 5), far_out=(4, 5),
         scratch=[
+            near(xs), near(xs), near(tile), near(tile), near(xs), near(tile),
             near((1, panels), jnp.int32),
             near((1, panels), jnp.int32),
             near((panels, LANES), BF16),
             near((1, panels), jnp.int32),
-            DMA((4,)),
+            near((devices, rows, LANES), BF16),
+            DMA((11,)),
         ],
-        name="route",
-    )
+    )
+    halo = swaps(*packed)
     got = lax.all_to_all(send, axes, split_axis=0, concat_axis=0, tiled=True)
-
-    packed = call(
-        pack_first, faces, alpha, vel_x, vel_z,
-        far_in=(0, 1, 2),
-        scratch=[near(xs), near(xs), near(tile), near(tile), near(xs), near(tile), DMA((6,))],
-        name="pack_first",
-    )
     alpha_next, *packed = call(
-        advect, [field] + two_faces, alpha, vel_x, vel_z, press_guess, *swaps(*packed),
-        far_in=(3,), far_out=(0,),
-        scratch=[near(alpha.shape), near(xs), near(xs), near(tile), near(tile), DMA((parts,)), DMA((4,))],
-        name="advect",
+        advect, [field] + two_faces, alpha, vel_x, vel_z, press_guess, *halo,
+        far_in=(0, 1, 2, 3), far_out=(0,),
+        scratch=[near(alpha.shape)] * 4 + [near(xs), near(xs), near(tile), near(tile), DMA((4, parts)), DMA((4,))],
     )
     halo = swaps(*packed)
-    near_alpha, cx, cz, cy, inverse = call(
-        coefficients,
-        [field, shape((cells_x + 1,) + xs), field, field, field],
-        alpha_next, got,
-        far_in=(0,),
-        in_specs={1: pl.BlockSpec(memory_space=pl.ANY)},
-        scratch=[DMA((1, parts))],
-        name="coefficients",
-    )
-    rhs, row = call(
-        functools.partial(scatter, capacity),
-        [field, shape((devices, LANES), jnp.int32)],
-        got, divergence,
-        far_in=(1,),
+    half, cx, cz, cy, inverse, rhs, pressure, row = call(
+        functools.partial(middle, capacity),
+        [field, shape((cells_x + 1,) + xs), field, field, field, field, field, shape((devices, LANES), jnp.int32)],
+        got, alpha_next, divergence, press_guess,
+        far_in=(1, 2, 3),
         scratch=[
             near((devices * rows, LANES)),
             near((devices, LANES), jnp.int32),
             pltpu.SMEM((devices, LANES), jnp.int32),
             near(lines),
             near(alpha.shape),
-            DMA((1, parts)),
+            near(alpha.shape),
+            DMA((4,)),
             DMA,
         ],
-        name="scatter",
-    )
-    (pressure,) = call(sweep, [field], press_guess, cx, cz, cy, inverse, rhs, name="sweep")
+    )
     pressure, inverse, gx, gz, *packed = call(
         close,
         [field, field, shape((2,) + xs), shape((2,) + zs)] + faces,
-        pressure, inverse, near_alpha, *halo,
+        pressure, inverse, half, *halo,
         aliases={0: 0, 1: 1},
         scratch=[near((2,) + xs)],
-        name="close",
     )
     halo = swaps(*packed)
-    (pressure,) = call(sweep, [field], pressure, cx, cz, cy, inverse, rhs, name="sweep")
-    pressure, *packed = call(
-        fix_and_send, [field] + faces, pressure, *halo, gx, gz, aliases={0: 0}, name="fix"
-    )
+    (pressure,) = call(next_sweep, [field], pressure, cx, cz, cy, inverse, rhs)
+    pressure, *packed = call(fix_and_send, [field] + faces, pressure, *halo, gx, gz, aliases={0: 0})
     halo = swaps(*packed)
-    (pressure,) = call(sweep, [field], pressure, cx, cz, cy, inverse, rhs, name="sweep")
-    pressure, back = call(
+    last, out = call(last_sweep, [field, field], pressure, cx, cz, cy, inverse, rhs, far_out=(1,), scratch=[DMA])
+    _, back, pressure = call(
         functools.partial(fix_and_gather, capacity),
-        [field, shape((devices, capacity, LANES), BF16)],
-        pressure, *halo, gx, gz, row,
-        far_out=(0,),
-        in_specs={7: pl.BlockSpec(memory_space=pltpu.SMEM)},
-        scratch=[near(alpha.shape), near(lines), near((devices * capacity, LANES)), DMA],
-        name="gather",
+        [field, shape((devices, capacity, LANES), BF16), field],
+        last, *halo, gx, gz, row, out,
+        far_in=(8,), far_out=(2,),
+        aliases={0: 0, 8: 2},
+        scratch=[
+            near(lines),
+            near((devices * capacity, LANES)),
+            pltpu.SMEM((devices, LANES), jnp.int32),
+            DMA,
+            DMA((4,)),
+        ],
     )
     returned = lax.all_to_all(back, axes, split_axis=0, concat_axis=0, tiled=True)
-    panel_pressure = pl.pallas_call(
-        unroute,
-        out_shape=shape((panels, LANES), BF16),
-        in_specs=[WHOLE] * 2,
-        out_specs=WHOLE,
-        name="unroute",
-    )(returned, slot)
+    (panel_pressure,) = call(leave, [shape((panels, LANES), BF16)], returned, slot, free_out=(0,), limit=4 * MIB)
     return (pressure, alpha_next, panel_pressure)
 
 

time: 66.7 us -> 62.7 us (0.940)
  Pallas kernels: 26.9 us -> 22.1 us
  starting transfers between devices: 24.2 us -> 25.9 us
    pallas_call x11 -> x9, Pallas kernels: 25 us -> 22.1 us  [call(): pl.pallas_call(kernel, out_shape=shapes, in_specs=specs, out_specs=[FAR i...]
    pallas_call x1 -> x0, Pallas kernels: 1.82 us -> none  [body(): pl.pallas_call(unroute, out_shape=shape((panels, LANES), BF16), in_specs=...]
    ppermute x16, starting transfers between devices: 16.9 us -> 18.6 us  [swap(): return lax.ppermute(block, ('slab', 'depth'), pairs)]
  transfers between devices with their start and end apart: 17 -> 17, of which waited for: 2 -> 2; matrix products, arithmetic and copies ran while one was open for 0% -> 0% of each run, Pallas kernels for 29% -> 27%
where the time goes in v3:
time: 62.7 us; the launch traced here: 62.5 us
  starting transfers between devices  25.9 us (41%)
  Pallas kernels  22.1 us (35%)
  blocking collectives  10.9 us (17%)
  waiting for transfers between devices  2.79 us (4%)
  between operations  0.76 us (1%)
    pallas_call x9, Pallas kernels, call(): pl.pallas_call(kernel, out_shape=shapes, in_specs=specs, out_specs=[FAR i...  22.1 us
    ppermute x16, starting transfers between devices, swap(): return lax.ppermute(block, ('slab', 'depth'), pairs)  18.6 us
    all_to_all x1, blocking collectives, body(): lax.all_to_all(back, axes, split_axis=0, concat_axis=0, tiled=True)  10.9 us
    all_to_all x1, starting transfers between devices, body(): got = lax.all_to_all(send, axes, split_axis=0, concat_axis=0, tiled=True)  7.33 us
    ppermute x16, waiting for transfers between devices, swap(): return lax.ppermute(block, ('slab', 'depth'), pairs)  2.79 us
  transfers between devices with their start and end apart: 17, of which 2 were waited for; matrix products, arithmetic and copies ran while one was open for 0% of the time, Pallas kernels for 27%

profile of v3, /device:TPU:0, one launch (start us, length us, event | category | flops | bytes accessed | tf_op | source)
XLA Modules:
  0.0 62.5 jit_solution(1829516950630697904)
XLA Ops:
  0.6 2.0 %shard_map.103 = (bf16[64,512]{1,0:T(8,128)(2,1)S(1)}, bf16[64,512]{1,0:T(8,128)(2,1)S(1)}, f32[16,512]{1,0:T(8,128)S(1)}, f32[16,512]{1,0:T(8,128)S(1)}, bf16[3...) custom-call(f32[16,64,512]{2,1,0:T(8,128)} %alpha_h.1, f32[16,64,512]{2,1,0:T(8,128)} %vx_h.1, f32[16,64,512]{2,1,0:T(8,128)} %vz_h.1, ...), custom_call_target="tpu_custom_call" | custom-call | tf_op jit(solution)/shard_map/pallas_call | solution.py:29
  2.7 7.3 %all-to-all-start = ((bf16[32,24,128]{2,1,0:T(8,128)(2,1)}), bf16[32,24,128]{2,1,0:T(8,128)(2,1)S(1)}, u32[]{:S(2)}, u32[]{:S(2)}) async-start(bf16[32,24,128]{2,1,0:T(8,128)(2,1)} %get-tuple-element.39), calls=%async_computation | async-start | bytes 393216 | tf_op jit(solution)/shard_map/all_to_all | solution.py:672
  10.0 1.8 %collective-permute-start = (bf16[64,512]{1,0:T(8,128)(2,1)S(1)}, bf16[64,512]{1,0:T(8,128)(2,1)S(1)}, u32[]{:S(2)}, u32[]{:S(2)}) collective-permute-start(bf16[64,512]{1,0:T(8,128)(2,1)S(1)} %get-tuple-element.40), channel_id=1, source_target_pairs={{0,4},{1,5},{2,6},{3,7},{4,0},{5,1},{6,2},{7,3},{8,12},{9,13},{10,... | collective-permute-start | bytes 196616 | tf_op jit(solution)/shard_map/ppermute | solution.py:61
  11.9 0.5 collective-permute-start.2
  12.4 2.4 %collective-permute-start.3 = (f32[16,512]{1,0:T(8,128)S(1)}, f32[16,512]{1,0:T(8,128)S(1)}, u32[]{:S(2)}, u32[]{:S(2)}) collective-permute-start(f32[16,512]{1,0:T(8,128)S(1)} %get-tuple-element.43), channel_id=1, source_target_pairs={{0,4},{1,2},{2,1},{3,7},{4,0},{5,6},{6,5},{7,3},{8,12},{9,10},{10,... | collective-permute-start | bytes 98312 | tf_op jit(solution)/shard_map/ppermute | solution.py:61
  14.8 0.0 collective-permute-done.2.ze_in
  14.8 2.0 %collective-permute-done.3.zo_in = f32[16,512]{1,0:T(8,128)S(1)} collective-permute-done((f32[16,512]{1,0:T(8,128)S(1)}, f32[16,512]{1,0:T(8,128)S(1)}, u32[]{:S(2)}, u32[]{:S(2)}) %collective-permute-start.3) | collective-permute-done | bytes 32800 | tf_op jit(solution)/shard_map/ppermute | solution.py:61
  16.8 4.7 %shard_map.104 = (f32[16,64,512]{2,1,0:T(8,128)}, bf16[2,64,512]{2,1,0:T(8,128)(2,1)S(1)}, bf16[2,64,512]{2,1,0:T(8,128)(2,1)S(1)}, f32[2,16,512]{2,1,0:T(8,128)S(1)}, f32[2,16,512]{2,1,0:T(8,128)S(1)}) custom-call(f32[16,64,512]{2,1,0:T(8,128)} %alpha_h.1, f32[16,64,512]{2,1,0:T(8,128)} %vx_h.1, f32[16,64,512]{2,1,0:T(8,128)} %vz_h.1, f32[16,64,512]{2,1,0:T(8,128)} %p_h.3, ...), custom_call_target="tpu_custom_call" | custom-call | tf_op jit(solution)/shard_map/pallas_call | solution.py:29
  21.4 2.3 %collective-permute-start.4 = (bf16[2,64,512]{2,1,0:T(8,128)(2,1)S(1)}, bf16[2,64,512]{2,1,0:T(8,128)(2,1)S(1)}, u32[]{:S(2)}, u32[]{:S(2)}) collective-permute-start(bf16[2,64,512]{2,1,0:T(8,128)(2,1)S(1)} %get-tuple-element.48), channel_id=1, source_target_pairs={{0,4},{1,5},{2,6},{3,7},{4,0},{5,1},{6,2},{7,3},{8,12},{9,13},{10,... | collective-permute-start | bytes 393224 | tf_op jit(solution)/shard_map/ppermute | solution.py:61
  23.7 0.0 collective-permute-start.5
  23.7 0.5 collective-permute-start.6
  24.2 3.4 %collective-permute-start.7 = (f32[2,16,512]{2,1,0:T(8,128)S(1)}, f32[2,16,512]{2,1,0:T(8,128)S(1)}, u32[]{:S(2)}, u32[]{:S(2)}) collective-permute-start(f32[2,16,512]{2,1,0:T(8,128)S(1)} %get-tuple-element.51), channel_id=1, source_target_pairs={{0,4},{1,2},{2,1},{3,7},{4,0},{5,6},{6,5},{7,3},{8,12},{9,10},{10,... | collective-permute-start | bytes 196616 | tf_op jit(solution)/shard_map/ppermute | solution.py:61
  27.6 0.0 all-to-all-done.got
  27.6 8.3 %shard_map.105 = (f32[16,64,512]{2,1,0:T(8,128)S(1)}, f32[17,64,512]{2,1,0:T(8,128)S(1)}, f32[16,64,512]{2,1,0:T(8,128)S(1)}, f32[16,64,512]{2,1,0:T(8,128)S(1)}...) custom-call(bf16[32,24,128]{2,1,0:T(8,128)(2,1)S(1)} %all-to-all-don, ...), custom_call_target="tpu_custom_call" | custom-call | tf_op jit(solution)/shard_map/pallas_call | solution.py:29
  36.0 0.0 collective-permute-done.6.ze_in
  36.0 0.0 collective-permute-done.5.xo_in
  36.0 0.7 %shard_map.106 = (f32[16,64,512]{2,1,0:T(8,128)S(1)}, f32[16,64,512]{2,1,0:T(8,128)S(1)}, f32[2,64,512]{2,1,0:T(8,128)S(1)}, f32[2,16,512]{2,1,0:T(8,128)S(1)}, ...) custom-call(f32[16,64,512]{2,1,0:T(8,128)S(1)} %get-tuple-element.45, ...), custom_call_target="tpu_custom_call", output_to_operand_aliasing={{0}: (0, {}), {1}: (1, {})} | custom-call | tf_op jit(solution)/shard_map/pallas_call | solution.py:29
  36.7 0.1 collective-permute-start.8
  36.8 1.3 %collective-permute-start.9 = (bf16[64,512]{1,0:T(8,128)(2,1)S(1)}, bf16[64,512]{1,0:T(8,128)(2,1)S(1)}, u32[]{:S(2)}, u32[]{:S(2)}) collective-permute-start(bf16[64,512]{1,0:T(8,128)(2,1)S(1)} %get-tuple-element.59), channel_id=1, source_target_pairs={{0,1},{1,0},{2,3},{3,2},{4,8},{5,9},{6,10},{7,11},{8,4},{9,5},{10,... | collective-permute-start | bytes 196616 | tf_op jit(solution)/shard_map/ppermute | solution.py:61
  38.1 0.0 collective-permute-start.10
  38.1 1.7 %collective-permute-start.11 = (f32[16,512]{1,0:T(8,128)S(1)}, f32[16,512]{1,0:T(8,128)S(1)}, u32[]{:S(2)}, u32[]{:S(2)}) collective-permute-start(f32[16,512]{1,0:T(8,128)S(1)} %get-tuple-element.61), channel_id=1, source_target_pairs={{0,4},{1,2},{2,1},{3,7},{4,0},{5,6},{6,5},{7,3},{8,12},{9,10},{10,... | collective-permute-start | bytes 98312 | tf_op jit(solution)/shard_map/ppermute | solution.py:61
  39.8 1.5 %shard_map.107.p_in = f32[16,64,512]{2,1,0:T(8,128)S(1)} custom-call(f32[16,64,512]{2,1,0:T(8,128)S(1)} %get-tuple-element.52.p, f32[17,64,512]{2,1,0:T(8,128)S(1)} %get-tuple-element.53.cx, f32[16,64,512]{2,1,0:T(8,128)S(1)} %get-tuple-element.54.cz, f32[16,64,512]{2,1,0:T(8,128)S(1)} %get-tuple-element.55.cy, ...), custom_call_target="tpu_custom_call" | custom-call | tf_op jit(solution)/shard_map/pallas_call | solution.py:29
  41.3 0.8 %collective-permute-done.11.zo_in = f32[16,512]{1,0:T(8,128)S(1)} collective-permute-done((f32[16,512]{1,0:T(8,128)S(1)}, f32[16,512]{1,0:T(8,128)S(1)}, u32[]{:S(2)}, u32[]{:S(2)}) %collective-permute-start.11) | collective-permute-done | bytes 32800 | tf_op jit(solution)/shard_map/ppermute | solution.py:61
  42.0 0.4 shard_map.108
  42.4 2.4 %collective-permute-start.12 = (bf16[64,512]{1,0:T(8,128)(2,1)S(1)}, bf16[64,512]{1,0:T(8,128)(2,1)S(1)}, u32[]{:S(2)}, u32[]{:S(2)}) collective-permute-start(bf16[64,512]{1,0:T(8,128)(2,1)S(1)} %get-tuple-element.66), channel_id=1, source_target_pairs={{0,4},{1,5},{2,6},{3,7},{4,0},{5,1},{6,2},{7,3},{8,12},{9,13},{10,... | collective-permute-start | bytes 196616 | tf_op jit(solution)/shard_map/ppermute | solution.py:61
  44.8 0.5 collective-permute-start.14
  45.3 1.7 %collective-permute-start.15 = (f32[16,512]{1,0:T(8,128)S(1)}, f32[16,512]{1,0:T(8,128)S(1)}, u32[]{:S(2)}, u32[]{:S(2)}) collective-permute-start(f32[16,512]{1,0:T(8,128)S(1)} %get-tuple-element.69), channel_id=1, source_target_pairs={{0,4},{1,2},{2,1},{3,7},{4,0},{5,6},{6,5},{7,3},{8,12},{9,10},{10,... | collective-permute-start | bytes 98312 | tf_op jit(solution)/shard_map/ppermute | solution.py:61
  47.0 2.1 %shard_map.109 = (f32[16,64,512]{2,1,0:T(8,128)S(1)}, f32[16,64,512]{2,1,0:T(8,128)}) custom-call(f32[16,64,512]{2,1,0:T(8,128)S(1)} %get-tuple-element.64.p, f32[17,64,512]{2,1,0:T(8,128)S(1)} %get-tuple-element.53.cx, f32[16,64,512]{2,1,0:T(8,128)S(1)} %get-tuple-element.54.cz, f32[16,64,512]{2,1,0:T(8,128)S(1)} %get-tuple-element.55.cy, ...), custom_call_target="tpu_custom_call" | custom-call | tf_op jit(solution)/shard_map/pallas_call | solution.py:29
  49.1 0.0 collective-permute-done.15.zo_in
  49.2 1.4 %shard_map.110 = (f32[16,64,512]{2,1,0:T(8,128)S(1)}, bf16[32,16,128]{2,1,0:T(8,128)(2,1)S(1)}, f32[16,64,512]{2,1,0:T(8,128)}) custom-call(f32[16,64,512]{2,1,0:T(8,128)S(1)} %get-tuple-element.65.p_in, bf16[64,512]{1,0:T(8,128)(2,1)S(1)} %collective-permute-done.12.xe_in, ...), custom_call_target="tpu_custom_call", output_to_operand_aliasing={{0}: (0, {}), {2}: (8, {})} | custom-call | tf_op jit(solution)/shard_map/pallas_call | solution.py:29
  50.6 10.9 %all_to_all.10.back = bf16[32,16,128]{2,1,0:T(8,128)(2,1)S(1)} all-to-all(bf16[32,16,128]{2,1,0:T(8,128)(2,1)S(1)} %get-tuple-element.73), channel_id=1, replica_groups=mesh['slab'=8,'depth'=4] {'slab','depth'}, dimensions={0} | all-to-all | bytes 262144 | tf_op jit(solution)/shard_map/all_to_all | solution.py:721
  61.6 0.9 %shard_map.111 = bf16[256,128]{1,0:T(8,128)(2,1)} custom-call(bf16[32,16,128]{2,1,0:T(8,128)(2,1)S(1)} %all_to_all.10.back, s32[1,256]{1,0:T(1,128)S(1)} %get-tuple-element.74.slot), custom_call_target="tpu_custom_call" | custom-call | tf_op jit(solution)/shard_map/pallas_call | solution.py:29
  (12 shorter events, 0.0 us)
Async XLA Ops:
  2.7 24.9 %all-to-all-start = ((bf16[32,24,128]{2,1,0:T(8,128)(2,1)}), bf16[32,24,128]{2,1,0:T(8,128)(2,1)S(1)}, u32[]{:S(2)}, u32[]{:S(2)}) async-start(bf16[32,24,128]{2,1,0:T(8,128)(2,1)} %get-tuple-element.39), calls=%async_computation | async-start | bytes 393216 | tf_op jit(solution)/shard_map/all_to_all | solution.py:672
  10.0 6.7 %collective-permute-start = (bf16[64,512]{1,0:T(8,128)(2,1)S(1)}, bf16[64,512]{1,0:T(8,128)(2,1)S(1)}, u32[]{:S(2)}, u32[]{:S(2)}) collective-permute-start(bf16[64,512]{1,0:T(8,128)(2,1)S(1)} %get-tuple-element.40), channel_id=1, source_target_pairs={{0,4},{1,5},{2,6},{3,7},{4,0},{5,1},{6,2},{7,3},{8,12},{9,13},{10,... | collective-permute-start | bytes 196616 | tf_op jit(solution)/shard_map/ppermute | solution.py:61
  11.9 4.9 %collective-permute-start.1 = (bf16[64,512]{1,0:T(8,128)(2,1)S(1)}, bf16[64,512]{1,0:T(8,128)(2,1)S(1)}, u32[]{:S(2)}, u32[]{:S(2)}) collective-permute-start(bf16[64,512]{1,0:T(8,128)(2,1)S(1)} %get-tuple-element.41), channel_id=1, source_target_pairs={{0,1},{1,0},{2,3},{3,2},{4,8},{5,9},{6,10},{7,11},{8,4},{9,5},{10,... | collective-permute-start | bytes 196616 | tf_op jit(solution)/shard_map/ppermute | solution.py:61
  11.9 2.9 %collective-permute-start.2 = (f32[16,512]{1,0:T(8,128)S(1)}, f32[16,512]{1,0:T(8,128)S(1)}, u32[]{:S(2)}, u32[]{:S(2)}) collective-permute-start(f32[16,512]{1,0:T(8,128)S(1)} %get-tuple-element.42), channel_id=1, source_target_pairs={{0,1},{1,0},{2,3},{3,2},{4,5},{5,4},{6,7},{7,6},{8,9},{9,8},{10,11... | collective-permute-start | bytes 98312 | tf_op jit(solution)/shard_map/ppermute | solution.py:61
  12.4 4.4 %collective-permute-start.3 = (f32[16,512]{1,0:T(8,128)S(1)}, f32[16,512]{1,0:T(8,128)S(1)}, u32[]{:S(2)}, u32[]{:S(2)}) collective-permute-start(f32[16,512]{1,0:T(8,128)S(1)} %get-tuple-element.43), channel_id=1, source_target_pairs={{0,4},{1,2},{2,1},{3,7},{4,0},{5,6},{6,5},{7,3},{8,12},{9,10},{10,... | collective-permute-start | bytes 98312 | tf_op jit(solution)/shard_map/ppermute | solution.py:61
  21.4 14.6 %collective-permute-start.4 = (bf16[2,64,512]{2,1,0:T(8,128)(2,1)S(1)}, bf16[2,64,512]{2,1,0:T(8,128)(2,1)S(1)}, u32[]{:S(2)}, u32[]{:S(2)}) collective-permute-start(bf16[2,64,512]{2,1,0:T(8,128)(2,1)S(1)} %get-tuple-element.48), channel_id=1, source_target_pairs={{0,4},{1,5},{2,6},{3,7},{4,0},{5,1},{6,2},{7,3},{8,12},{9,13},{10,... | collective-permute-start | bytes 393224 | tf_op jit(solution)/shard_map/ppermute | solution.py:61
  23.7 12.3 %collective-permute-start.5 = (bf16[2,64,512]{2,1,0:T(8,128)(2,1)S(1)}, bf16[2,64,512]{2,1,0:T(8,128)(2,1)S(1)}, u32[]{:S(2)}, u32[]{:S(2)}) collective-permute-start(bf16[2,64,512]{2,1,0:T(8,128)(2,1)S(1)} %get-tuple-element.49), channel_id=1, source_target_pairs={{0,1},{1,0},{2,3},{3,2},{4,8},{5,9},{6,10},{7,11},{8,4},{9,5},{10,... | collective-permute-start | bytes 393224 | tf_op jit(solution)/shard_map/ppermute | solution.py:61
  23.7 12.2 %collective-permute-start.6 = (f32[2,16,512]{2,1,0:T(8,128)S(1)}, f32[2,16,512]{2,1,0:T(8,128)S(1)}, u32[]{:S(2)}, u32[]{:S(2)}) collective-permute-start(f32[2,16,512]{2,1,0:T(8,128)S(1)} %get-tuple-element.50), channel_id=1, source_target_pairs={{0,1},{1,0},{2,3},{3,2},{4,5},{5,4},{6,7},{7,6},{8,9},{9,8},{10,11... | collective-permute-start | bytes 196616 | tf_op jit(solution)/shard_map/ppermute | solution.py:61
  24.2 11.7 %collective-permute-start.7 = (f32[2,16,512]{2,1,0:T(8,128)S(1)}, f32[2,16,512]{2,1,0:T(8,128)S(1)}, u32[]{:S(2)}, u32[]{:S(2)}) collective-permute-start(f32[2,16,512]{2,1,0:T(8,128)S(1)} %get-tuple-element.51), channel_id=1, source_target_pairs={{0,4},{1,2},{2,1},{3,7},{4,0},{5,6},{6,5},{7,3},{8,12},{9,10},{10,... | collective-permute-start | bytes 196616 | tf_op jit(solution)/shard_map/ppermute | solution.py:61
  36.7 5.3 %collective-permute-start.8 = (bf16[64,512]{1,0:T(8,128)(2,1)S(1)}, bf16[64,512]{1,0:T(8,128)(2,1)S(1)}, u32[]{:S(2)}, u32[]{:S(2)}) collective-permute-start(bf16[64,512]{1,0:T(8,128)(2,1)S(1)} %get-tuple-element.58), channel_id=1, source_target_pairs={{0,4},{1,5},{2,6},{3,7},{4,0},{5,1},{6,2},{7,3},{8,12},{9,13},{10,... | collective-permute-start | bytes 196616 | tf_op jit(solution)/shard_map/ppermute | solution.py:61
  36.8 5.2 %collective-permute-start.9 = (bf16[64,512]{1,0:T(8,128)(2,1)S(1)}, bf16[64,512]{1,0:T(8,128)(2,1)S(1)}, u32[]{:S(2)}, u32[]{:S(2)}) collective-permute-start(bf16[64,512]{1,0:T(8,128)(2,1)S(1)} %get-tuple-element.59), channel_id=1, source_target_pairs={{0,1},{1,0},{2,3},{3,2},{4,8},{5,9},{6,10},{7,11},{8,4},{9,5},{10,... | collective-permute-start | bytes 196616 | tf_op jit(solution)/shard_map/ppermute | solution.py:61
  38.1 3.2 %collective-permute-start.10 = (f32[16,512]{1,0:T(8,128)S(1)}, f32[16,512]{1,0:T(8,128)S(1)}, u32[]{:S(2)}, u32[]{:S(2)}) collective-permute-start(f32[16,512]{1,0:T(8,128)S(1)} %get-tuple-element.60), channel_id=1, source_target_pairs={{0,1},{1,0},{2,3},{3,2},{4,5},{5,4},{6,7},{7,6},{8,9},{9,8},{10,11... | collective-permute-start | bytes 98312 | tf_op jit(solution)/shard_map/ppermute | solution.py:61
  38.1 3.9 %collective-permute-start.11 = (f32[16,512]{1,0:T(8,128)S(1)}, f32[16,512]{1,0:T(8,128)S(1)}, u32[]{:S(2)}, u32[]{:S(2)}) collective-permute-start(f32[16,512]{1,0:T(8,128)S(1)} %get-tuple-element.61), channel_id=1, source_target_pairs={{0,4},{1,2},{2,1},{3,7},{4,0},{5,6},{6,5},{7,3},{8,12},{9,10},{10,... | collective-permute-start | bytes 98312 | tf_op jit(solution)/shard_map/ppermute | solution.py:61
  42.4 6.8 %collective-permute-start.12 = (bf16[64,512]{1,0:T(8,128)(2,1)S(1)}, bf16[64,512]{1,0:T(8,128)(2,1)S(1)}, u32[]{:S(2)}, u32[]{:S(2)}) collective-permute-start(bf16[64,512]{1,0:T(8,128)(2,1)S(1)} %get-tuple-element.66), channel_id=1, source_target_pairs={{0,4},{1,5},{2,6},{3,7},{4,0},{5,1},{6,2},{7,3},{8,12},{9,13},{10,... | collective-permute-start | bytes 196616 | tf_op jit(solution)/shard_map/ppermute | solution.py:61
  44.8 4.4 %collective-permute-start.13 = (bf16[64,512]{1,0:T(8,128)(2,1)S(1)}, bf16[64,512]{1,0:T(8,128)(2,1)S(1)}, u32[]{:S(2)}, u32[]{:S(2)}) collective-permute-start(bf16[64,512]{1,0:T(8,128)(2,1)S(1)} %get-tuple-element.67), channel_id=1, source_target_pairs={{0,1},{1,0},{2,3},{3,2},{4,8},{5,9},{6,10},{7,11},{8,4},{9,5},{10,... | collective-permute-start | bytes 196616 | tf_op jit(solution)/shard_map/ppermute | solution.py:61
  44.8 4.4 %collective-permute-start.14 = (f32[16,512]{1,0:T(8,128)S(1)}, f32[16,512]{1,0:T(8,128)S(1)}, u32[]{:S(2)}, u32[]{:S(2)}) collective-permute-start(f32[16,512]{1,0:T(8,128)S(1)} %get-tuple-element.68), channel_id=1, source_target_pairs={{0,1},{1,0},{2,3},{3,2},{4,5},{5,4},{6,7},{7,6},{8,9},{9,8},{10,11... | collective-permute-start | bytes 98312 | tf_op jit(solution)/shard_map/ppermute | solution.py:61
  45.3 3.9 %collective-permute-start.15 = (f32[16,512]{1,0:T(8,128)S(1)}, f32[16,512]{1,0:T(8,128)S(1)}, u32[]{:S(2)}, u32[]{:S(2)}) collective-permute-start(f32[16,512]{1,0:T(8,128)S(1)} %get-tuple-element.69), channel_id=1, source_target_pairs={{0,4},{1,2},{2,1},{3,7},{4,0},{5,6},{6,5},{7,3},{8,12},{9,10},{10,... | collective-permute-start | bytes 98312 | tf_op jit(solution)/shard_map/ppermute | solution.py:61

commit v4 on v3

--- a/solution.py
+++ b/solution.py
@@ -151,9 +151,9 @@
     digits = lax.dot_general(
         (hot_f * high).astype(BF16), at_high, contract, preferred_element_type=F32
     ) + lax.dot_general((hot_f * low).astype(BF16), at_low, contract, preferred_element_type=F32)
-    records = records.reshape(devices, rows, LANES)
-    is_digit = lax.broadcasted_iota(jnp.int32, records.shape, 1) >= capacity
-    send[...] = jnp.where(is_digit, digits[:, None, :], records).astype(BF16)
+    digits = jnp.broadcast_to(digits[:, None, :], (devices, rows, LANES)).reshape(devices * rows, LANES)
+    is_digit = lax.rem(lax.broadcasted_iota(jnp.int32, records.shape, 0), rows) >= capacity
+    send[...] = jnp.where(is_digit, digits, records).astype(BF16)
     send_out = pltpu.make_async_copy(send, send_h, sems.at[10])
     send_out.start()
     for copy in copies[3:]:
@@ -180,9 +180,9 @@
 
 
 def advect(
-    alpha_h, vx_h, vz_h, p_h, xe_in, xo_in, ze_in, zo_in,
-    out_h, xe, xo, ze, zo,
-    alpha, vx, vz, out, p0, p1, pz0, pz1, sems, p_sems,
+    alpha, vx_h, vz_h, p_h, xe_in, xo_in, ze_in, zo_in,
+    out_h, early, xe, xo, ze, zo,
+    vx, vz, out, p0, p1, pz0, pz1, sems, p_sems,
 ):
     cells_x, cells_z, beam = alpha.shape
     chunks = cells_z // SUB
@@ -191,7 +191,7 @@
     top = row_is((SUB, beam), 0)
     bottom = row_is((SUB, beam), SUB - 1)
     parts = parts_of(cells_x)
-    fields = ((alpha_h, alpha), (vx_h, vx), (vz_h, vz))
+    fields = ((vx_h, vx), (vz_h, vz))
     ins = fetch_fields(fields, sems)
     p_ins = fetch(x_planes(p_h) + z_tiles(p_h), [p0, p1, pz0, pz1], p_sems)
     outs = [
@@ -263,6 +263,7 @@
         if n > 0:
             outs[n - 1].start()
     outs[-1].start()
+    early[...] = out[pl.ds(0, early.shape[0])]
 
     for copy in p_ins:
         copy.wait()
@@ -284,8 +285,8 @@
     chunks = cells_z // SUB
     top = row_is((SUB, beam), 0)
     bottom = row_is((SUB, beam), SUB - 1)
-    lane = lax.broadcasted_iota(jnp.int32, (SUB, beam), 1)
-    end_lane = lane[:, beam - LANES:] == beam - 1
+    lane = lax.broadcasted_iota(jnp.int32, (SUB, LANES), 1)
+    start_lane, end_lane = lane == 0, lane == LANES - 1
     none = jnp.zeros((cells_z, beam), F32)
     cx[0] = none
     cx[cells_x] = none
@@ -293,8 +294,12 @@
     def at(k):
         return pl.ds(k * SUB, SUB)
 
+    def first_lane_zero(v):
+        return jnp.concatenate([jnp.where(start_lane, 0.0, v[:, :LANES]), v[:, LANES:]], axis=1)
+
     def plane(x, last):
         above = jnp.zeros((SUB, beam), F32)
+        rolled = pltpu.roll(half[x, at(chunks - 1), :], 1, 0)
         for k in reversed(range(chunks)):
             r = half[x, at(k), :]
             total = cx[x, at(k), :]
@@ -302,18 +307,18 @@
                 hx = 1.0 / (r + half[x + 1, at(k), :])
                 cx[x + 1, at(k), :] = hx
                 total = total + hx
-            rolled = pltpu.roll(r, 1, 0)
             if k == 0:
                 hz = jnp.where(top, 0.0, 1.0 / (r + rolled))
             else:
                 below = pltpu.roll(half[x, at(k - 1), :], 1, 0)
                 hz = 1.0 / (r + jnp.where(top, below, rolled))
+                rolled = below
             cz[x, at(k), :] = hz
             up = pltpu.roll(hz, SUB - 1, 0)
             total = total + (hz + jnp.where(bottom, above, up))
             above = up
-            hy_all = 1.0 / (r + jnp.where(lane == 0, 0.0, pltpu.roll(r, 1, 1)))
-            hy = jnp.where(lane == 0, 0.0, hy_all)
+            hy_all = 1.0 / (r + first_lane_zero(pltpu.roll(r, 1, 1)))
+            hy = first_lane_zero(hy_all)
             cy[x, at(k), :] = hy
             edge = jnp.where(end_lane, 1.0 / r[:, beam - LANES:], 0.0)
             hy_up = pltpu.roll(hy, beam - 1, 1)
@@ -324,7 +329,7 @@
 
     begin = 0
     for stop in arrived():
-        @unrolled(begin, stop - 1, 3)
+        @unrolled(begin, stop - 1, 1)
         def _(x):
             plane(x, False)
 
@@ -416,14 +421,15 @@
 
 
 def middle(
-    capacity, got, alpha_h, div_h, p_h,
+    capacity, rows, got, early, alpha_h, div_h, p_h,
     half, cx, cz, cy, inverse, rhs, p, row_out,
-    rec32, row_v, row_s, hull, div, p0, sems, sem,
+    hull, div, p0, rec32, row_v, row_s, sems, sem,
 ):
-    devices, rows, _ = got.shape
+    devices = got.shape[0] // rows
     cells_x, cells_z, beam = rhs.shape
     blocks = beam // LANES
-    digits = got[:, rows - 1, :].astype(F32)
+    rec32[...] = got[...].astype(F32)
+    digits = rec32[pl.ds(rows - 1, devices, stride=rows), :]
     seg = (digits * float(DIGIT) + pltpu.roll(digits, LANES - capacity, 1)).astype(jnp.int32) - DIGIT
     across = seg // blocks
     row = ((across // cells_z) * blocks + seg % blocks) * cells_z + across % cells_z
@@ -431,31 +437,36 @@
     slots = slots + lax.broadcasted_iota(jnp.int32, seg.shape, 1)
     row = jnp.where(seg < 0, slots % hull.shape[0], row)
     row_v[...] = row
-    row_out[...] = row
     copy = pltpu.make_async_copy(row_v, row_s, sem)
     copy.start()
-    cut = max(1, cells_x // 4)
-    parts = [(0, cut), (cut, cells_x)]
-    alpha_in = fetch(
-        [alpha_h.at[pl.ds(i, j - i)] for i, j in parts], [half.at[pl.ds(i, j - i)] for i, j in parts], sems
-    )
+    per = LANES // capacity
+    lane = lax.broadcasted_iota(jnp.int32, (devices // per, LANES), 1)
+    table = jnp.zeros(lane.shape, jnp.int32)
+    for j in range(per):
+        piece = pltpu.roll(row_v[pl.ds(j, devices // per, stride=per), :], j * capacity, 1)
+        table = jnp.where(lane // capacity == j, piece, table)
+    row_out[pl.ds(0, devices // per)] = table
+    cut = early.shape[0]
+    late = pl.ds(cut, cells_x - cut)
+    alpha_in = pltpu.make_async_copy(alpha_h.at[late], half.at[late], sems.at[0])
+    alpha_in.start()
     rest = [
-        pltpu.make_async_copy(h, v, sems.at[2 + n]) for n, (h, v) in enumerate(((div_h, div), (p_h, p0)))
+        pltpu.make_async_copy(h, v, sems.at[1 + n]) for n, (h, v) in enumerate(((div_h, div), (p_h, p0)))
     ]
     for other in rest:
         other.start()
-    rec32[...] = got[...].astype(F32).reshape(devices * rows, LANES)
-    hull[...] = jnp.zeros_like(hull)
 
     def arrived():
-        for (i, j), part in zip(parts, alpha_in):
-            part.wait()
-
-            @unrolled(i, j)
-            def _(x):
-                half[x] = 0.5 + 4.5 * half[x]
-
-            yield j
+        half[pl.ds(0, cut)] = 0.5 + 4.5 * early[...]
+        yield cut
+        hull[...] = jnp.zeros_like(hull)
+        alpha_in.wait()
+
+        @unrolled(cut, cells_x)
+        def _(x):
+            half[x] = 0.5 + 4.5 * half[x]
+
+        yield cells_x
 
     coefficients(half, cx, cz, cy, inverse, arrived)
     copy.wait()
@@ -463,8 +474,7 @@
     @pl.loop(0, devices)
     def _(d):
         for s in range(capacity):
-            n = row_s[d, s]
-            hull[pl.ds(n, 1), :] += rec32[pl.ds(d * rows + s, 1), :]
+            hull[pl.ds(row_s[d, s], 1), :] += rec32[pl.ds(d * rows + s, 1), :]
 
     for other in rest:
         other.wait()
@@ -588,17 +598,16 @@
 
 
 def fix_and_gather(
-    capacity, p_in, xe_in, xo_in, ze_in, zo_in, gx, gz, row_v, out_in, p, back, out_h, split, rows32, row, sem, sems
+    p_in, xe_in, xo_in, ze_in, zo_in, gx, gz, row_v, out_in, p, back, out_h, split, rows32, row, sem, sems
 ):
     del out_in
     cells_x, cells_z, beam = p.shape
-    row_copy = pltpu.make_async_copy(row_v, row, sem)
+    row_copy = pltpu.make_async_copy(row_v.at[pl.ds(0, row.shape[0])], row, sem)
     row_copy.start()
     add_borders(p_in, xe_in, xo_in, ze_in, zo_in, gx, gz, p)
     count = early_planes(cells_x)
     outs = fetch(border_parts(p, count), border_parts(out_h, count), sems)
     blocks = beam // LANES
-    devices = back.shape[0]
 
     @pl.loop(0, cells_x)
     def _(x):
@@ -608,10 +617,10 @@
 
     row_copy.wait()
 
-    @pl.loop(0, devices)
-    def _(d):
-        for s in range(capacity):
-            rows32[pl.ds(d * capacity + s, 1), :] = split[pl.ds(row[d, s], 1), :]
+    @pl.loop(0, row.shape[0])
+    def _(g):
+        for lane in range(LANES):
+            rows32[pl.ds(g * LANES + lane, 1), :] = split[pl.ds(row[g, lane], 1), :]
 
     back[...] = rows32[...].astype(BF16).reshape(back.shape)
     for copy in outs:
@@ -636,7 +645,7 @@
     capacity = 2 * panels // devices
     cells_x, cells_z, beam = alpha.shape
     field = shape(alpha.shape)
-    rows = -(-(capacity + 1) // SUB) * SUB
+    rows = (capacity + 2) // 2 * 2
     axes = ("slab", "depth")
 
     xs, zs = (cells_z, beam), (cells_x, beam)
@@ -644,6 +653,7 @@
     faces = [shape(xs, BF16)] * 2 + [shape(zs)] * 2
     two_faces = [shape((2,) + xs, BF16)] * 2 + [shape((2,) + zs)] * 2
     parts = len(parts_of(cells_x))
+    table = (devices * capacity // LANES, LANES)
     lines = (cells_x * cells_z * beam // LANES, LANES)
 
     def near(dims, dtype=F32):
@@ -654,7 +664,7 @@
 
     *packed, send, slot = call(
         functools.partial(enter, capacity, rows, devices),
-        faces + [shape((devices, rows, LANES), BF16), shape((1, panels), jnp.int32)],
+        faces + [shape((devices * rows, LANES), BF16), shape((1, panels), jnp.int32)],
         alpha, vel_x, vel_z,
         panel_dest.reshape(1, panels), panel_segment.reshape(1, panels), panel_records,
         far_in=(0, 1, 2, 3, 4, 5), far_out=(4, 5),
@@ -664,31 +674,34 @@
             near((1, panels), jnp.int32),
             near((panels, LANES), BF16),
             near((1, panels), jnp.int32),
-            near((devices, rows, LANES), BF16),
+            near((devices * rows, LANES), BF16),
             DMA((11,)),
         ],
     )
     halo = swaps(*packed)
-    got = lax.all_to_all(send, axes, split_axis=0, concat_axis=0, tiled=True)
-    alpha_next, *packed = call(
-        advect, [field] + two_faces, alpha, vel_x, vel_z, press_guess, *halo,
-        far_in=(0, 1, 2, 3), far_out=(0,),
-        scratch=[near(alpha.shape)] * 4 + [near(xs), near(xs), near(tile), near(tile), DMA((4, parts)), DMA((4,))],
+    got = lax.all_to_all(
+        send.reshape(devices, rows // 2, 2, LANES), axes, split_axis=0, concat_axis=0, tiled=True
+    ).reshape(devices * rows, LANES)
+    cut = max(1, cells_x // 4)
+    alpha_next, early, *packed = call(
+        advect, [field, shape((cut,) + xs)] + two_faces, alpha, vel_x, vel_z, press_guess, *halo,
+        far_in=(1, 2, 3), far_out=(0,),
+        scratch=[near(alpha.shape)] * 3 + [near(xs), near(xs), near(tile), near(tile), DMA((4, parts)), DMA((4,))],
     )
     halo = swaps(*packed)
     half, cx, cz, cy, inverse, rhs, pressure, row = call(
-        functools.partial(middle, capacity),
+        functools.partial(middle, capacity, rows),
         [field, shape((cells_x + 1,) + xs), field, field, field, field, field, shape((devices, LANES), jnp.int32)],
-        got, alpha_next, divergence, press_guess,
-        far_in=(1, 2, 3),
+        got, early, alpha_next, divergence, press_guess,
+        far_in=(2, 3, 4),
         scratch=[
+            near(lines),
+            near(alpha.shape),
+            near(alpha.shape),
             near((devices * rows, LANES)),
             near((devices, LANES), jnp.int32),
             pltpu.SMEM((devices, LANES), jnp.int32),
-            near(lines),
-            near(alpha.shape),
-            near(alpha.shape),
-            DMA((4,)),
+            DMA((3,)),
             DMA,
         ],
     )
@@ -705,7 +718,7 @@
     halo = swaps(*packed)
     last, out = call(last_sweep, [field, field], pressure, cx, cz, cy, inverse, rhs, far_out=(1,), scratch=[DMA])
     _, back, pressure = call(
-        functools.partial(fix_and_gather, capacity),
+        fix_and_gather,
         [field, shape((devices, capacity, LANES), BF16), field],
         last, *halo, gx, gz, row, out,
         far_in=(8,), far_out=(2,),
@@ -713,7 +726,7 @@
         scratch=[
             near(lines),
             near((devices * capacity, LANES)),
-            pltpu.SMEM((devices, LANES), jnp.int32),
+            pltpu.SMEM(table, jnp.int32),
             DMA,
             DMA((4,)),
         ],

time: 62.7 us -> 60.5 us (0.965)
  Pallas kernels: 22.1 us -> 20.4 us
    pallas_call x9, Pallas kernels: 22.1 us -> 20.4 us  [call(): pl.pallas_call(kernel, out_shape=shapes, in_specs=specs, out_specs=[FAR i...]
  transfers between devices with their start and end apart: 17 -> 17, of which waited for: 2 -> 2; matrix products, arithmetic and copies ran while one was open for 0% -> 0% of each run, Pallas kernels for 27% -> 25%
where the time goes in v4:
time: 60.5 us; the launch traced here: 60.3 us
  starting transfers between devices  25.4 us (42%)
  Pallas kernels  20.4 us (34%)
  blocking collectives  10.9 us (18%)
  waiting for transfers between devices  2.71 us (4%)
  between operations  0.79 us (1%)
    pallas_call x9, Pallas kernels, call(): pl.pallas_call(kernel, out_shape=shapes, in_specs=specs, out_specs=[FAR i...  20.4 us
    ppermute x16, starting transfers between devices, swap(): return lax.ppermute(block, ('slab', 'depth'), pairs)  18.1 us
    all_to_all x1, blocking collectives, body(): lax.all_to_all(back, axes, split_axis=0, concat_axis=0, tiled=True)  10.9 us
    all_to_all x1, starting transfers between devices, body(): lax.all_to_all(send.reshape(devices, rows // 2, 2, LANES), axes, split_ax...  7.33 us
    ppermute x16, waiting for transfers between devices, swap(): return lax.ppermute(block, ('slab', 'depth'), pairs)  2.71 us
  transfers between devices with their start and end apart: 17, of which 2 were waited for; matrix products, arithmetic and copies ran while one was open for 0% of the time, Pallas kernels for 25%

profile of v4, /device:TPU:0, one launch (start us, length us, event | category | flops | bytes accessed | tf_op | source)
XLA Modules:
  0.0 60.3 jit_solution(6636514943093087221)
XLA Ops:
  0.6 2.2 %shard_map.103 = (bf16[64,512]{1,0:T(8,128)(2,1)S(1)}, bf16[64,512]{1,0:T(8,128)(2,1)S(1)}, f32[16,512]{1,0:T(8,128)S(1)}, f32[16,512]{1,0:T(8,128)S(1)}, bf16[5...) custom-call(f32[16,64,512]{2,1,0:T(8,128)} %alpha.3, f32[16,64,512]{2,1,0:T(8,128)} %vx_h.1, f32[16,64,512]{2,1,0:T(8,128)} %vz_h.1, ...), custom_call_target="tpu_custom_call" | custom-call | tf_op jit(solution)/shard_map/pallas_call | solution.py:29
  2.8 7.3 %all-to-all-start = ((bf16[32,9,2,128]{3,2,1,0:T(2,128)(2,1)}), bf16[32,9,2,128]{3,2,1,0:T(2,128)(2,1)S(1)}, u32[]{:S(2)}, u32[]{:S(2)}) async-start(bf16[32,9,2,128]{3,2,1,0:T(2,128)(2,1)} %bitcast.2), calls=%async_computation | async-start | bytes 294912 | tf_op jit(solution)/shard_map/all_to_all | solution.py:682
  10.2 1.8 %collective-permute-start = (bf16[64,512]{1,0:T(8,128)(2,1)S(1)}, bf16[64,512]{1,0:T(8,128)(2,1)S(1)}, u32[]{:S(2)}, u32[]{:S(2)}) collective-permute-start(bf16[64,512]{1,0:T(8,128)(2,1)S(1)} %get-tuple-element.41), channel_id=1, source_target_pairs={{0,4},{1,5},{2,6},{3,7},{4,0},{5,1},{6,2},{7,3},{8,12},{9,13},{10,... | collective-permute-start | bytes 196616 | tf_op jit(solution)/shard_map/ppermute | solution.py:61
  12.0 0.5 collective-permute-start.2
  12.5 2.4 %collective-permute-start.3 = (f32[16,512]{1,0:T(8,128)S(1)}, f32[16,512]{1,0:T(8,128)S(1)}, u32[]{:S(2)}, u32[]{:S(2)}) collective-permute-start(f32[16,512]{1,0:T(8,128)S(1)} %get-tuple-element.44), channel_id=1, source_target_pairs={{0,4},{1,2},{2,1},{3,7},{4,0},{5,6},{6,5},{7,3},{8,12},{9,10},{10,... | collective-permute-start | bytes 98312 | tf_op jit(solution)/shard_map/ppermute | solution.py:61
  15.0 0.0 collective-permute-done.2.ze_in
  15.0 2.0 %collective-permute-done.3.zo_in = f32[16,512]{1,0:T(8,128)S(1)} collective-permute-done((f32[16,512]{1,0:T(8,128)S(1)}, f32[16,512]{1,0:T(8,128)S(1)}, u32[]{:S(2)}, u32[]{:S(2)}) %collective-permute-start.3) | collective-permute-done | bytes 32800 | tf_op jit(solution)/shard_map/ppermute | solution.py:61
  17.0 0.0 collective-permute-done.xe_in
  17.0 0.0 collective-permute-done.1.xo_in
  17.0 3.8 %shard_map.104 = (f32[16,64,512]{2,1,0:T(8,128)}, f32[4,64,512]{2,1,0:T(8,128)S(1)}, bf16[2,64,512]{2,1,0:T(8,128)(2,1)S(1)}, bf16[2,64,512]{2,1,0:T(8,128)(2,1)...) custom-call(f32[16,64,512]{2,1,0:T(8,128)S(1)} %copy-done, f32[16,64,512]{2,1,0:T(8,128)} %vx_h.1, ...), custom_call_target="tpu_custom_call" | custom-call | tf_op jit(solution)/shard_map/pallas_call | solution.py:29
  20.8 2.0 %collective-permute-start.4 = (bf16[2,64,512]{2,1,0:T(8,128)(2,1)S(1)}, bf16[2,64,512]{2,1,0:T(8,128)(2,1)S(1)}, u32[]{:S(2)}, u32[]{:S(2)}) collective-permute-start(bf16[2,64,512]{2,1,0:T(8,128)(2,1)S(1)} %get-tuple-element.50), channel_id=1, source_target_pairs={{0,4},{1,5},{2,6},{3,7},{4,0},{5,1},{6,2},{7,3},{8,12},{9,13},{10,... | collective-permute-start | bytes 393224 | tf_op jit(solution)/shard_map/ppermute | solution.py:61
  22.8 0.0 collective-permute-start.5
  22.8 0.5 collective-permute-start.6
  23.3 2.9 %collective-permute-start.7 = (f32[2,16,512]{2,1,0:T(8,128)S(1)}, f32[2,16,512]{2,1,0:T(8,128)S(1)}, u32[]{:S(2)}, u32[]{:S(2)}) collective-permute-start(f32[2,16,512]{2,1,0:T(8,128)S(1)} %get-tuple-element.53), channel_id=1, source_target_pairs={{0,4},{1,2},{2,1},{3,7},{4,0},{5,6},{6,5},{7,3},{8,12},{9,10},{10,... | collective-permute-start | bytes 196616 | tf_op jit(solution)/shard_map/ppermute | solution.py:61
  26.2 7.6 %shard_map.105 = (f32[16,64,512]{2,1,0:T(8,128)S(1)}, f32[17,64,512]{2,1,0:T(8,128)S(1)}, f32[16,64,512]{2,1,0:T(8,128)S(1)}, f32[16,64,512]{2,1,0:T(8,128)S(1)}...) custom-call(bf16[576,128]{1,0:T(8,128)(2,1)S(1)} %bitcast.4, ...), custom_call_target="tpu_custom_call" | custom-call | tf_op jit(solution)/shard_map/pallas_call | solution.py:29
  33.8 0.0 collective-permute-done.6.ze_in
  33.9 0.0 collective-permute-done.4.xe_in
  33.9 0.0 collective-permute-done.5.xo_in
  33.9 0.7 %shard_map.106 = (f32[16,64,512]{2,1,0:T(8,128)S(1)}, f32[16,64,512]{2,1,0:T(8,128)S(1)}, f32[2,64,512]{2,1,0:T(8,128)S(1)}, f32[2,16,512]{2,1,0:T(8,128)S(1)}, ...) custom-call(f32[16,64,512]{2,1,0:T(8,128)S(1)} %get-tuple-element.47, ...), custom_call_target="tpu_custom_call", output_to_operand_aliasing={{0}: (0, {}), {1}: (1, {})} | custom-call | tf_op jit(solution)/shard_map/pallas_call | solution.py:29
  34.6 0.1 collective-permute-start.8
  34.7 0.9 %collective-permute-start.9 = (bf16[64,512]{1,0:T(8,128)(2,1)S(1)}, bf16[64,512]{1,0:T(8,128)(2,1)S(1)}, u32[]{:S(2)}, u32[]{:S(2)}) collective-permute-start(bf16[64,512]{1,0:T(8,128)(2,1)S(1)} %get-tuple-element.61), channel_id=1, source_target_pairs={{0,1},{1,0},{2,3},{3,2},{4,8},{5,9},{6,10},{7,11},{8,4},{9,5},{10,... | collective-permute-start | bytes 196616 | tf_op jit(solution)/shard_map/ppermute | solution.py:61
  35.6 2.0 %collective-permute-start.11 = (f32[16,512]{1,0:T(8,128)S(1)}, f32[16,512]{1,0:T(8,128)S(1)}, u32[]{:S(2)}, u32[]{:S(2)}) collective-permute-start(f32[16,512]{1,0:T(8,128)S(1)} %get-tuple-element.63), channel_id=1, source_target_pairs={{0,4},{1,2},{2,1},{3,7},{4,0},{5,6},{6,5},{7,3},{8,12},{9,10},{10,... | collective-permute-start | bytes 98312 | tf_op jit(solution)/shard_map/ppermute | solution.py:61
  37.6 1.5 %shard_map.107.p_in = f32[16,64,512]{2,1,0:T(8,128)S(1)} custom-call(f32[16,64,512]{2,1,0:T(8,128)S(1)} %get-tuple-element.54.p, f32[17,64,512]{2,1,0:T(8,128)S(1)} %get-tuple-element.55.cx, f32[16,64,512]{2,1,0:T(8,128)S(1)} %get-tuple-element.56.cz, f32[16,64,512]{2,1,0:T(8,128)S(1)} %get-tuple-element.57.cy, ...), custom_call_target="tpu_custom_call" | custom-call | tf_op jit(solution)/shard_map/pallas_call | solution.py:29
  39.1 0.6 %collective-permute-done.11.zo_in = f32[16,512]{1,0:T(8,128)S(1)} collective-permute-done((f32[16,512]{1,0:T(8,128)S(1)}, f32[16,512]{1,0:T(8,128)S(1)}, u32[]{:S(2)}, u32[]{:S(2)}) %collective-permute-start.11) | collective-permute-done | bytes 32800 | tf_op jit(solution)/shard_map/ppermute | solution.py:61
  39.8 0.4 shard_map.108
  40.1 2.5 %collective-permute-start.12 = (bf16[64,512]{1,0:T(8,128)(2,1)S(1)}, bf16[64,512]{1,0:T(8,128)(2,1)S(1)}, u32[]{:S(2)}, u32[]{:S(2)}) collective-permute-start(bf16[64,512]{1,0:T(8,128)(2,1)S(1)} %get-tuple-element.68), channel_id=1, source_target_pairs={{0,4},{1,5},{2,6},{3,7},{4,0},{5,1},{6,2},{7,3},{8,12},{9,13},{10,... | collective-permute-start | bytes 196616 | tf_op jit(solution)/shard_map/ppermute | solution.py:61
  42.6 0.5 collective-permute-start.14
  43.1 1.9 %collective-permute-start.15 = (f32[16,512]{1,0:T(8,128)S(1)}, f32[16,512]{1,0:T(8,128)S(1)}, u32[]{:S(2)}, u32[]{:S(2)}) collective-permute-start(f32[16,512]{1,0:T(8,128)S(1)} %get-tuple-element.71), channel_id=1, source_target_pairs={{0,4},{1,2},{2,1},{3,7},{4,0},{5,6},{6,5},{7,3},{8,12},{9,10},{10,... | collective-permute-start | bytes 98312 | tf_op jit(solution)/shard_map/ppermute | solution.py:61
  45.1 2.1 %shard_map.109 = (f32[16,64,512]{2,1,0:T(8,128)S(1)}, f32[16,64,512]{2,1,0:T(8,128)}) custom-call(f32[16,64,512]{2,1,0:T(8,128)S(1)} %get-tuple-element.66.p, f32[17,64,512]{2,1,0:T(8,128)S(1)} %get-tuple-element.55.cx, f32[16,64,512]{2,1,0:T(8,128)S(1)} %get-tuple-element.56.cz, f32[16,64,512]{2,1,0:T(8,128)S(1)} %get-tuple-element.57.cy, ...), custom_call_target="tpu_custom_call" | custom-call | tf_op jit(solution)/shard_map/pallas_call | solution.py:29
  47.2 1.2 %shard_map.110 = (f32[16,64,512]{2,1,0:T(8,128)S(1)}, bf16[32,16,128]{2,1,0:T(8,128)(2,1)S(1)}, f32[16,64,512]{2,1,0:T(8,128)}) custom-call(f32[16,64,512]{2,1,0:T(8,128)S(1)} %get-tuple-element.67.p_in, bf16[64,512]{1,0:T(8,128)(2,1)S(1)} %collective-permute-done.12.xe_in, ...), custom_call_target="tpu_custom_call", output_to_operand_aliasing={{0}: (0, {}), {2}: (8, {})} | custom-call | tf_op jit(solution)/shard_map/pallas_call | solution.py:29
  48.5 10.9 %all_to_all.10.back = bf16[32,16,128]{2,1,0:T(8,128)(2,1)S(1)} all-to-all(bf16[32,16,128]{2,1,0:T(8,128)(2,1)S(1)} %get-tuple-element.75), channel_id=1, replica_groups=mesh['slab'=8,'depth'=4] {'slab','depth'}, dimensions={0} | all-to-all | bytes 262144 | tf_op jit(solution)/shard_map/all_to_all | solution.py:734
  59.4 0.9 %shard_map.111 = bf16[256,128]{1,0:T(8,128)(2,1)} custom-call(bf16[32,16,128]{2,1,0:T(8,128)(2,1)S(1)} %all_to_all.10.back, s32[1,256]{1,0:T(1,128)S(1)} %get-tuple-element.76.slot), custom_call_target="tpu_custom_call" | custom-call | tf_op jit(solution)/shard_map/pallas_call | solution.py:29
  (14 shorter events, 0.0 us)
Async XLA Ops:
  0.6 16.4 %copy-start = (f32[16,64,512]{2,1,0:T(8,128)S(1)}, f32[16,64,512]{2,1,0:T(8,128)}, u32[]{:S(2)}) copy-start(f32[16,64,512]{2,1,0:T(8,128)} %alpha.3) | copy-start | bytes 6291460
  2.8 23.3 %all-to-all-start = ((bf16[32,9,2,128]{3,2,1,0:T(2,128)(2,1)}), bf16[32,9,2,128]{3,2,1,0:T(2,128)(2,1)S(1)}, u32[]{:S(2)}, u32[]{:S(2)}) async-start(bf16[32,9,2,128]{3,2,1,0:T(2,128)(2,1)} %bitcast.2), calls=%async_computation | async-start | bytes 294912 | tf_op jit(solution)/shard_map/all_to_all | solution.py:682
  10.2 6.8 %collective-permute-start = (bf16[64,512]{1,0:T(8,128)(2,1)S(1)}, bf16[64,512]{1,0:T(8,128)(2,1)S(1)}, u32[]{:S(2)}, u32[]{:S(2)}) collective-permute-start(bf16[64,512]{1,0:T(8,128)(2,1)S(1)} %get-tuple-element.41), channel_id=1, source_target_pairs={{0,4},{1,5},{2,6},{3,7},{4,0},{5,1},{6,2},{7,3},{8,12},{9,13},{10,... | collective-permute-start | bytes 196616 | tf_op jit(solution)/shard_map/ppermute | solution.py:61
  12.0 5.0 %collective-permute-start.1 = (bf16[64,512]{1,0:T(8,128)(2,1)S(1)}, bf16[64,512]{1,0:T(8,128)(2,1)S(1)}, u32[]{:S(2)}, u32[]{:S(2)}) collective-permute-start(bf16[64,512]{1,0:T(8,128)(2,1)S(1)} %get-tuple-element.42), channel_id=1, source_target_pairs={{0,1},{1,0},{2,3},{3,2},{4,8},{5,9},{6,10},{7,11},{8,4},{9,5},{10,... | collective-permute-start | bytes 196616 | tf_op jit(solution)/shard_map/ppermute | solution.py:61
  12.0 2.9 %collective-permute-start.2 = (f32[16,512]{1,0:T(8,128)S(1)}, f32[16,512]{1,0:T(8,128)S(1)}, u32[]{:S(2)}, u32[]{:S(2)}) collective-permute-start(f32[16,512]{1,0:T(8,128)S(1)} %get-tuple-element.43), channel_id=1, source_target_pairs={{0,1},{1,0},{2,3},{3,2},{4,5},{5,4},{6,7},{7,6},{8,9},{9,8},{10,11... | collective-permute-start | bytes 98312 | tf_op jit(solution)/shard_map/ppermute | solution.py:61
  12.5 4.5 %collective-permute-start.3 = (f32[16,512]{1,0:T(8,128)S(1)}, f32[16,512]{1,0:T(8,128)S(1)}, u32[]{:S(2)}, u32[]{:S(2)}) collective-permute-start(f32[16,512]{1,0:T(8,128)S(1)} %get-tuple-element.44), channel_id=1, source_target_pairs={{0,4},{1,2},{2,1},{3,7},{4,0},{5,6},{6,5},{7,3},{8,12},{9,10},{10,... | collective-permute-start | bytes 98312 | tf_op jit(solution)/shard_map/ppermute | solution.py:61
  20.8 13.1 %collective-permute-start.4 = (bf16[2,64,512]{2,1,0:T(8,128)(2,1)S(1)}, bf16[2,64,512]{2,1,0:T(8,128)(2,1)S(1)}, u32[]{:S(2)}, u32[]{:S(2)}) collective-permute-start(bf16[2,64,512]{2,1,0:T(8,128)(2,1)S(1)} %get-tuple-element.50), channel_id=1, source_target_pairs={{0,4},{1,5},{2,6},{3,7},{4,0},{5,1},{6,2},{7,3},{8,12},{9,13},{10,... | collective-permute-start | bytes 393224 | tf_op jit(solution)/shard_map/ppermute | solution.py:61
  22.8 11.1 %collective-permute-start.5 = (bf16[2,64,512]{2,1,0:T(8,128)(2,1)S(1)}, bf16[2,64,512]{2,1,0:T(8,128)(2,1)S(1)}, u32[]{:S(2)}, u32[]{:S(2)}) collective-permute-start(bf16[2,64,512]{2,1,0:T(8,128)(2,1)S(1)} %get-tuple-element.51), channel_id=1, source_target_pairs={{0,1},{1,0},{2,3},{3,2},{4,8},{5,9},{6,10},{7,11},{8,4},{9,5},{10,... | collective-permute-start | bytes 393224 | tf_op jit(solution)/shard_map/ppermute | solution.py:61
  22.8 11.0 %collective-permute-start.6 = (f32[2,16,512]{2,1,0:T(8,128)S(1)}, f32[2,16,512]{2,1,0:T(8,128)S(1)}, u32[]{:S(2)}, u32[]{:S(2)}) collective-permute-start(f32[2,16,512]{2,1,0:T(8,128)S(1)} %get-tuple-element.52), channel_id=1, source_target_pairs={{0,1},{1,0},{2,3},{3,2},{4,5},{5,4},{6,7},{7,6},{8,9},{9,8},{10,11... | collective-permute-start | bytes 196616 | tf_op jit(solution)/shard_map/ppermute | solution.py:61
  23.3 10.5 %collective-permute-start.7 = (f32[2,16,512]{2,1,0:T(8,128)S(1)}, f32[2,16,512]{2,1,0:T(8,128)S(1)}, u32[]{:S(2)}, u32[]{:S(2)}) collective-permute-start(f32[2,16,512]{2,1,0:T(8,128)S(1)} %get-tuple-element.53), channel_id=1, source_target_pairs={{0,4},{1,2},{2,1},{3,7},{4,0},{5,6},{6,5},{7,3},{8,12},{9,10},{10,... | collective-permute-start | bytes 196616 | tf_op jit(solution)/shard_map/ppermute | solution.py:61
  34.6 5.2 %collective-permute-start.8 = (bf16[64,512]{1,0:T(8,128)(2,1)S(1)}, bf16[64,512]{1,0:T(8,128)(2,1)S(1)}, u32[]{:S(2)}, u32[]{:S(2)}) collective-permute-start(bf16[64,512]{1,0:T(8,128)(2,1)S(1)} %get-tuple-element.60), channel_id=1, source_target_pairs={{0,4},{1,5},{2,6},{3,7},{4,0},{5,1},{6,2},{7,3},{8,12},{9,13},{10,... | collective-permute-start | bytes 196616 | tf_op jit(solution)/shard_map/ppermute | solution.py:61
  34.7 5.1 %collective-permute-start.9 = (bf16[64,512]{1,0:T(8,128)(2,1)S(1)}, bf16[64,512]{1,0:T(8,128)(2,1)S(1)}, u32[]{:S(2)}, u32[]{:S(2)}) collective-permute-start(bf16[64,512]{1,0:T(8,128)(2,1)S(1)} %get-tuple-element.61), channel_id=1, source_target_pairs={{0,1},{1,0},{2,3},{3,2},{4,8},{5,9},{6,10},{7,11},{8,4},{9,5},{10,... | collective-permute-start | bytes 196616 | tf_op jit(solution)/shard_map/ppermute | solution.py:61
  35.6 3.5 %collective-permute-start.10 = (f32[16,512]{1,0:T(8,128)S(1)}, f32[16,512]{1,0:T(8,128)S(1)}, u32[]{:S(2)}, u32[]{:S(2)}) collective-permute-start(f32[16,512]{1,0:T(8,128)S(1)} %get-tuple-element.62), channel_id=1, source_target_pairs={{0,1},{1,0},{2,3},{3,2},{4,5},{5,4},{6,7},{7,6},{8,9},{9,8},{10,11... | collective-permute-start | bytes 98312 | tf_op jit(solution)/shard_map/ppermute | solution.py:61
  35.6 4.1 %collective-permute-start.11 = (f32[16,512]{1,0:T(8,128)S(1)}, f32[16,512]{1,0:T(8,128)S(1)}, u32[]{:S(2)}, u32[]{:S(2)}) collective-permute-start(f32[16,512]{1,0:T(8,128)S(1)} %get-tuple-element.63), channel_id=1, source_target_pairs={{0,4},{1,2},{2,1},{3,7},{4,0},{5,6},{6,5},{7,3},{8,12},{9,10},{10,... | collective-permute-start | bytes 98312 | tf_op jit(solution)/shard_map/ppermute | solution.py:61
  40.1 7.1 %collective-permute-start.12 = (bf16[64,512]{1,0:T(8,128)(2,1)S(1)}, bf16[64,512]{1,0:T(8,128)(2,1)S(1)}, u32[]{:S(2)}, u32[]{:S(2)}) collective-permute-start(bf16[64,512]{1,0:T(8,128)(2,1)S(1)} %get-tuple-element.68), channel_id=1, source_target_pairs={{0,4},{1,5},{2,6},{3,7},{4,0},{5,1},{6,2},{7,3},{8,12},{9,13},{10,... | collective-permute-start | bytes 196616 | tf_op jit(solution)/shard_map/ppermute | solution.py:61
  42.6 4.6 %collective-permute-start.13 = (bf16[64,512]{1,0:T(8,128)(2,1)S(1)}, bf16[64,512]{1,0:T(8,128)(2,1)S(1)}, u32[]{:S(2)}, u32[]{:S(2)}) collective-permute-start(bf16[64,512]{1,0:T(8,128)(2,1)S(1)} %get-tuple-element.69), channel_id=1, source_target_pairs={{0,1},{1,0},{2,3},{3,2},{4,8},{5,9},{6,10},{7,11},{8,4},{9,5},{10,... | collective-permute-start | bytes 196616 | tf_op jit(solution)/shard_map/ppermute | solution.py:61
  42.6 4.5 %collective-permute-start.14 = (f32[16,512]{1,0:T(8,128)S(1)}, f32[16,512]{1,0:T(8,128)S(1)}, u32[]{:S(2)}, u32[]{:S(2)}) collective-permute-start(f32[16,512]{1,0:T(8,128)S(1)} %get-tuple-element.70), channel_id=1, source_target_pairs={{0,1},{1,0},{2,3},{3,2},{4,5},{5,4},{6,7},{7,6},{8,9},{9,8},{10,11... | collective-permute-start | bytes 98312 | tf_op jit(solution)/shard_map/ppermute | solution.py:61
  43.1 4.0 %collective-permute-start.15 = (f32[16,512]{1,0:T(8,128)S(1)}, f32[16,512]{1,0:T(8,128)S(1)}, u32[]{:S(2)}, u32[]{:S(2)}) collective-permute-start(f32[16,512]{1,0:T(8,128)S(1)} %get-tuple-element.71), channel_id=1, source_target_pairs={{0,4},{1,2},{2,1},{3,7},{4,0},{5,6},{6,5},{7,3},{8,12},{9,10},{10,... | collective-permute-start | bytes 98312 | tf_op jit(solution)/shard_map/ppermute | solution.py:61

commit v5 on v4

--- a/solution.py
+++ b/solution.py
@@ -397,7 +397,7 @@
     rows(0, 0)
     rows(cells_x - 1, 1)
 
-    @pl.loop(1, cells_x - 1)
+    @unrolled(1, cells_x - 1)
     def _(x):
         rows(x, None)
 
@@ -543,7 +543,7 @@
             v = jnp.where(ev_x, a, b) if side else jnp.where(ev_x, b, a)
             p[x, at(k), :] = p[x, at(k), :] + gx[side, at(k), :] * v.astype(F32)
 
-    @pl.loop(0, cells_x)
+    @unrolled(0, cells_x)
     def _(x):
         faces = []
         for side, k in ((0, 0), (1, chunks - 1)):
@@ -585,7 +585,7 @@
 
 
 def early_planes(cells_x):
-    return max(1, cells_x * 3 // 4 - 1)
+    return max(1, cells_x // 2 - 1)
 
 
 def last_sweep(p, cx, cz, cy, inverse, rhs, out, out_h, sem):
@@ -609,7 +609,7 @@
     outs = fetch(border_parts(p, count), border_parts(out_h, count), sems)
     blocks = beam // LANES
 
-    @pl.loop(0, cells_x)
+    @unrolled(0, cells_x)
     def _(x):
         for b, lanes in by_lanes(p):
             first = pl.multiple_of((x * blocks + b) * cells_z, SUB)

time: 60.5 us -> 60.3 us (level)
  Pallas kernels: 20.4 us -> 19.7 us
    pallas_call x9, Pallas kernels: 20.4 us -> 19.7 us  [call(): pl.pallas_call(kernel, out_shape=shapes, in_specs=specs, out_specs=[FAR i...]
  transfers between devices with their start and end apart: 17 -> 17, of which waited for: 2 -> 3; matrix products, arithmetic and copies ran while one was open for 0% -> 0% of each run, Pallas kernels for 25% -> 24%
where the time goes in v5:
time: 60.3 us; the launch traced here: 60.1 us
  starting transfers between devices  25.4 us (42%)
  Pallas kernels  19.7 us (33%)
  blocking collectives  11.1 us (18%)
  waiting for transfers between devices  3.09 us (5%)
  between operations  0.78 us (1%)
    pallas_call x9, Pallas kernels, call(): pl.pallas_call(kernel, out_shape=shapes, in_specs=specs, out_specs=[FAR i...  19.7 us
    ppermute x16, starting transfers between devices, swap(): return lax.ppermute(block, ('slab', 'depth'), pairs)  18.1 us
    all_to_all x1, blocking collectives, body(): lax.all_to_all(back, axes, split_axis=0, concat_axis=0, tiled=True)  11.1 us
    all_to_all x1, starting transfers between devices, body(): lax.all_to_all(send.reshape(devices, rows // 2, 2, LANES), axes, split_ax...  7.33 us
    ppermute x16, waiting for transfers between devices, swap(): return lax.ppermute(block, ('slab', 'depth'), pairs)  3.09 us
  transfers between devices with their start and end apart: 17, of which 3 were waited for; matrix products, arithmetic and copies ran while one was open for 0% of the time, Pallas kernels for 24%

profile of v5, /device:TPU:0, one launch (start us, length us, event | category | flops | bytes accessed | tf_op | source)
XLA Modules:
  0.0 60.1 jit_solution(2672034758590495406)
XLA Ops:
  0.6 2.2 %shard_map.103 = (bf16[64,512]{1,0:T(8,128)(2,1)S(1)}, bf16[64,512]{1,0:T(8,128)(2,1)S(1)}, f32[16,512]{1,0:T(8,128)S(1)}, f32[16,512]{1,0:T(8,128)S(1)}, bf16[5...) custom-call(f32[16,64,512]{2,1,0:T(8,128)} %alpha.3, f32[16,64,512]{2,1,0:T(8,128)} %vx_h.1, f32[16,64,512]{2,1,0:T(8,128)} %vz_h.1, ...), custom_call_target="tpu_custom_call" | custom-call | tf_op jit(solution)/shard_map/pallas_call | solution.py:29
  2.8 7.3 %all-to-all-start = ((bf16[32,9,2,128]{3,2,1,0:T(2,128)(2,1)}), bf16[32,9,2,128]{3,2,1,0:T(2,128)(2,1)S(1)}, u32[]{:S(2)}, u32[]{:S(2)}) async-start(bf16[32,9,2,128]{3,2,1,0:T(2,128)(2,1)} %bitcast.2), calls=%async_computation | async-start | bytes 294912 | tf_op jit(solution)/shard_map/all_to_all | solution.py:682
  10.2 1.8 %collective-permute-start = (bf16[64,512]{1,0:T(8,128)(2,1)S(1)}, bf16[64,512]{1,0:T(8,128)(2,1)S(1)}, u32[]{:S(2)}, u32[]{:S(2)}) collective-permute-start(bf16[64,512]{1,0:T(8,128)(2,1)S(1)} %get-tuple-element.41), channel_id=1, source_target_pairs={{0,4},{1,5},{2,6},{3,7},{4,0},{5,1},{6,2},{7,3},{8,12},{9,13},{10,... | collective-permute-start | bytes 196616 | tf_op jit(solution)/shard_map/ppermute | solution.py:61
  12.0 0.5 collective-permute-start.2
  12.5 2.4 %collective-permute-start.3 = (f32[16,512]{1,0:T(8,128)S(1)}, f32[16,512]{1,0:T(8,128)S(1)}, u32[]{:S(2)}, u32[]{:S(2)}) collective-permute-start(f32[16,512]{1,0:T(8,128)S(1)} %get-tuple-element.44), channel_id=1, source_target_pairs={{0,4},{1,2},{2,1},{3,7},{4,0},{5,6},{6,5},{7,3},{8,12},{9,10},{10,... | collective-permute-start | bytes 98312 | tf_op jit(solution)/shard_map/ppermute | solution.py:61
  15.0 0.0 collective-permute-done.2.ze_in
  15.0 2.0 %collective-permute-done.3.zo_in = f32[16,512]{1,0:T(8,128)S(1)} collective-permute-done((f32[16,512]{1,0:T(8,128)S(1)}, f32[16,512]{1,0:T(8,128)S(1)}, u32[]{:S(2)}, u32[]{:S(2)}) %collective-permute-start.3) | collective-permute-done | bytes 32800 | tf_op jit(solution)/shard_map/ppermute | solution.py:61
  17.0 0.0 collective-permute-done.xe_in
  17.0 0.0 collective-permute-done.1.xo_in
  17.0 3.8 %shard_map.104 = (f32[16,64,512]{2,1,0:T(8,128)}, f32[4,64,512]{2,1,0:T(8,128)S(1)}, bf16[2,64,512]{2,1,0:T(8,128)(2,1)S(1)}, bf16[2,64,512]{2,1,0:T(8,128)(2,1)...) custom-call(f32[16,64,512]{2,1,0:T(8,128)S(1)} %copy-done, f32[16,64,512]{2,1,0:T(8,128)} %vx_h.1, ...), custom_call_target="tpu_custom_call" | custom-call | tf_op jit(solution)/shard_map/pallas_call | solution.py:29
  20.8 2.0 %collective-permute-start.4 = (bf16[2,64,512]{2,1,0:T(8,128)(2,1)S(1)}, bf16[2,64,512]{2,1,0:T(8,128)(2,1)S(1)}, u32[]{:S(2)}, u32[]{:S(2)}) collective-permute-start(bf16[2,64,512]{2,1,0:T(8,128)(2,1)S(1)} %get-tuple-element.50), channel_id=1, source_target_pairs={{0,4},{1,5},{2,6},{3,7},{4,0},{5,1},{6,2},{7,3},{8,12},{9,13},{10,... | collective-permute-start | bytes 393224 | tf_op jit(solution)/shard_map/ppermute | solution.py:61
  22.8 0.0 collective-permute-start.5
  22.8 0.5 collective-permute-start.6
  23.3 2.9 %collective-permute-start.7 = (f32[2,16,512]{2,1,0:T(8,128)S(1)}, f32[2,16,512]{2,1,0:T(8,128)S(1)}, u32[]{:S(2)}, u32[]{:S(2)}) collective-permute-start(f32[2,16,512]{2,1,0:T(8,128)S(1)} %get-tuple-element.53), channel_id=1, source_target_pairs={{0,4},{1,2},{2,1},{3,7},{4,0},{5,6},{6,5},{7,3},{8,12},{9,10},{10,... | collective-permute-start | bytes 196616 | tf_op jit(solution)/shard_map/ppermute | solution.py:61
  26.2 7.6 %shard_map.105 = (f32[16,64,512]{2,1,0:T(8,128)S(1)}, f32[17,64,512]{2,1,0:T(8,128)S(1)}, f32[16,64,512]{2,1,0:T(8,128)S(1)}, f32[16,64,512]{2,1,0:T(8,128)S(1)}...) custom-call(bf16[576,128]{1,0:T(8,128)(2,1)S(1)} %bitcast.4, ...), custom_call_target="tpu_custom_call" | custom-call | tf_op jit(solution)/shard_map/pallas_call | solution.py:29
  33.8 0.0 collective-permute-done.6.ze_in
  33.9 0.0 collective-permute-done.4.xe_in
  33.9 0.6 %shard_map.106 = (f32[16,64,512]{2,1,0:T(8,128)S(1)}, f32[16,64,512]{2,1,0:T(8,128)S(1)}, f32[2,64,512]{2,1,0:T(8,128)S(1)}, f32[2,16,512]{2,1,0:T(8,128)S(1)}, ...) custom-call(f32[16,64,512]{2,1,0:T(8,128)S(1)} %get-tuple-element.47, ...), custom_call_target="tpu_custom_call", output_to_operand_aliasing={{0}: (0, {}), {1}: (1, {})} | custom-call | tf_op jit(solution)/shard_map/pallas_call | solution.py:29
  34.5 0.1 collective-permute-start.8
  34.6 0.9 %collective-permute-start.9 = (bf16[64,512]{1,0:T(8,128)(2,1)S(1)}, bf16[64,512]{1,0:T(8,128)(2,1)S(1)}, u32[]{:S(2)}, u32[]{:S(2)}) collective-permute-start(bf16[64,512]{1,0:T(8,128)(2,1)S(1)} %get-tuple-element.61), channel_id=1, source_target_pairs={{0,1},{1,0},{2,3},{3,2},{4,8},{5,9},{6,10},{7,11},{8,4},{9,5},{10,... | collective-permute-start | bytes 196616 | tf_op jit(solution)/shard_map/ppermute | solution.py:61
  35.6 2.0 %collective-permute-start.11 = (f32[16,512]{1,0:T(8,128)S(1)}, f32[16,512]{1,0:T(8,128)S(1)}, u32[]{:S(2)}, u32[]{:S(2)}) collective-permute-start(f32[16,512]{1,0:T(8,128)S(1)} %get-tuple-element.63), channel_id=1, source_target_pairs={{0,4},{1,2},{2,1},{3,7},{4,0},{5,6},{6,5},{7,3},{8,12},{9,10},{10,... | collective-permute-start | bytes 98312 | tf_op jit(solution)/shard_map/ppermute | solution.py:61
  37.5 1.5 %shard_map.107.p_in = f32[16,64,512]{2,1,0:T(8,128)S(1)} custom-call(f32[16,64,512]{2,1,0:T(8,128)S(1)} %get-tuple-element.54.p, f32[17,64,512]{2,1,0:T(8,128)S(1)} %get-tuple-element.55.cx, f32[16,64,512]{2,1,0:T(8,128)S(1)} %get-tuple-element.56.cz, f32[16,64,512]{2,1,0:T(8,128)S(1)} %get-tuple-element.57.cy, ...), custom_call_target="tpu_custom_call" | custom-call | tf_op jit(solution)/shard_map/pallas_call | solution.py:29
  39.1 0.6 %collective-permute-done.11.zo_in = f32[16,512]{1,0:T(8,128)S(1)} collective-permute-done((f32[16,512]{1,0:T(8,128)S(1)}, f32[16,512]{1,0:T(8,128)S(1)}, u32[]{:S(2)}, u32[]{:S(2)}) %collective-permute-start.11) | collective-permute-done | bytes 32800 | tf_op jit(solution)/shard_map/ppermute | solution.py:61
  39.7 0.2 shard_map.108
  39.9 2.5 %collective-permute-start.12 = (bf16[64,512]{1,0:T(8,128)(2,1)S(1)}, bf16[64,512]{1,0:T(8,128)(2,1)S(1)}, u32[]{:S(2)}, u32[]{:S(2)}) collective-permute-start(bf16[64,512]{1,0:T(8,128)(2,1)S(1)} %get-tuple-element.68), channel_id=1, source_target_pairs={{0,4},{1,5},{2,6},{3,7},{4,0},{5,1},{6,2},{7,3},{8,12},{9,13},{10,... | collective-permute-start | bytes 196616 | tf_op jit(solution)/shard_map/ppermute | solution.py:61
  42.4 0.5 collective-permute-start.14
  42.9 1.9 %collective-permute-start.15 = (f32[16,512]{1,0:T(8,128)S(1)}, f32[16,512]{1,0:T(8,128)S(1)}, u32[]{:S(2)}, u32[]{:S(2)}) collective-permute-start(f32[16,512]{1,0:T(8,128)S(1)} %get-tuple-element.71), channel_id=1, source_target_pairs={{0,4},{1,2},{2,1},{3,7},{4,0},{5,6},{6,5},{7,3},{8,12},{9,10},{10,... | collective-permute-start | bytes 98312 | tf_op jit(solution)/shard_map/ppermute | solution.py:61
  44.9 1.6 %shard_map.109 = (f32[16,64,512]{2,1,0:T(8,128)S(1)}, f32[16,64,512]{2,1,0:T(8,128)}) custom-call(f32[16,64,512]{2,1,0:T(8,128)S(1)} %get-tuple-element.66.p, f32[17,64,512]{2,1,0:T(8,128)S(1)} %get-tuple-element.55.cx, f32[16,64,512]{2,1,0:T(8,128)S(1)} %get-tuple-element.56.cz, f32[16,64,512]{2,1,0:T(8,128)S(1)} %get-tuple-element.57.cy, ...), custom_call_target="tpu_custom_call" | custom-call | tf_op jit(solution)/shard_map/pallas_call | solution.py:29
  46.5 0.4 collective-permute-done.15.zo_in
  46.9 1.3 %shard_map.110 = (f32[16,64,512]{2,1,0:T(8,128)S(1)}, bf16[32,16,128]{2,1,0:T(8,128)(2,1)S(1)}, f32[16,64,512]{2,1,0:T(8,128)}) custom-call(f32[16,64,512]{2,1,0:T(8,128)S(1)} %get-tuple-element.67.p_in, bf16[64,512]{1,0:T(8,128)(2,1)S(1)} %collective-permute-done.12.xe_in, ...), custom_call_target="tpu_custom_call", output_to_operand_aliasing={{0}: (0, {}), {2}: (8, {})} | custom-call | tf_op jit(solution)/shard_map/pallas_call | solution.py:29
  48.1 11.1 %all_to_all.10.back = bf16[32,16,128]{2,1,0:T(8,128)(2,1)S(1)} all-to-all(bf16[32,16,128]{2,1,0:T(8,128)(2,1)S(1)} %get-tuple-element.75), channel_id=1, replica_groups=mesh['slab'=8,'depth'=4] {'slab','depth'}, dimensions={0} | all-to-all | bytes 262144 | tf_op jit(solution)/shard_map/all_to_all | solution.py:734
  59.2 0.9 %shard_map.111 = bf16[256,128]{1,0:T(8,128)(2,1)} custom-call(bf16[32,16,128]{2,1,0:T(8,128)(2,1)S(1)} %all_to_all.10.back, s32[1,256]{1,0:T(1,128)S(1)} %get-tuple-element.76.slot), custom_call_target="tpu_custom_call" | custom-call | tf_op jit(solution)/shard_map/pallas_call | solution.py:29
  (14 shorter events, 0.0 us)
Async XLA Ops:
  0.6 16.4 %copy-start = (f32[16,64,512]{2,1,0:T(8,128)S(1)}, f32[16,64,512]{2,1,0:T(8,128)}, u32[]{:S(2)}) copy-start(f32[16,64,512]{2,1,0:T(8,128)} %alpha.3) | copy-start | bytes 6291460
  2.8 23.3 %all-to-all-start = ((bf16[32,9,2,128]{3,2,1,0:T(2,128)(2,1)}), bf16[32,9,2,128]{3,2,1,0:T(2,128)(2,1)S(1)}, u32[]{:S(2)}, u32[]{:S(2)}) async-start(bf16[32,9,2,128]{3,2,1,0:T(2,128)(2,1)} %bitcast.2), calls=%async_computation | async-start | bytes 294912 | tf_op jit(solution)/shard_map/all_to_all | solution.py:682
  10.2 6.8 %collective-permute-start = (bf16[64,512]{1,0:T(8,128)(2,1)S(1)}, bf16[64,512]{1,0:T(8,128)(2,1)S(1)}, u32[]{:S(2)}, u32[]{:S(2)}) collective-permute-start(bf16[64,512]{1,0:T(8,128)(2,1)S(1)} %get-tuple-element.41), channel_id=1, source_target_pairs={{0,4},{1,5},{2,6},{3,7},{4,0},{5,1},{6,2},{7,3},{8,12},{9,13},{10,... | collective-permute-start | bytes 196616 | tf_op jit(solution)/shard_map/ppermute | solution.py:61
  12.0 5.0 %collective-permute-start.1 = (bf16[64,512]{1,0:T(8,128)(2,1)S(1)}, bf16[64,512]{1,0:T(8,128)(2,1)S(1)}, u32[]{:S(2)}, u32[]{:S(2)}) collective-permute-start(bf16[64,512]{1,0:T(8,128)(2,1)S(1)} %get-tuple-element.42), channel_id=1, source_target_pairs={{0,1},{1,0},{2,3},{3,2},{4,8},{5,9},{6,10},{7,11},{8,4},{9,5},{10,... | collective-permute-start | bytes 196616 | tf_op jit(solution)/shard_map/ppermute | solution.py:61
  12.0 2.9 %collective-permute-start.2 = (f32[16,512]{1,0:T(8,128)S(1)}, f32[16,512]{1,0:T(8,128)S(1)}, u32[]{:S(2)}, u32[]{:S(2)}) collective-permute-start(f32[16,512]{1,0:T(8,128)S(1)} %get-tuple-element.43), channel_id=1, source_target_pairs={{0,1},{1,0},{2,3},{3,2},{4,5},{5,4},{6,7},{7,6},{8,9},{9,8},{10,11... | collective-permute-start | bytes 98312 | tf_op jit(solution)/shard_map/ppermute | solution.py:61
  12.5 4.5 %collective-permute-start.3 = (f32[16,512]{1,0:T(8,128)S(1)}, f32[16,512]{1,0:T(8,128)S(1)}, u32[]{:S(2)}, u32[]{:S(2)}) collective-permute-start(f32[16,512]{1,0:T(8,128)S(1)} %get-tuple-element.44), channel_id=1, source_target_pairs={{0,4},{1,2},{2,1},{3,7},{4,0},{5,6},{6,5},{7,3},{8,12},{9,10},{10,... | collective-permute-start | bytes 98312 | tf_op jit(solution)/shard_map/ppermute | solution.py:61
  20.8 13.1 %collective-permute-start.4 = (bf16[2,64,512]{2,1,0:T(8,128)(2,1)S(1)}, bf16[2,64,512]{2,1,0:T(8,128)(2,1)S(1)}, u32[]{:S(2)}, u32[]{:S(2)}) collective-permute-start(bf16[2,64,512]{2,1,0:T(8,128)(2,1)S(1)} %get-tuple-element.50), channel_id=1, source_target_pairs={{0,4},{1,5},{2,6},{3,7},{4,0},{5,1},{6,2},{7,3},{8,12},{9,13},{10,... | collective-permute-start | bytes 393224 | tf_op jit(solution)/shard_map/ppermute | solution.py:61
  22.8 11.1 %collective-permute-start.5 = (bf16[2,64,512]{2,1,0:T(8,128)(2,1)S(1)}, bf16[2,64,512]{2,1,0:T(8,128)(2,1)S(1)}, u32[]{:S(2)}, u32[]{:S(2)}) collective-permute-start(bf16[2,64,512]{2,1,0:T(8,128)(2,1)S(1)} %get-tuple-element.51), channel_id=1, source_target_pairs={{0,1},{1,0},{2,3},{3,2},{4,8},{5,9},{6,10},{7,11},{8,4},{9,5},{10,... | collective-permute-start | bytes 393224 | tf_op jit(solution)/shard_map/ppermute | solution.py:61
  22.8 11.0 %collective-permute-start.6 = (f32[2,16,512]{2,1,0:T(8,128)S(1)}, f32[2,16,512]{2,1,0:T(8,128)S(1)}, u32[]{:S(2)}, u32[]{:S(2)}) collective-permute-start(f32[2,16,512]{2,1,0:T(8,128)S(1)} %get-tuple-element.52), channel_id=1, source_target_pairs={{0,1},{1,0},{2,3},{3,2},{4,5},{5,4},{6,7},{7,6},{8,9},{9,8},{10,11... | collective-permute-start | bytes 196616 | tf_op jit(solution)/shard_map/ppermute | solution.py:61
  23.3 10.5 %collective-permute-start.7 = (f32[2,16,512]{2,1,0:T(8,128)S(1)}, f32[2,16,512]{2,1,0:T(8,128)S(1)}, u32[]{:S(2)}, u32[]{:S(2)}) collective-permute-start(f32[2,16,512]{2,1,0:T(8,128)S(1)} %get-tuple-element.53), channel_id=1, source_target_pairs={{0,4},{1,2},{2,1},{3,7},{4,0},{5,6},{6,5},{7,3},{8,12},{9,10},{10,... | collective-permute-start | bytes 196616 | tf_op jit(solution)/shard_map/ppermute | solution.py:61
  34.5 5.2 %collective-permute-start.8 = (bf16[64,512]{1,0:T(8,128)(2,1)S(1)}, bf16[64,512]{1,0:T(8,128)(2,1)S(1)}, u32[]{:S(2)}, u32[]{:S(2)}) collective-permute-start(bf16[64,512]{1,0:T(8,128)(2,1)S(1)} %get-tuple-element.60), channel_id=1, source_target_pairs={{0,4},{1,5},{2,6},{3,7},{4,0},{5,1},{6,2},{7,3},{8,12},{9,13},{10,... | collective-permute-start | bytes 196616 | tf_op jit(solution)/shard_map/ppermute | solution.py:61
  34.6 5.1 %collective-permute-start.9 = (bf16[64,512]{1,0:T(8,128)(2,1)S(1)}, bf16[64,512]{1,0:T(8,128)(2,1)S(1)}, u32[]{:S(2)}, u32[]{:S(2)}) collective-permute-start(bf16[64,512]{1,0:T(8,128)(2,1)S(1)} %get-tuple-element.61), channel_id=1, source_target_pairs={{0,1},{1,0},{2,3},{3,2},{4,8},{5,9},{6,10},{7,11},{8,4},{9,5},{10,... | collective-permute-start | bytes 196616 | tf_op jit(solution)/shard_map/ppermute | solution.py:61
  35.5 3.5 %collective-permute-start.10 = (f32[16,512]{1,0:T(8,128)S(1)}, f32[16,512]{1,0:T(8,128)S(1)}, u32[]{:S(2)}, u32[]{:S(2)}) collective-permute-start(f32[16,512]{1,0:T(8,128)S(1)} %get-tuple-element.62), channel_id=1, source_target_pairs={{0,1},{1,0},{2,3},{3,2},{4,5},{5,4},{6,7},{7,6},{8,9},{9,8},{10,11... | collective-permute-start | bytes 98312 | tf_op jit(solution)/shard_map/ppermute | solution.py:61
  35.6 4.1 %collective-permute-start.11 = (f32[16,512]{1,0:T(8,128)S(1)}, f32[16,512]{1,0:T(8,128)S(1)}, u32[]{:S(2)}, u32[]{:S(2)}) collective-permute-start(f32[16,512]{1,0:T(8,128)S(1)} %get-tuple-element.63), channel_id=1, source_target_pairs={{0,4},{1,2},{2,1},{3,7},{4,0},{5,6},{6,5},{7,3},{8,12},{9,10},{10,... | collective-permute-start | bytes 98312 | tf_op jit(solution)/shard_map/ppermute | solution.py:61
  39.9 6.9 %collective-permute-start.12 = (bf16[64,512]{1,0:T(8,128)(2,1)S(1)}, bf16[64,512]{1,0:T(8,128)(2,1)S(1)}, u32[]{:S(2)}, u32[]{:S(2)}) collective-permute-start(bf16[64,512]{1,0:T(8,128)(2,1)S(1)} %get-tuple-element.68), channel_id=1, source_target_pairs={{0,4},{1,5},{2,6},{3,7},{4,0},{5,1},{6,2},{7,3},{8,12},{9,13},{10,... | collective-permute-start | bytes 196616 | tf_op jit(solution)/shard_map/ppermute | solution.py:61
  42.4 4.4 %collective-permute-start.13 = (bf16[64,512]{1,0:T(8,128)(2,1)S(1)}, bf16[64,512]{1,0:T(8,128)(2,1)S(1)}, u32[]{:S(2)}, u32[]{:S(2)}) collective-permute-start(bf16[64,512]{1,0:T(8,128)(2,1)S(1)} %get-tuple-element.69), channel_id=1, source_target_pairs={{0,1},{1,0},{2,3},{3,2},{4,8},{5,9},{6,10},{7,11},{8,4},{9,5},{10,... | collective-permute-start | bytes 196616 | tf_op jit(solution)/shard_map/ppermute | solution.py:61
  42.4 4.0 %collective-permute-start.14 = (f32[16,512]{1,0:T(8,128)S(1)}, f32[16,512]{1,0:T(8,128)S(1)}, u32[]{:S(2)}, u32[]{:S(2)}) collective-permute-start(f32[16,512]{1,0:T(8,128)S(1)} %get-tuple-element.70), channel_id=1, source_target_pairs={{0,1},{1,0},{2,3},{3,2},{4,5},{5,4},{6,7},{7,6},{8,9},{9,8},{10,11... | collective-permute-start | bytes 98312 | tf_op jit(solution)/shard_map/ppermute | solution.py:61
  42.9 3.9 %collective-permute-start.15 = (f32[16,512]{1,0:T(8,128)S(1)}, f32[16,512]{1,0:T(8,128)S(1)}, u32[]{:S(2)}, u32[]{:S(2)}) collective-permute-start(f32[16,512]{1,0:T(8,128)S(1)} %get-tuple-element.71), channel_id=1, source_target_pairs={{0,4},{1,2},{2,1},{3,7},{4,0},{5,6},{6,5},{7,3},{8,12},{9,10},{10,... | collective-permute-start | bytes 98312 | tf_op jit(solution)/shard_map/ppermute | solution.py:61
